TPU v7x, 256 devices: a whole 4x4x8 slice. The times are simulated.
256 devices in a mesh: rep: 4 (over y), fsdp: 64 (over x, z, core).
Axes of the slice: x: 4, y: 4, z: 8, core: 2. Of those that a mesh axis runs over, the one named last changes fastest.
Arguments:
- activations: bfloat16 [65536, 512], P(('rep', 'fsdp')), may hold values from -6 to 6
- output_grads: bfloat16 [65536, 8192], P(('rep', 'fsdp'))
- master: float32 [8192, 512], P('fsdp'), may hold values from -6 to 6
- first_moment: float32 [8192, 512], P('fsdp'), may hold values from -4 to 4
- second_moment: float32 [8192, 512], P('fsdp'), may hold values from 0.2 to 2
Outputs:
- new_master: float32 [8192, 512], P('fsdp')
- new_first: float32 [8192, 512], P('fsdp')
- new_second: float32 [8192, 512], P('fsdp')
- params: bfloat16 [8192, 512], replicated
All inputs are finite; a program needn't handle non-finite values.
Results may differ from a plain program's by a relative error of at most 0.0004.
Values may be sent and summed in bfloat16 or wider, within the bound.
No kernel may reach another device: no remote copies, remote signals or barrier semaphores. Data moves between devices by JAX's collectives and lax.ppermute only.
A program may use at most 128 MiB of HBM per device.

v0:
```python
import jax
import jax.numpy as jnp
from jax import lax
from jax.sharding import PartitionSpec as P

dot_epsilon = 1e-06
beta_one = 0.9
beta_two = 0.95
adam_epsilon = 1e-08
learn_rate = 0.02
decay_rate = 0.1
contract_first = (((0,), (0,)), ((), ()))


def swapped(shard, axis, apart):
    return lax.ppermute(shard, axis, [(i, i ^ 1 << apart) for i in range(lax.axis_size(axis))])


def reversed_bits(number_in, bit_count):
    result = 0
    for position in range(bit_count):
        result = result << 1 | number_in >> position & 1
    return result


def local(activations, output_grads, master, first_moment, second_moment):
    grad_shard = lax.psum_scatter(
        lax.dot_general(
            output_grads, activations, contract_first, preferred_element_type=jnp.float32
        ),
        "fsdp",
        scatter_dimension=0,
        tiled=True,
    )
    replica_count = lax.axis_size("rep")
    level_total = replica_count.bit_length() - 1
    replica = lax.axis_index("rep")
    current = grad_shard
    for level_index in range(level_total):
        side_bit = replica >> level_index & 1
        low_side = side_bit == 0
        half_rows = current.shape[0] // 2
        lower_half = current[:half_rows]
        upper_half = current[half_rows:]
        kept_rows = jnp.where(low_side, lower_half, upper_half)
        outgoing = jnp.where(low_side, upper_half, lower_half)
        incoming = swapped(outgoing, "rep", level_index)
        left_vec = jnp.where(low_side, kept_rows, incoming)
        right_vec = jnp.where(low_side, incoming, kept_rows)
        partial_dots = jnp.stack(
            [
                jnp.sum(left_vec * right_vec),
                jnp.sum(left_vec * left_vec),
                jnp.sum(right_vec * right_vec),
            ]
        )
        totals = lax.psum(partial_dots, "fsdp")
        for inner_bit in range(level_index + 1):
            totals = totals + swapped(totals, "rep", inner_bit)
        left_coef = 1.0 - totals[0] / (2.0 * (totals[1] + dot_epsilon))
        right_coef = 1.0 - totals[0] / (2.0 * (totals[2] + dot_epsilon))
        current = left_coef * left_vec + right_coef * right_vec
    piece_rows = current.shape[0]
    gathered = lax.all_gather(current, "rep", axis=0, tiled=True)
    ordered = [
        gathered[
            reversed_bits(place, level_total)
            * piece_rows : (reversed_bits(place, level_total) + 1)
            * piece_rows
        ]
        for place in range(replica_count)
    ]
    combined = jnp.concatenate(ordered, axis=0)
    correct_one = 1.0 - (beta_one**50) ** 2
    correct_two = 1.0 - (beta_two**50) ** 2
    new_first = beta_one * first_moment + (1.0 - beta_one) * combined
    new_second = beta_two * second_moment + (1.0 - beta_two) * combined * combined
    update = (
        new_first / correct_one / (jnp.sqrt(new_second / correct_two) + adam_epsilon)
        + decay_rate * master
    )
    new_master = master - learn_rate * update
    params = lax.all_gather(new_master.astype(jnp.bfloat16), "fsdp", axis=0, tiled=True)
    return (new_master, new_first, new_second, params)


def solution(mesh):
    in_specs = (
        P(("rep", "fsdp"), None),
        P(("rep", "fsdp"), None),
        P("fsdp", None),
        P("fsdp", None),
        P("fsdp", None),
    )
    out_specs = (P("fsdp", None), P("fsdp", None), P("fsdp", None), P())
    return jax.shard_map(local, mesh=mesh, in_specs=in_specs, out_specs=out_specs, check_vma=False)
```

profile of v0, /device:TPU:1, one launch (start us, length us, event | category | flops | bytes accessed | tf_op | source)
XLA Modules:
  0.0 601.0 jit_solution(10944400333961210456)
XLA Ops:
  7.2 0.0 copy-start
  7.2 0.0 reduce-scatter.2.cloned.1.call-start
  7.2 0.9 copy-done
  8.1 10.3 %fusion.6 = f32[8192,512]{1,0:T(8,128)} fusion(bf16[256,8192]{1,0:T(8,128)(2,1)} %param.6, bf16[256,512]{1,0:T(8,128)(2,1)S(1)} %copy-done), kind=kOutput, calls=%fused_computation.27 | convolution fusion | flops 2147483648 | bytes 21233664 | tf_op jit(solution)/shard_map/dot_general | solution.py:28
  18.4 0.0 copy-start.1
  18.4 0.0 copy-start.2
  18.4 0.0 copy-start.3
  18.4 0.0 reduce-scatter.2.cloned.1.call-update
  18.4 0.0 all-gather.2.cloned.1.call-start
  18.5 189.2 %reduce-scatter.2.cloned.1.call-done = f32[128,512]{1,0:T(8,128)} async-done(((f32[8192,512]{1,0:T(8,128)}), f32[128,512]{1,0:T(8,128)}) %reduce-scatter.2.cloned.1.call-update) | async-done | bytes 262160 | tf_op jit(solution)/shard_map/reduce_scatter | solution.py:27
  207.7 1.0 slice_select_fusion
  208.7 0.9 collective-permute-start
  209.6 3.0 collective-permute-done
  212.6 1.6 multiply_reduce_fusion.2
  214.2 2.0 pad_maximum_fusion.1
  216.2 129.1 %psum.14 = f32[3]{0:T(128)S(1)} all-reduce(f32[3]{0:T(128)S(1)} %pad_maximum_fusion.1), channel_id=1, replica_groups=mesh['rep'=4,'fsdp'=64] {'fsdp'}, use_global_device_ids=true, to_apply=%region_4.5 | all-reduce | flops 3 | bytes 24 | tf_op jit(solution)/shard_map/psum | solution.py:57
  345.3 1.3 collective-permute-start.1
  346.6 1.2 collective-permute-done.1
  347.8 0.6 fusion.5
  351.0 2.6 collective-permute-start.2
  353.7 2.1 collective-permute-done.2
  355.7 0.6 multiply_reduce_fusion.5
  356.4 2.0 pad_maximum_fusion.2
  358.4 126.3 %psum.15 = f32[3]{0:T(128)S(1)} all-reduce(f32[3]{0:T(128)S(1)} %pad_maximum_fusion.2), channel_id=1, replica_groups=mesh['rep'=4,'fsdp'=64] {'fsdp'}, use_global_device_ids=true, to_apply=%region_8.9 | all-reduce | flops 3 | bytes 24 | tf_op jit(solution)/shard_map/psum | solution.py:57
  484.7 1.3 collective-permute-start.3
  486.0 1.2 collective-permute-done.3
  487.2 2.5 collective-permute-start.4
  489.7 1.3 collective-permute-done.4
  491.1 0.6 fusion.4
  494.3 9.5 %all_gather.6 = f32[128,512]{1,0:T(8,128)S(1)} all-gather(f32[32,512]{1,0:T(8,128)S(1)} %multiply_add_fusion.2), channel_id=1, replica_groups=mesh['rep'=4,'fsdp'=64] {'rep'}, dimensions={0}, use_global_device_ids=true | all-gather | bytes 327680 | tf_op jit(solution)/shard_map/all_gather | solution.py:64
  503.8 0.0 copy-done.1
  503.8 0.0 copy-done.2
  503.9 0.0 copy-done.3
  503.9 1.1 fusion.1
  504.9 0.0 all-gather.2.cloned.1.call-update
  504.9 81.9 %all-gather.2.cloned.1.call-done = bf16[8192,512]{1,0:T(8,128)(2,1)} async-done(((bf16[128,512]{1,0:T(8,128)(2,1)}), bf16[8192,512]{1,0:T(8,128)(2,1)}) %all-gather.2.cloned.1.call-update) | async-done | bytes 8388624 | tf_op jit(solution)/shard_map/all_gather | solution.py:83
  586.9 7.3 %copy.10 = bf16[8192,512]{1,0:T(8,128)(2,1)} copy(bf16[8192,512]{1,0:T(8,128)(2,1)} %all-gather.2.cloned.1.call-done) | data formatting | bytes 16777216
  (7 shorter events, 0.1 us)
Async XLA Ops:
  7.2 1.0 copy-start
  7.2 200.5 %reduce-scatter.2.cloned.1.call-start = ((), (), s32[]{:S(2)}) async-start(), calls=%async_computation.1 | async-start | bytes 17039360 | tf_op jit(solution)/shard_map/reduce_scatter | solution.py:27
  18.4 485.4 %copy-start.1 = (f32[128,512]{1,0:T(8,128)S(1)}, f32[128,512]{1,0:T(8,128)}, u32[]{:S(2)}) copy-start(f32[128,512]{1,0:T(8,128)} %param.7) | copy-start | bytes 786436
  18.4 485.4 %copy-start.2 = (f32[128,512]{1,0:T(8,128)S(1)}, f32[128,512]{1,0:T(8,128)}, u32[]{:S(2)}) copy-start(f32[128,512]{1,0:T(8,128)} %param.8) | copy-start | bytes 786436
  18.4 485.5 %copy-start.3 = (f32[128,512]{1,0:T(8,128)S(1)}, f32[128,512]{1,0:T(8,128)}, u32[]{:S(2)}) copy-start(f32[128,512]{1,0:T(8,128)} %param.9) | copy-start | bytes 786436
  18.4 568.4 %all-gather.2.cloned.1.call-start = ((), (), s32[]{:S(2)}) async-start(), calls=%async_computation.2 | async-start | bytes 8519680 | tf_op jit(solution)/shard_map/all_gather | solution.py:83
  208.7 3.9 collective-permute-start
  345.3 2.5 collective-permute-start.1
  351.0 4.7 collective-permute-start.2
  484.7 2.5 collective-permute-start.3
  487.2 3.9 collective-permute-start.4
Sparse Core Ops, SparseCore 0:
  18.6 189.1 reduce-scatter.1
  505.1 81.7 all-gather.1
where the time goes:
time: 601 us
  waiting for transfers between devices  280 us (47%)
  blocking collectives  265 us (44%)
  between operations  19.3 us (3%)
  matrix products  10.3 us (2%)
  local copies, waits for them, and re-layouts  9.44 us (2%)
  starting transfers between devices  8.68 us (1%)
  other arithmetic  8.38 us (1%)
    psum x2, blocking collectives, local(): totals = lax.psum(partial_dots, 'fsdp')  255 us
    reduce_scatter x1, waiting for transfers between devices, local(): lax.psum_scatter(lax.dot_general(output_grads, activations, contract_firs...  189 us
    all_gather x1, waiting for transfers between devices, local(): lax.all_gather(new_master.astype(jnp.bfloat16), 'fsdp', axis=0, tiled=True)  81.9 us
  transfers between devices with their start and end apart: 7, of which 7 were waited for; matrix products, arithmetic and copies ran while one was open for 0% of the time, Pallas kernels for 0%

commit v1 on v0

v1 whole, which is shorter than its diff:
```python
import jax
import jax.numpy as jnp
from jax import lax
from jax.sharding import Mesh, PartitionSpec as P

dot_epsilon = 1e-06
beta_one = 0.9
beta_two = 0.95
adam_epsilon = 1e-08
learn_rate = 0.02
decay_rate = 0.1
contract_first = (((0,), (0,)), ((), ()))
GROUP = ("x", "z", "core")


def shifted(value, axis, step):
    size = lax.axis_size(axis)
    return lax.ppermute(value, axis, [(i, (i + step) % size) for i in range(size)])


def add_top(whole, part):
    rows = part.shape[0]
    return jnp.concatenate([whole[:rows] + part, whole[rows:]], axis=0)


def add_bottom(whole, part):
    rows = whole.shape[0] - part.shape[0]
    return jnp.concatenate([whole[:rows], whole[rows:] + part], axis=0)


def ring_reduce(chunk, axis):
    size = lax.axis_size(axis)
    half = size // 2
    far = chunk(half)
    rows = far.shape[0] // 2
    up = shifted(far[:rows], axis, 1)
    down = shifted(far[rows:], axis, -1)
    for reach in range(half - 1, 0, -1):
        if reach == half - 1:
            send_up, send_down = add_top(chunk(reach), up), add_bottom(chunk(-reach), down)
        else:
            send_up, send_down = chunk(reach) + up, chunk(-reach) + down
        up = shifted(send_up, axis, 1)
        down = shifted(send_down, axis, -1)
    return chunk(0) + up + down


def by_place(whole, axis):
    size = lax.axis_size(axis)
    place = lax.axis_index(axis)

    def chunk(step):
        return lax.dynamic_index_in_dim(whole, (place + step + size) % size, 0, keepdims=False)

    return chunk


def group_members(own):
    place = lax.axis_index("rep")
    below, above, across = shifted(own, "rep", 1), shifted(own, "rep", -1), shifted(own, "rep", 2)
    members = []
    for member in range(4):
        value = jnp.where(
            place == member,
            own,
            jnp.where(
                place == (member + 1) % 4, below, jnp.where(place == (member + 3) % 4, above, across)
            ),
        )
        members.append(value)
    return members


def pair_coefs(cross, left_sq, right_sq):
    return (
        1.0 - cross / (2.0 * (left_sq + dot_epsilon)),
        1.0 - cross / (2.0 * (right_sq + dot_epsilon)),
    )


def local(activations, output_grads, master, first_moment, second_moment):
    core = lax.axis_index("core")
    x_place = lax.axis_index("x")
    tokens, features = output_grads.shape
    width = activations.shape[1]
    rows = master.shape[0]
    half = width // 2
    with jax.named_scope("core_swap"):
        by_core = output_grads.reshape(tokens, features // (2 * rows), 2, rows)
        kept = jnp.where(core == 0, by_core[:, :, 0], by_core[:, :, 1]).reshape(tokens, features // 2)
        given = jnp.where(core == 0, by_core[:, :, 1], by_core[:, :, 0]).reshape(tokens, features // 2)
        grads = jnp.concatenate([kept, shifted(given, "core", 1)], axis=0)
        acts = jnp.concatenate([activations, shifted(activations, "core", 1)], axis=0)

    def product(grad_columns, act_columns):
        return lax.dot_general(
            grad_columns, act_columns, contract_first, preferred_element_type=jnp.float32
        )

    with jax.named_scope("reduce_b"):
        sums_b = product(grads, acts[:, half:]).reshape(4, 8, rows, half)
        sums_b = jnp.swapaxes(sums_b, 0, 1).reshape(8 * 4 * rows, half)
        sums_b = lax.psum_scatter(sums_b, "z", scatter_dimension=0, tiled=True)
    with jax.named_scope("reduce_a"):
        strip = features // 8

        def chunk_a(step):
            place = (x_place + step + 4) % 4
            return product(lax.dynamic_slice_in_dim(grads, place * strip, strip, 1), acts[:, :half])

        sums_a = ring_reduce(chunk_a, "x").reshape(8, rows, half)
        grad_a = ring_reduce(by_place(sums_a, "z"), "z")
    with jax.named_scope("reduce_b2"):
        grad_b = ring_reduce(by_place(sums_b.reshape(4, rows, half), "x"), "x")
    with jax.named_scope("members"):
        members_a = group_members(grad_a)
        members_b = group_members(grad_b)
        members = [jnp.concatenate(pair, axis=1) for pair in zip(members_a, members_b)]
    with jax.named_scope("gram"):
        pairs = [(i, j) for i in range(4) for j in range(i, 4)]
        sums = [jnp.sum(members[i] * members[j]) for i, j in pairs]
        row = jnp.concatenate([jnp.stack(sums), jnp.zeros((128 - len(sums),), jnp.float32)])
        everyone = lax.all_to_all(jnp.broadcast_to(row, (64, 1, 128)), GROUP, 0, 0)
        totals = jnp.sum(everyone, axis=(0, 1))
        gram = {pair: totals[index] for index, pair in enumerate(pairs)}
    with jax.named_scope("combine"):
        c0, c1 = pair_coefs(gram[0, 1], gram[0, 0], gram[1, 1])
        c2, c3 = pair_coefs(gram[2, 3], gram[2, 2], gram[3, 3])
        low_sq = c0 * c0 * gram[0, 0] + 2.0 * c0 * c1 * gram[0, 1] + c1 * c1 * gram[1, 1]
        high_sq = c2 * c2 * gram[2, 2] + 2.0 * c2 * c3 * gram[2, 3] + c3 * c3 * gram[3, 3]
        cross = c0 * (c2 * gram[0, 2] + c3 * gram[0, 3]) + c1 * (c2 * gram[1, 2] + c3 * gram[1, 3])
        low, high = pair_coefs(cross, jnp.maximum(low_sq, 0.0), jnp.maximum(high_sq, 0.0))
        combined = low * (c0 * members[0] + c1 * members[1]) + high * (
            c2 * members[2] + c3 * members[3]
        )
    with jax.named_scope("adamw"):
        correct_one = 1.0 - (beta_one**50) ** 2
        correct_two = 1.0 - (beta_two**50) ** 2
        new_first = beta_one * first_moment + (1.0 - beta_one) * combined
        new_second = beta_two * second_moment + (1.0 - beta_two) * combined * combined
        update = (
            new_first / correct_one / (jnp.sqrt(new_second / correct_two) + adam_epsilon)
            + decay_rate * master
        )
        new_master = master - learn_rate * update
    with jax.named_scope("params"):
        params = lax.all_gather(new_master.astype(jnp.bfloat16), GROUP, axis=0, tiled=True)
    return (new_master, new_first, new_second, params)


def solution(mesh):
    fine = Mesh(mesh.devices.reshape(4, 4, 8, 2), ("rep",) + GROUP)
    everyone = P(("rep",) + GROUP, None)
    block = P(GROUP, None)
    return jax.shard_map(
        local,
        mesh=fine,
        in_specs=(everyone, everyone, block, block, block),
        out_specs=(block, block, block, P()),
        check_vma=False,
    )
```

time: 601 us -> 257 us (0.43)
  blocking collectives: 265 us -> 25.9 us
  waiting for transfers between devices: 280 us -> 130 us
  starting transfers between devices: 8.68 us -> 33.6 us
  local copies, waits for them, and re-layouts: 9.44 us -> 25.2 us
  between operations: 19.3 us -> 26 us
    psum x2 -> x0, blocking collectives: 255 us -> none  [local(): totals = lax.psum(partial_dots, 'fsdp')]
    reduce_scatter x1, waiting for transfers between devices: 189 us -> 0.01 us  [local(): sums_b = lax.psum_scatter(sums_b, 'z', scatter_dimension=0, tiled=True)]
    ppermute x5 -> x24, waiting for transfers between devices: 8.82 us -> 54.5 us  [shifted(): lax.ppermute(value, axis, [(i, (i + step) % size) for i in range(size)])]
    all_to_all x0 -> x1, blocking collectives: none -> 25.9 us  [local(): everyone = lax.all_to_all(jnp.broadcast_to(row, (64, 1, 128)), GROUP, 0, 0)]
    ppermute x5 -> x24, starting transfers between devices: 8.61 us -> 33.6 us  [shifted(): lax.ppermute(value, axis, [(i, (i + step) % size) for i in range(size)])]
    all_gather x1 -> x0, blocking collectives: 9.52 us -> none  [local(): gathered = lax.all_gather(current, 'rep', axis=0, tiled=True)]
    concatenate x0 -> x2, local copies, waits for them, and re-layouts: none -> 6.42 us  [the longest x1 6.4 us: local(): jnp.concatenate([jnp.stack(sums), jnp.zeros((128 - len(sums),), jnp.float...]
    all_gather x1, waiting for transfers between devices: 81.9 us -> 75.9 us  [local(): lax.all_gather(new_master.astype(jnp.bfloat16), GROUP, axis=0, tiled=True)]
  transfers between devices with their start and end apart: 7 -> 26, of which waited for: 7 -> 13; matrix products, arithmetic and copies ran while one was open for 0% -> 4% of each run, Pallas kernels for 0% -> 0%
where the time goes in v1:
time: 257 us; the launch traced here: 256 us
  waiting for transfers between devices  130 us (51%)
  starting transfers between devices  33.6 us (13%)
  between operations  26 us (10%)
  blocking collectives  25.9 us (10%)
  local copies, waits for them, and re-layouts  25.2 us (10%)
  other arithmetic  7.97 us (3%)
  matrix products  6.9 us (3%)
    all_gather x1, waiting for transfers between devices, local(): lax.all_gather(new_master.astype(jnp.bfloat16), GROUP, axis=0, tiled=True)  75.9 us
    ppermute x24, waiting for transfers between devices, shifted(): lax.ppermute(value, axis, [(i, (i + step) % size) for i in range(size)])  54.5 us
    ppermute x24, starting transfers between devices, shifted(): lax.ppermute(value, axis, [(i, (i + step) % size) for i in range(size)])  33.6 us
    all_to_all x1, blocking collectives, local(): everyone = lax.all_to_all(jnp.broadcast_to(row, (64, 1, 128)), GROUP, 0, 0)  25.9 us
    unnamed x17, local copies, waits for them, and re-layouts  13.8 us
    dot_general x5, matrix products, product(): lax.dot_general(grad_columns, act_columns, contract_first, preferred_elem...  6.9 us
    concatenate x1, local copies, waits for them, and re-layouts, local(): jnp.concatenate([jnp.stack(sums), jnp.zeros((128 - len(sums),), jnp.float...  6.4 us
  transfers between devices with their start and end apart: 26, of which 13 were waited for; matrix products, arithmetic and copies ran while one was open for 4% of the time, Pallas kernels for 0%

profile of v1, /device:TPU:1, one launch (start us, length us, event | category | flops | bytes accessed | tf_op | source)
XLA Modules:
  0.0 256.1 jit_solution(2416143929010002792)
XLA Ops:
  7.2 0.0 reduce-scatter.2.cloned.1.call-start
  7.2 6.4 %copy.14 = bf16[256,8192]{0,1:T(8,128)(2,1)} copy(bf16[256,8192]{1,0:T(8,128)(2,1)} %param.6) | data formatting | bytes 8388608 | tf_op args[1]
  13.6 2.5 broadcast_select_fusion.1
  16.1 3.3 %collective-permute-start = (bf16[256,4096]{0,1:T(8,128)(2,1)S(1)}, bf16[256,4096]{0,1:T(8,128)(2,1)S(1)}, u32[]{:S(2)}, u32[]{:S(2)}) collective-permute-start(bf16[256,4096]{0,1:T(8,128)(2,1)S(1)} %bitcast.92), channel_id=1, source_target_pairs={{0,1},{1,0},{2,3},{3,2},{4,5},{5,4},{6,7},{7,6},{8,9},{9,8},{10,11... | collective-permute-start | bytes 6291464 | tf_op jit(solution)/shard_map/core_swap/ppermute | solution.py:18
  19.5 0.1 collective-permute-start.1
  19.6 4.0 %collective-permute-done.1 = bf16[256,512]{1,0:T(8,128)(2,1)S(1)} collective-permute-done((bf16[256,512]{1,0:T(8,128)(2,1)S(1)}, bf16[256,512]{1,0:T(8,128)(2,1)S(1)}, u32[]{:S(2)}, u32[]{:S(2)}) %collective-permute-start.1) | collective-permute-done | bytes 262176 | tf_op jit(solution)/shard_map/core_swap/ppermute | solution.py:18
  23.7 1.3 fusion
  24.9 0.1 copy-done
  25.0 2.3 copy.15
  27.3 0.0 reduce-scatter.2.cloned.1.call-update
  27.3 0.0 all-gather.2.cloned.1.call-start
  27.4 1.5 fusion.8
  28.9 1.0 fusion.36
  29.9 0.7 collective-permute-start.4
  30.7 0.7 collective-permute-start.2
  31.4 1.5 fusion.5
  32.9 0.4 fusion.11
  33.3 10.0 %collective-permute-done.4 = f32[512,256]{1,0:T(8,128)S(1)} collective-permute-done((f32[512,256]{1,0:T(8,128)}, f32[512,256]{1,0:T(8,128)S(1)}, u32[]{:S(2)}, u32[]{:S(2)}) %collective-permute-start.4) | collective-permute-done | bytes 524320 | tf_op jit(solution)/shard_map/reduce_a/ppermute | solution.py:18
  43.4 0.1 fusion.37
  43.5 0.1 pad_maximum_fusion.3
  43.6 1.9 collective-permute-start.5
  45.5 0.1 slice_add_fusion.1
  45.6 1.0 pad_maximum_fusion.2
  46.6 20.6 %collective-permute-done.5 = f32[1024,256]{1,0:T(8,128)} collective-permute-done((f32[1024,256]{1,0:T(8,128)S(1)}, f32[1024,256]{1,0:T(8,128)}, u32[]{:S(2)}, u32[]{:S(2)}) %collective-permute-start.5) | collective-permute-done | bytes 1048608 | tf_op jit(solution)/shard_map/reduce_a/ppermute | solution.py:18
  67.3 4.0 %collective-permute-done.3 = f32[1024,256]{1,0:T(8,128)} collective-permute-done((f32[1024,256]{1,0:T(8,128)}, f32[1024,256]{1,0:T(8,128)}, u32[]{:S(2)}, u32[]{:S(2)}) %collective-permute-start.3) | collective-permute-done | bytes 1048608 | tf_op jit(solution)/shard_map/reduce_a/ppermute | solution.py:18
  71.3 2.2 fusion.1
  73.6 1.7 collective-permute-start.6
  75.3 4.3 %collective-permute-start.10 = (f32[64,256]{1,0:T(8,128)S(1)}, f32[64,256]{1,0:T(8,128)S(1)}, u32[]{:S(2)}, u32[]{:S(2)}) collective-permute-start(f32[64,256]{1,0:T(8,128)S(1)} %get-tuple-element.26), channel_id=1, source_target_pairs={{0,14},{2,0},{4,2},{6,4},{8,6},{10,8},{12,10},{14,12},{1,15},{3,1}... | collective-permute-start | bytes 196616 | tf_op jit(solution)/shard_map/reduce_a/ppermute | solution.py:18
  79.6 3.5 %collective-permute-done.6 = f32[64,256]{1,0:T(8,128)S(1)} collective-permute-done((f32[64,256]{1,0:T(8,128)S(1)}, f32[64,256]{1,0:T(8,128)S(1)}, u32[]{:S(2)}, u32[]{:S(2)}) %collective-permute-start.6) | collective-permute-done | bytes 65568 | tf_op jit(solution)/shard_map/reduce_a/ppermute | solution.py:18
  83.2 0.1 collective-permute-start.7
  83.3 2.7 %collective-permute-start.11 = (f32[128,256]{1,0:T(8,128)S(1)}, f32[128,256]{1,0:T(8,128)S(1)}, u32[]{:S(2)}, u32[]{:S(2)}) collective-permute-start(f32[128,256]{1,0:T(8,128)S(1)} %pad_maximum_fusion.9), channel_id=1, source_target_pairs={{0,14},{2,0},{4,2},{6,4},{8,6},{10,8},{12,10},{14,12},{1,15},{3,1}... | collective-permute-start | bytes 393224 | tf_op jit(solution)/shard_map/reduce_a/ppermute | solution.py:18
  86.0 2.3 collective-permute-done.7
  88.3 0.3 collective-permute-start.8
  88.6 5.0 %collective-permute-done.8 = f32[128,256]{1,0:T(8,128)S(1)} collective-permute-done((f32[128,256]{1,0:T(8,128)S(1)}, f32[128,256]{1,0:T(8,128)S(1)}, u32[]{:S(2)}, u32[]{:S(2)}) %collective-permute-start.8) | collective-permute-done | bytes 131104 | tf_op jit(solution)/shard_map/reduce_a/ppermute | solution.py:18
  93.6 0.1 collective-permute-start.12
  93.8 1.4 collective-permute-start.9
  95.2 1.0 dynamic-slice_bitcast_fusion.4
  96.1 0.1 collective-permute-start.17
  96.2 2.7 %collective-permute-start.19 = (f32[64,256]{1,0:T(8,128)S(1)}, f32[64,256]{1,0:T(8,128)S(1)}, u32[]{:S(2)}, u32[]{:S(2)}) collective-permute-start(f32[64,256]{1,0:T(8,128)S(1)} %get-tuple-element.50), channel_id=1, source_target_pairs={{0,48},{16,0},{32,16},{48,32},{1,49},{17,1},{33,17},{49,33},{2,50}... | collective-permute-start | bytes 196616 | tf_op jit(solution)/shard_map/reduce_b2/ppermute | solution.py:18
  98.9 1.5 collective-permute-start.13
  100.4 0.2 collective-permute-done.17
  100.5 0.9 fusion.22
  101.4 3.0 %collective-permute-start.20 = (f32[128,256]{1,0:T(8,128)S(1)}, f32[128,256]{1,0:T(8,128)S(1)}, u32[]{:S(2)}, u32[]{:S(2)}) collective-permute-start(f32[128,256]{1,0:T(8,128)S(1)} %pad_maximum_fusion.11), channel_id=1, source_target_pairs={{0,48},{16,0},{32,16},{48,32},{1,49},{17,1},{33,17},{49,33},{2,50}... | collective-permute-start | bytes 393224 | tf_op jit(solution)/shard_map/reduce_b2/ppermute | solution.py:18
  104.5 0.1 collective-permute-start.18
  104.7 3.0 %collective-permute-start.16 = (f32[128,256]{1,0:T(8,128)S(1)}, f32[128,256]{1,0:T(8,128)S(1)}, u32[]{:S(2)}, u32[]{:S(2)}) collective-permute-start(f32[128,256]{1,0:T(8,128)S(1)} %fusion.20), channel_id=1, source_target_pairs={{0,128},{64,192},{128,0},{192,64},{1,129},{65,193},{129,1},{193,65... | collective-permute-start | bytes 393224 | tf_op jit(solution)/shard_map/members/ppermute | solution.py:18
  107.7 0.8 collective-permute-start.15
  108.5 0.7 collective-permute-start.14
  109.2 0.5 collective-permute-done.18
  109.6 0.9 fusion.19
  110.5 3.0 %collective-permute-start.23 = (f32[128,256]{1,0:T(8,128)S(1)}, f32[128,256]{1,0:T(8,128)S(1)}, u32[]{:S(2)}, u32[]{:S(2)}) collective-permute-start(f32[128,256]{1,0:T(8,128)S(1)} %fusion.19), channel_id=1, source_target_pairs={{0,128},{64,192},{128,0},{192,64},{1,129},{65,193},{129,1},{193,65... | collective-permute-start | bytes 393224 | tf_op jit(solution)/shard_map/members/ppermute | solution.py:18
  113.5 0.8 collective-permute-start.22
  114.3 0.7 collective-permute-start.21
  115.0 0.1 select_select_fusion.3
  115.1 1.6 collective-permute-done.23
  116.7 2.5 collective-permute-done.22
  119.2 0.2 collective-permute-done.21
  119.4 0.1 select_select_fusion.2
  119.5 0.9 multiply_reduce_fusion
  120.3 6.4 %concatenate.51 = f32[128]{0:T(128)S(1)} concatenate(f32[1]{0:T(128)} %bitcast.26, f32[1]{0:T(128)} %bitcast.27, f32[1]{0:T(128)} %bitcast.28, f32[1]{0:T(128)} %bitcast.29, f32[1]{0:T(128)} %bitcast.30, f32[1]{0:T(128)} %bitcast.31, f32[1]{0:T(128)} %bitcast.32, f32[1]{0:T(128)} %bitcast.33, f32[1]{0:T(128)} %bitcast.34, f32[1]{0:T(128)} %bitcast.35, f32[118]{0:T(128)S(1)} %broadcast_in_dim.6), dimensions={0} | concatenate | bytes 1024 | tf_op jit(solution)/shard_map/gram/concatenate | solution.py:122
  126.8 25.9 %all_to_all.5 = f32[64,1,128]{2,1,0:T(1,128)S(1)} all-to-all(f32[64,1,128]{2,1,0:T(1,128)S(1)} %broadcast_in_dim.7), channel_id=1, replica_groups=mesh['rep'=4,'x'=4,'z'=8,'core'=2] {'x','z','core'}, dimensions={0} | all-to-all | bytes 65536 | tf_op jit(solution)/shard_map/gram/all_to_all | solution.py:123
  152.7 0.7 fusion.38
  164.9 1.1 fusion.34
  166.0 75.9 %all-gather.2.cloned.1.call-done = bf16[8192,512]{1,0:T(8,128)(2,1)} async-done(((bf16[128,512]{1,0:T(8,128)(2,1)}), bf16[8192,512]{1,0:T(8,128)(2,1)}) %all-gather.2.cloned.1.call-update) | async-done | bytes 8388624 | tf_op jit(solution)/shard_map/params/all_gather | solution.py:147
  241.9 7.3 %copy.19 = bf16[8192,512]{1,0:T(8,128)(2,1)} copy(bf16[8192,512]{1,0:T(8,128)(2,1)} %all-gather.2.cloned.1.call-done) | data formatting | bytes 16777216
  (43 shorter events, 0.4 us)
Async XLA Ops:
  7.2 88.0 %reduce-scatter.2.cloned.1.call-start = ((), (), s32[]{:S(2)}) async-start(), calls=%async_computation.2 | async-start | bytes 4718592 | tf_op jit(solution)/shard_map/reduce_b/reduce_scatter | solution.py:103
  13.6 5.9 %copy-start.6 = (bf16[256,512]{1,0:T(8,128)(2,1)S(1)}, bf16[256,512]{1,0:T(8,128)(2,1)}, u32[]{:S(2)}) copy-start(bf16[256,512]{1,0:T(8,128)(2,1)} %param.5) | copy-start | bytes 786436
  16.1 7.5 %collective-permute-start = (bf16[256,4096]{0,1:T(8,128)(2,1)S(1)}, bf16[256,4096]{0,1:T(8,128)(2,1)S(1)}, u32[]{:S(2)}, u32[]{:S(2)}) collective-permute-start(bf16[256,4096]{0,1:T(8,128)(2,1)S(1)} %bitcast.92), channel_id=1, source_target_pairs={{0,1},{1,0},{2,3},{3,2},{4,5},{5,4},{6,7},{7,6},{8,9},{9,8},{10,11... | collective-permute-start | bytes 6291464 | tf_op jit(solution)/shard_map/core_swap/ppermute | solution.py:18
  19.5 4.2 %collective-permute-start.1 = (bf16[256,512]{1,0:T(8,128)(2,1)S(1)}, bf16[256,512]{1,0:T(8,128)(2,1)S(1)}, u32[]{:S(2)}, u32[]{:S(2)}) collective-permute-start(bf16[256,512]{1,0:T(8,128)(2,1)S(1)} %copy-done.6), channel_id=1, source_target_pairs={{0,1},{1,0},{2,3},{3,2},{4,5},{5,4},{6,7},{7,6},{8,9},{9,8},{10,11... | collective-permute-start | bytes 786440 | tf_op jit(solution)/shard_map/core_swap/ppermute | solution.py:18
  23.6 9.2 %copy-start.2 = (bf16[512,512]{1,0:T(8,128)(2,1)}, bf16[512,512]{1,0:T(8,128)(2,1)S(1)}, u32[]{:S(2)}) copy-start(bf16[512,512]{1,0:T(8,128)(2,1)S(1)} %constant_dynamic-update-slice_fusion) | copy-start | bytes 1572868
  23.7 1.4 copy-start
  27.3 214.6 %all-gather.2.cloned.1.call-start = ((), (), s32[]{:S(2)}) async-start(), calls=%async_computation.3 | async-start | bytes 8519680 | tf_op jit(solution)/shard_map/params/all_gather | solution.py:147
  29.9 13.4 %collective-permute-start.4 = (f32[512,256]{1,0:T(8,128)}, f32[512,256]{1,0:T(8,128)S(1)}, u32[]{:S(2)}, u32[]{:S(2)}) collective-permute-start(f32[512,256]{1,0:T(8,128)} %get-tuple-element.31), channel_id=1, source_target_pairs={{0,48},{16,0},{32,16},{48,32},{1,49},{17,1},{33,17},{49,33},{2,50}... | collective-permute-start | bytes 1572872 | tf_op jit(solution)/shard_map/reduce_a/ppermute | solution.py:18
  30.7 2.2 copy-start.1
  30.7 14.8 %collective-permute-start.2 = (f32[512,256]{1,0:T(8,128)}, f32[512,256]{1,0:T(8,128)S(1)}, u32[]{:S(2)}, u32[]{:S(2)}) collective-permute-start(f32[512,256]{1,0:T(8,128)} %get-tuple-element.30), channel_id=1, source_target_pairs={{0,16},{16,32},{32,48},{48,0},{1,17},{17,33},{33,49},{49,1},{2,18}... | collective-permute-start | bytes 1572872 | tf_op jit(solution)/shard_map/reduce_a/ppermute | solution.py:18
  43.6 23.7 %collective-permute-start.5 = (f32[1024,256]{1,0:T(8,128)S(1)}, f32[1024,256]{1,0:T(8,128)}, u32[]{:S(2)}, u32[]{:S(2)}) collective-permute-start(f32[1024,256]{1,0:T(8,128)S(1)} %pad_maximum_fusion.3), channel_id=1, source_target_pairs={{0,48},{16,0},{32,16},{48,32},{1,49},{17,1},{33,17},{49,33},{2,50}... | collective-permute-start | bytes 3145736 | tf_op jit(solution)/shard_map/reduce_a/ppermute | solution.py:18
  46.6 24.7 %collective-permute-start.3 = (f32[1024,256]{1,0:T(8,128)}, f32[1024,256]{1,0:T(8,128)}, u32[]{:S(2)}, u32[]{:S(2)}) collective-permute-start(f32[1024,256]{1,0:T(8,128)} %pad_maximum_fusion.2), channel_id=1, source_target_pairs={{0,16},{16,32},{32,48},{48,0},{1,17},{17,33},{33,49},{49,1},{2,18}... | collective-permute-start | bytes 3145736 | tf_op jit(solution)/shard_map/reduce_a/ppermute | solution.py:18
  73.6 9.5 %collective-permute-start.6 = (f32[64,256]{1,0:T(8,128)S(1)}, f32[64,256]{1,0:T(8,128)S(1)}, u32[]{:S(2)}, u32[]{:S(2)}) collective-permute-start(f32[64,256]{1,0:T(8,128)S(1)} %get-tuple-element.24), channel_id=1, source_target_pairs={{0,2},{2,4},{4,6},{6,8},{8,10},{10,12},{12,14},{14,0},{1,3},{3,5},... | collective-permute-start | bytes 196616 | tf_op jit(solution)/shard_map/reduce_a/ppermute | solution.py:18
  75.3 7.8 %collective-permute-start.10 = (f32[64,256]{1,0:T(8,128)S(1)}, f32[64,256]{1,0:T(8,128)S(1)}, u32[]{:S(2)}, u32[]{:S(2)}) collective-permute-start(f32[64,256]{1,0:T(8,128)S(1)} %get-tuple-element.26), channel_id=1, source_target_pairs={{0,14},{2,0},{4,2},{6,4},{8,6},{10,8},{12,10},{14,12},{1,15},{3,1}... | collective-permute-start | bytes 196616 | tf_op jit(solution)/shard_map/reduce_a/ppermute | solution.py:18
  83.2 5.1 %collective-permute-start.7 = (f32[128,256]{1,0:T(8,128)S(1)}, f32[128,256]{1,0:T(8,128)S(1)}, u32[]{:S(2)}, u32[]{:S(2)}) collective-permute-start(f32[128,256]{1,0:T(8,128)S(1)} %pad_maximum_fusion.8), channel_id=1, source_target_pairs={{0,2},{2,4},{4,6},{6,8},{8,10},{10,12},{12,14},{14,0},{1,3},{3,5},... | collective-permute-start | bytes 393224 | tf_op jit(solution)/shard_map/reduce_a/ppermute | solution.py:18
  83.3 5.3 %collective-permute-start.11 = (f32[128,256]{1,0:T(8,128)S(1)}, f32[128,256]{1,0:T(8,128)S(1)}, u32[]{:S(2)}, u32[]{:S(2)}) collective-permute-start(f32[128,256]{1,0:T(8,128)S(1)} %pad_maximum_fusion.9), channel_id=1, source_target_pairs={{0,14},{2,0},{4,2},{6,4},{8,6},{10,8},{12,10},{14,12},{1,15},{3,1}... | collective-permute-start | bytes 393224 | tf_op jit(solution)/shard_map/reduce_a/ppermute | solution.py:18
  88.3 5.3 %collective-permute-start.8 = (f32[128,256]{1,0:T(8,128)S(1)}, f32[128,256]{1,0:T(8,128)S(1)}, u32[]{:S(2)}, u32[]{:S(2)}) collective-permute-start(f32[128,256]{1,0:T(8,128)S(1)} %bitcast_add_fusion.3), channel_id=1, source_target_pairs={{0,2},{2,4},{4,6},{6,8},{8,10},{10,12},{12,14},{14,0},{1,3},{3,5},... | collective-permute-start | bytes 393224 | tf_op jit(solution)/shard_map/reduce_a/ppermute | solution.py:18
  93.6 5.3 %collective-permute-start.12 = (f32[128,256]{1,0:T(8,128)S(1)}, f32[128,256]{1,0:T(8,128)S(1)}, u32[]{:S(2)}, u32[]{:S(2)}) collective-permute-start(f32[128,256]{1,0:T(8,128)S(1)} %get-tuple-element.21), channel_id=1, source_target_pairs={{0,14},{2,0},{4,2},{6,4},{8,6},{10,8},{12,10},{14,12},{1,15},{3,1}... | collective-permute-start | bytes 393224 | tf_op jit(solution)/shard_map/reduce_a/ppermute | solution.py:18
  93.8 10.8 %collective-permute-start.9 = (f32[128,256]{1,0:T(8,128)S(1)}, f32[128,256]{1,0:T(8,128)S(1)}, u32[]{:S(2)}, u32[]{:S(2)}) collective-permute-start(f32[128,256]{1,0:T(8,128)S(1)} %get-tuple-element.20), channel_id=1, source_target_pairs={{0,2},{2,4},{4,6},{6,8},{8,10},{10,12},{12,14},{14,0},{1,3},{3,5},... | collective-permute-start | bytes 393224 | tf_op jit(solution)/shard_map/reduce_a/ppermute | solution.py:18
  96.1 4.4 %collective-permute-start.17 = (f32[64,256]{1,0:T(8,128)S(1)}, f32[64,256]{1,0:T(8,128)S(1)}, u32[]{:S(2)}, u32[]{:S(2)}) collective-permute-start(f32[64,256]{1,0:T(8,128)S(1)} %get-tuple-element.48), channel_id=1, source_target_pairs={{0,16},{16,32},{32,48},{48,0},{1,17},{17,33},{33,49},{49,1},{2,18}... | collective-permute-start | bytes 196616 | tf_op jit(solution)/shard_map/reduce_b2/ppermute | solution.py:18
  96.2 4.3 %collective-permute-start.19 = (f32[64,256]{1,0:T(8,128)S(1)}, f32[64,256]{1,0:T(8,128)S(1)}, u32[]{:S(2)}, u32[]{:S(2)}) collective-permute-start(f32[64,256]{1,0:T(8,128)S(1)} %get-tuple-element.50), channel_id=1, source_target_pairs={{0,48},{16,0},{32,16},{48,32},{1,49},{17,1},{33,17},{49,33},{2,50}... | collective-permute-start | bytes 196616 | tf_op jit(solution)/shard_map/reduce_b2/ppermute | solution.py:18
  98.9 5.7 %collective-permute-start.13 = (f32[128,256]{1,0:T(8,128)S(1)}, f32[128,256]{1,0:T(8,128)S(1)}, u32[]{:S(2)}, u32[]{:S(2)}) collective-permute-start(f32[128,256]{1,0:T(8,128)S(1)} %bitcast_add_fusion.2), channel_id=1, source_target_pairs={{0,14},{2,0},{4,2},{6,4},{8,6},{10,8},{12,10},{14,12},{1,15},{3,1}... | collective-permute-start | bytes 393224 | tf_op jit(solution)/shard_map/reduce_a/ppermute | solution.py:18
  101.4 7.7 %collective-permute-start.20 = (f32[128,256]{1,0:T(8,128)S(1)}, f32[128,256]{1,0:T(8,128)S(1)}, u32[]{:S(2)}, u32[]{:S(2)}) collective-permute-start(f32[128,256]{1,0:T(8,128)S(1)} %pad_maximum_fusion.11), channel_id=1, source_target_pairs={{0,48},{16,0},{32,16},{48,32},{1,49},{17,1},{33,17},{49,33},{2,50}... | collective-permute-start | bytes 393224 | tf_op jit(solution)/shard_map/reduce_b2/ppermute | solution.py:18
  104.5 5.1 %collective-permute-start.18 = (f32[128,256]{1,0:T(8,128)S(1)}, f32[128,256]{1,0:T(8,128)S(1)}, u32[]{:S(2)}, u32[]{:S(2)}) collective-permute-start(f32[128,256]{1,0:T(8,128)S(1)} %pad_maximum_fusion.10), channel_id=1, source_target_pairs={{0,16},{16,32},{32,48},{48,0},{1,17},{17,33},{33,49},{49,1},{2,18}... | collective-permute-start | bytes 393224 | tf_op jit(solution)/shard_map/reduce_b2/ppermute | solution.py:18
  104.7 60.2 %copy-start.3 = (f32[128,512]{1,0:T(8,128)S(1)}, f32[128,512]{1,0:T(8,128)}, u32[]{:S(2)}) copy-start(f32[128,512]{1,0:T(8,128)} %param.7) | copy-start | bytes 786436
  104.7 60.2 %copy-start.4 = (f32[128,512]{1,0:T(8,128)S(1)}, f32[128,512]{1,0:T(8,128)}, u32[]{:S(2)}) copy-start(f32[128,512]{1,0:T(8,128)} %param.8) | copy-start | bytes 786436
  104.7 60.2 %copy-start.5 = (f32[128,512]{1,0:T(8,128)S(1)}, f32[128,512]{1,0:T(8,128)}, u32[]{:S(2)}) copy-start(f32[128,512]{1,0:T(8,128)} %param.9) | copy-start | bytes 786436
  104.7 9.6 %collective-permute-start.16 = (f32[128,256]{1,0:T(8,128)S(1)}, f32[128,256]{1,0:T(8,128)S(1)}, u32[]{:S(2)}, u32[]{:S(2)}) collective-permute-start(f32[128,256]{1,0:T(8,128)S(1)} %fusion.20), channel_id=1, source_target_pairs={{0,128},{64,192},{128,0},{192,64},{1,129},{65,193},{129,1},{193,65... | collective-permute-start | bytes 393224 | tf_op jit(solution)/shard_map/members/ppermute | solution.py:18
  107.7 7.3 %collective-permute-start.15 = (f32[128,256]{1,0:T(8,128)S(1)}, f32[128,256]{1,0:T(8,128)S(1)}, u32[]{:S(2)}, u32[]{:S(2)}) collective-permute-start(f32[128,256]{1,0:T(8,128)S(1)} %fusion.20), channel_id=1, source_target_pairs={{0,192},{64,0},{128,64},{192,128},{1,193},{65,1},{129,65},{193,129... | collective-permute-start | bytes 393224 | tf_op jit(solution)/shard_map/members/ppermute | solution.py:18
  108.5 6.5 %collective-permute-start.14 = (f32[128,256]{1,0:T(8,128)S(1)}, f32[128,256]{1,0:T(8,128)S(1)}, u32[]{:S(2)}, u32[]{:S(2)}) collective-permute-start(f32[128,256]{1,0:T(8,128)S(1)} %fusion.20), channel_id=1, source_target_pairs={{0,64},{64,128},{128,192},{192,0},{1,65},{65,129},{129,193},{193,1... | collective-permute-start | bytes 393224 | tf_op jit(solution)/shard_map/members/ppermute | solution.py:18
  110.5 6.2 %collective-permute-start.23 = (f32[128,256]{1,0:T(8,128)S(1)}, f32[128,256]{1,0:T(8,128)S(1)}, u32[]{:S(2)}, u32[]{:S(2)}) collective-permute-start(f32[128,256]{1,0:T(8,128)S(1)} %fusion.19), channel_id=1, source_target_pairs={{0,128},{64,192},{128,0},{192,64},{1,129},{65,193},{129,1},{193,65... | collective-permute-start | bytes 393224 | tf_op jit(solution)/shard_map/members/ppermute | solution.py:18
  113.5 5.6 %collective-permute-start.22 = (f32[128,256]{1,0:T(8,128)S(1)}, f32[128,256]{1,0:T(8,128)S(1)}, u32[]{:S(2)}, u32[]{:S(2)}) collective-permute-start(f32[128,256]{1,0:T(8,128)S(1)} %fusion.19), channel_id=1, source_target_pairs={{0,192},{64,0},{128,64},{192,128},{1,193},{65,1},{129,65},{193,129... | collective-permute-start | bytes 393224 | tf_op jit(solution)/shard_map/members/ppermute | solution.py:18
  114.3 5.1 %collective-permute-start.21 = (f32[128,256]{1,0:T(8,128)S(1)}, f32[128,256]{1,0:T(8,128)S(1)}, u32[]{:S(2)}, u32[]{:S(2)}) collective-permute-start(f32[128,256]{1,0:T(8,128)S(1)} %fusion.19), channel_id=1, source_target_pairs={{0,64},{64,128},{128,192},{192,0},{1,65},{65,129},{129,193},{193,1... | collective-permute-start | bytes 393224 | tf_op jit(solution)/shard_map/members/ppermute | solution.py:18
Sparse Core Ops, SparseCore 0:
  27.5 56.9 reduce-scatter.1
  166.2 75.7 all-gather.1

commit v2 on v1

v2 whole, which is shorter than its diff:
```python
import functools

import jax
import jax.numpy as jnp
from jax import lax
from jax.experimental import pallas as pl
from jax.experimental.pallas import tpu as pltpu
from jax.sharding import Mesh, PartitionSpec as P

dot_epsilon = 1e-06
beta_one = 0.9
beta_two = 0.95
adam_epsilon = 1e-08
learn_rate = 0.02
decay_rate = 0.1
contract_first = (((0,), (0,)), ((), ()))
GROUP = ("x", "z", "core")
ROWS_A = 80


def shifted(value, axis, step):
    size = lax.axis_size(axis)
    return lax.ppermute(value, axis, [(i, (i + step) % size) for i in range(size)])


def add_top(whole, part):
    rows = part.shape[0]
    return jnp.concatenate([whole[:rows] + part, whole[rows:]], axis=0)


def add_bottom(whole, part):
    rows = whole.shape[0] - part.shape[0]
    return jnp.concatenate([whole[:rows], whole[rows:] + part], axis=0)


def ring_reduce(chunk, axis):
    size = lax.axis_size(axis)
    half = size // 2
    far = chunk(half)
    rows = far.shape[0] // 2
    up = shifted(far[:rows], axis, 1)
    down = shifted(far[rows:], axis, -1)
    for reach in range(half - 1, 0, -1):
        if reach == half - 1:
            send_up, send_down = add_top(chunk(reach), up), add_bottom(chunk(-reach), down)
        else:
            send_up, send_down = chunk(reach) + up, chunk(-reach) + down
        up = shifted(send_up, axis, 1)
        down = shifted(send_down, axis, -1)
    return chunk(0) + up + down


def by_place(whole, axis):
    size = lax.axis_size(axis)
    place = lax.axis_index(axis)

    def chunk(step):
        return lax.dynamic_index_in_dim(whole, (place + step + size) % size, 0, keepdims=False)

    return chunk


def neighbours(own, axis):
    return [own, shifted(own, axis, -1), shifted(own, axis, 2), shifted(own, axis, 1)]


def in_vmem(count):
    return [pl.BlockSpec(memory_space=pltpu.VMEM)] * count


def split_kernel(block, grads_ref, kept_ref, given_ref):
    low = lax.axis_index("core") == 0
    for z in range(8):
        for x in range(4):
            first = grads_ref[:, pl.ds((x * 16 + z * 2) * block, block)]
            second = grads_ref[:, pl.ds((x * 16 + z * 2 + 1) * block, block)]
            place = pl.ds((z * 4 + x) * block, block)
            kept_ref[:, place] = jnp.where(low, first, second)
            given_ref[:, place] = jnp.where(low, second, first)


def split_columns(grads, block):
    tokens, features = grads.shape
    step = tokens // 4
    half = jax.ShapeDtypeStruct((tokens, features // 2), grads.dtype)
    half_spec = pl.BlockSpec((step, features // 2), lambda i: (i, 0))
    return pl.pallas_call(
        lambda *refs: split_kernel(block, *refs),
        grid=(4,),
        in_specs=[pl.BlockSpec((step, features), lambda i: (i, 0))],
        out_specs=[half_spec, half_spec],
        out_shape=[half, half],
        name="split_columns",
    )(grads)


PAIRS = [(i, j) for i in range(4) for j in range(i, 4)]


def gram_kernel(a0, a1, a2, a3, b0, b1, b2, b3, members_ref, rows_ref):
    place = lax.axis_index("rep")
    half = a0.shape[1]
    for step, (left, right) in enumerate(zip((a0, a1, a2, a3), (b0, b1, b2, b3))):
        member = lax.rem(place + step, 4)
        members_ref[member, :, :half] = left[...]
        members_ref[member, :, half:] = right[...]
    lane = lax.broadcasted_iota(jnp.int32, (1, 128), 1)
    row = jnp.zeros((1, 128), jnp.float32)
    for index, (i, j) in enumerate(PAIRS):
        row = jnp.where(lane == index, jnp.sum(members_ref[i] * members_ref[j]), row)
    rows_ref[...] = jnp.broadcast_to(row[None], rows_ref.shape)


def gram_rows(pieces_a, pieces_b):
    rows, half = pieces_a[0].shape
    return pl.pallas_call(
        gram_kernel,
        in_specs=in_vmem(8),
        out_specs=in_vmem(2),
        out_shape=[
            jax.ShapeDtypeStruct((4, rows, 2 * half), jnp.float32),
            jax.ShapeDtypeStruct((64, 1, 128), jnp.float32),
        ],
        name="gram_rows",
    )(*pieces_a, *pieces_b)


def pair_coefs(cross, left_sq, right_sq):
    return (
        1.0 - cross / (2.0 * (left_sq + dot_epsilon)),
        1.0 - cross / (2.0 * (right_sq + dot_epsilon)),
    )


def update_kernel(
    everyone_ref, members_ref, master_ref, first_ref, second_ref,
    new_master_ref, new_first_ref, new_second_ref, params_a_ref, params_b_ref,
):
    totals = jnp.sum(everyone_ref[...], axis=0)
    gram = {pair: totals[:, index : index + 1] for index, pair in enumerate(PAIRS)}
    c0, c1 = pair_coefs(gram[0, 1], gram[0, 0], gram[1, 1])
    c2, c3 = pair_coefs(gram[2, 3], gram[2, 2], gram[3, 3])
    low_sq = c0 * c0 * gram[0, 0] + 2.0 * c0 * c1 * gram[0, 1] + c1 * c1 * gram[1, 1]
    high_sq = c2 * c2 * gram[2, 2] + 2.0 * c2 * c3 * gram[2, 3] + c3 * c3 * gram[3, 3]
    cross = c0 * (c2 * gram[0, 2] + c3 * gram[0, 3]) + c1 * (c2 * gram[1, 2] + c3 * gram[1, 3])
    low, high = pair_coefs(cross, jnp.maximum(low_sq, 0.0), jnp.maximum(high_sq, 0.0))
    combined = low * (c0 * members_ref[0] + c1 * members_ref[1]) + high * (
        c2 * members_ref[2] + c3 * members_ref[3]
    )
    correct_one = 1.0 - (beta_one**50) ** 2
    correct_two = 1.0 - (beta_two**50) ** 2
    new_first = beta_one * first_ref[...] + (1.0 - beta_one) * combined
    new_second = beta_two * second_ref[...] + (1.0 - beta_two) * combined * combined
    master = master_ref[...]
    update = (
        new_first / correct_one / (jnp.sqrt(new_second / correct_two) + adam_epsilon)
        + decay_rate * master
    )
    new_master = master - learn_rate * update
    new_first_ref[...] = new_first
    new_second_ref[...] = new_second
    new_master_ref[...] = new_master
    half = params_a_ref.shape[0]
    params_a_ref[...] = new_master[:half].astype(jnp.bfloat16)
    params_b_ref[...] = new_master[half:].astype(jnp.bfloat16)


def updated(everyone, members, master, first, second):
    rows, width = master.shape
    whole = jax.ShapeDtypeStruct((rows, width), jnp.float32)
    part_a = jax.ShapeDtypeStruct((ROWS_A, width), jnp.bfloat16)
    part_b = jax.ShapeDtypeStruct((rows - ROWS_A, width), jnp.bfloat16)
    return pl.pallas_call(
        update_kernel,
        in_specs=in_vmem(5),
        out_specs=in_vmem(5),
        out_shape=[whole, whole, whole, part_a, part_b],
        name="updated",
    )(everyone, members, master, first, second)


def place_kernel(size_a, order, *refs):
    pieces, out, sems = refs[: len(order)], refs[-2], refs[-1]
    core, x_place = lax.axis_index("core"), lax.axis_index("x")
    copies = []
    for piece, (colour, side, step) in zip(pieces, order):
        owner = core if side == 0 else 1 - core
        if colour == 0:
            for x in range(4):
                copies.append((piece.at[:, x], out.at[x, :, owner, pl.ds(0, size_a)]))
        else:
            x = lax.rem(x_place + step, 4)
            rows = piece.shape[1]
            copies.append((piece, out.at[x, :, owner, pl.ds(size_a, rows)]))
    started = [
        pltpu.make_async_copy(source, target, sems.at[index])
        for index, (source, target) in enumerate(copies)
    ]
    for copy in started:
        copy.start()
    for copy in started:
        copy.wait()


def placed(out, pieces, order, shape, size_a):
    first = out is None
    return pl.pallas_call(
        functools.partial(place_kernel, size_a, order),
        in_specs=in_vmem(len(pieces)) + ([] if first else [pl.BlockSpec(memory_space=pl.ANY)]),
        out_specs=pl.BlockSpec(memory_space=pl.ANY),
        out_shape=jax.ShapeDtypeStruct(shape, jnp.bfloat16),
        scratch_shapes=[pltpu.SemaphoreType.DMA((len(pieces) + 3,))],
        input_output_aliases={} if first else {len(pieces): 0},
        compiler_params=pltpu.CompilerParams(vmem_limit_bytes=32 * 1024 * 1024),
        name="placed",
    )(*pieces, *([] if first else [out]))


def gathered(params_a, params_b):
    rows_a, width = params_a.shape
    rows_b = params_b.shape[0]
    x_place = lax.axis_index("x")
    near = neighbours(params_a, "x")
    ordered = []
    for x in range(4):
        value = near[0]
        for step in range(1, 4):
            value = jnp.where((x_place + step) % 4 == x, near[step], value)
        ordered.append(value)
    line = jnp.concatenate(ordered, axis=0)
    line, params_b = lax.optimization_barrier((line, params_b))
    own_a = lax.all_gather(line, "z", axis=0, tiled=True).reshape(8, 4, rows_a, width)
    column = lax.all_to_all(jnp.broadcast_to(params_b[None], (8, rows_b, width)), "z", 0, 0)
    own_b = neighbours(column, "x")
    own_a, *own_b = lax.optimization_barrier((own_a, *own_b))
    other_b = [shifted(piece, "core", 1) for piece in own_b]
    other_a = shifted(own_a, "core", 1)
    order = [(1, 0, step) for step in range(4)] + [(1, 1, step) for step in range(4)] + [(0, 0, 0)]
    shape = (4, 8, 2, rows_a + rows_b, width)
    out = placed(None, [*own_b, *other_b, own_a], order, shape, rows_a)
    out = placed(out, [other_a], [(0, 1, 0)], shape, rows_a)
    return out.reshape(-1, width)


def local(activations, output_grads, master, first_moment, second_moment):
    width = activations.shape[1]
    rows = master.shape[0]
    half = width // 2
    with jax.named_scope("core_swap"):
        kept, given = split_columns(output_grads, rows)
        grads = jnp.concatenate([kept, shifted(given, "core", 1)], axis=0)
        acts = jnp.concatenate([activations, shifted(activations, "core", 1)], axis=0)

    def product(act_columns):
        return lax.dot_general(
            grads, act_columns, contract_first, preferred_element_type=jnp.float32
        )

    with jax.named_scope("reduce_b"):
        sums_b = lax.psum_scatter(
            product(acts[:, half:]), "z", scatter_dimension=0, tiled=True
        )
    with jax.named_scope("reduce_a"):
        sums_a = product(acts[:, :half]).reshape(8, 4, rows, half)
        x_place = lax.axis_index("x")

        def chunk_a(step):
            return lax.dynamic_index_in_dim(sums_a, (x_place + step + 4) % 4, 1, keepdims=False)

        sums_a = ring_reduce(chunk_a, "x")
        grad_a = ring_reduce(by_place(sums_a, "z"), "z")
    with jax.named_scope("reduce_b2"):
        grad_b = ring_reduce(by_place(sums_b.reshape(4, rows, half), "x"), "x")
    with jax.named_scope("members"):
        members, row = gram_rows(neighbours(grad_a, "rep"), neighbours(grad_b, "rep"))
    with jax.named_scope("gram"):
        everyone = lax.all_to_all(row, GROUP, 0, 0)
    with jax.named_scope("adamw"):
        new_master, new_first, new_second, params_a, params_b = updated(
            everyone, members, master, first_moment, second_moment
        )
    with jax.named_scope("params"):
        params = gathered(params_a, params_b)
    return (new_master, new_first, new_second, params)


def solution(mesh):
    fine = Mesh(mesh.devices.reshape(4, 4, 8, 2), ("rep",) + GROUP)
    everyone = P(("rep",) + GROUP, None)
    block = P(GROUP, None)
    return jax.shard_map(
        local,
        mesh=fine,
        in_specs=(everyone, everyone, block, block, block),
        out_specs=(block, block, block, P()),
        check_vma=False,
    )
```

time: 257 us -> 222 us (0.86)
  waiting for transfers between devices: 130 us -> 85.3 us
  local copies, waits for them, and re-layouts: 25.2 us -> 8.38 us
  blocking collectives: 25.9 us -> 42.6 us
  Pallas kernels: 0 us -> 14.5 us
  between operations: 26 us -> 14.5 us
  starting transfers between devices: 33.6 us -> 43.3 us
    all_gather x1, waiting for transfers between devices: 75.9 us -> 4.82 us  [gathered(): lax.all_gather(line, 'z', axis=0, tiled=True).reshape(8, 4, rows_a, width)]
    ppermute x24 -> x35, waiting for transfers between devices: 54.5 us -> 80.5 us  [shifted(): lax.ppermute(value, axis, [(i, (i + step) % size) for i in range(size)])]
    all_to_all x1 -> x2, blocking collectives: 25.9 us -> 42.6 us  [the longest x1 26.1 us: local(): everyone = lax.all_to_all(row, GROUP, 0, 0)]
    pallas_call x0 -> x5, Pallas kernels: none -> 14.5 us  [the longest x1 5.15 us: split_columns(): pl.pallas_call(lambda *refs: split_kernel(block, *refs), grid=(4,), in_sp...]
    ppermute x24 -> x35, starting transfers between devices: 33.6 us -> 43.2 us  [shifted(): lax.ppermute(value, axis, [(i, (i + step) % size) for i in range(size)])]
    unnamed x17 -> x26, local copies, waits for them, and re-layouts: 13.8 us -> 6.2 us
    concatenate x1, local copies, waits for them, and re-layouts: 6.4 us -> 0.21 us  [local(): grads = jnp.concatenate([kept, shifted(given, 'core', 1)], axis=0)]
    dot_general x5 -> x2, matrix products: 6.9 us -> 6.77 us  [product(): lax.dot_general(grads, act_columns, contract_first, preferred_element_typ...]
  transfers between devices with their start and end apart: 26 -> 37, of which waited for: 13 -> 23; matrix products, arithmetic and copies ran while one was open for 4% -> 5% of each run, Pallas kernels for 0% -> 1%
where the time goes in v2:
time: 222 us
  waiting for transfers between devices  85.3 us (38%)
  starting transfers between devices  43.3 us (20%)
  blocking collectives  42.6 us (19%)
  Pallas kernels  14.5 us (7%)
  between operations  14.5 us (7%)
  local copies, waits for them, and re-layouts  8.38 us (4%)
  matrix products  6.77 us (3%)
  other arithmetic  6.42 us (3%)
    ppermute x35, waiting for transfers between devices, shifted(): lax.ppermute(value, axis, [(i, (i + step) % size) for i in range(size)])  80.5 us
    ppermute x35, starting transfers between devices, shifted(): lax.ppermute(value, axis, [(i, (i + step) % size) for i in range(size)])  43.2 us
    all_to_all x1, blocking collectives, local(): everyone = lax.all_to_all(row, GROUP, 0, 0)  26.1 us
    all_to_all x1, blocking collectives, gathered(): lax.all_to_all(jnp.broadcast_to(params_b[None], (8, rows_b, width)), 'z',...  16.5 us
    dot_general x2, matrix products, product(): lax.dot_general(grads, act_columns, contract_first, preferred_element_typ...  6.77 us
    unnamed x26, local copies, waits for them, and re-layouts  6.2 us
    pallas_call x1, Pallas kernels, split_columns(): pl.pallas_call(lambda *refs: split_kernel(block, *refs), grid=(4,), in_sp...  5.15 us
    all_gather x1, waiting for transfers between devices, gathered(): lax.all_gather(line, 'z', axis=0, tiled=True).reshape(8, 4, rows_a, width)  4.82 us
  transfers between devices with their start and end apart: 37, of which 23 were waited for; matrix products, arithmetic and copies ran while one was open for 5% of the time, Pallas kernels for 1%

profile of v2, /device:TPU:1, one launch (start us, length us, event | category | flops | bytes accessed | tf_op | source)
XLA Modules:
  0.0 221.8 jit_solution(14867305700139361724)
XLA Ops:
  7.2 5.2 %split_columns.1 = (bf16[256,4096]{1,0:T(8,128)(2,1)}, bf16[256,4096]{1,0:T(8,128)(2,1)}) custom-call(bf16[256,8192]{1,0:T(8,128)(2,1)} %refs_0_.1), custom_call_target="tpu_custom_call" | custom-call | tf_op jit(solution)/shard_map/core_swap/split_columns/pallas_call | solution.py:87
  12.4 3.2 %collective-permute-start = (bf16[256,4096]{1,0:T(8,128)(2,1)}, bf16[256,4096]{1,0:T(8,128)(2,1)S(1)}, u32[]{:S(2)}, u32[]{:S(2)}) collective-permute-start(bf16[256,4096]{1,0:T(8,128)(2,1)} %get-tuple-element.21), channel_id=1, source_target_pairs={{0,1},{1,0},{2,3},{3,2},{4,5},{5,4},{6,7},{7,6},{8,9},{9,8},{10,11... | collective-permute-start | bytes 6291464 | tf_op jit(solution)/shard_map/core_swap/ppermute | solution.py:23
  15.7 1.7 constant_dynamic-update-slice_fusion.1
  17.5 2.2 collective-permute-done.1
  19.7 0.3 collective-permute-done
  20.2 2.0 copy-done.1
  22.2 3.3 %fusion.3 = f32[4096,256]{1,0:T(8,128)} fusion(bf16[512,4096]{1,0:T(8,128)(2,1)S(1)} %constant_dynamic-update-slice_fusion, bf16[512,512]{1,0:T(8,128)(2,1)S(1)} %constant_dynamic-update-slice_fusion.2), kind=kOutput, calls=%fused_computation.13 | convolution fusion | flops 1073741824 | bytes 8650752 | tf_op jit(solution)/shard_map/reduce_b/dot_general | solution.py:255
  25.6 3.5 %fusion.5 = f32[4096,256]{1,0:T(8,128)S(1)} fusion(bf16[512,4096]{1,0:T(8,128)(2,1)} %copy-done.1, bf16[512,512]{1,0:T(8,128)(2,1)S(1)} %constant_dynamic-update-slice_fusion.2), kind=kOutput, calls=%fused_computation.15 | convolution fusion | flops 1073741824 | bytes 8650752 | tf_op jit(solution)/shard_map/reduce_a/dot_general | solution.py:255
  29.4 2.7 %collective-permute-start.4 = (f32[4,128,256]{2,1,0:T(8,128)S(1)}, f32[4,128,256]{2,1,0:T(8,128)S(1)}, u32[]{:S(2)}, u32[]{:S(2)}) collective-permute-start(f32[4,128,256]{2,1,0:T(8,128)S(1)} %get-tuple-element.40), channel_id=1, source_target_pairs={{0,48},{16,0},{32,16},{48,32},{1,49},{17,1},{33,17},{49,33},{2,50}... | collective-permute-start | bytes 1572872 | tf_op jit(solution)/shard_map/reduce_a/ppermute | solution.py:23
  32.0 11.8 %collective-permute-done.2 = f32[4,128,256]{2,1,0:T(8,128)S(1)} collective-permute-done((f32[4,128,256]{2,1,0:T(8,128)S(1)}, f32[4,128,256]{2,1,0:T(8,128)S(1)}, u32[]{:S(2)}, u32[]{:S(2)}) %collective-permute-start.2) | collective-permute-done | bytes 524320 | tf_op jit(solution)/shard_map/reduce_a/ppermute | solution.py:23
  44.1 2.4 %collective-permute-start.5 = (f32[8,128,256]{2,1,0:T(8,128)S(1)}, f32[8,128,256]{2,1,0:T(8,128)S(1)}, u32[]{:S(2)}, u32[]{:S(2)}) collective-permute-start(f32[8,128,256]{2,1,0:T(8,128)S(1)} %pad_maximum_fusion.1), channel_id=1, source_target_pairs={{0,48},{16,0},{32,16},{48,32},{1,49},{17,1},{33,17},{49,33},{2,50}... | collective-permute-start | bytes 3145736 | tf_op jit(solution)/shard_map/reduce_a/ppermute | solution.py:23
  46.5 1.1 pad_maximum_fusion
  47.6 20.2 %collective-permute-done.5 = f32[8,128,256]{2,1,0:T(8,128)S(1)} collective-permute-done((f32[8,128,256]{2,1,0:T(8,128)S(1)}, f32[8,128,256]{2,1,0:T(8,128)S(1)}, u32[]{:S(2)}, u32[]{:S(2)}) %collective-permute-start.5) | collective-permute-done | bytes 1048608 | tf_op jit(solution)/shard_map/reduce_a/ppermute | solution.py:23
  67.8 4.2 %collective-permute-done.3 = f32[8,128,256]{2,1,0:T(8,128)S(1)} collective-permute-done((f32[8,128,256]{2,1,0:T(8,128)}, f32[8,128,256]{2,1,0:T(8,128)S(1)}, u32[]{:S(2)}, u32[]{:S(2)}) %collective-permute-start.3) | collective-permute-done | bytes 1048608 | tf_op jit(solution)/shard_map/reduce_a/ppermute | solution.py:23
  72.1 1.4 fusion
  73.6 3.8 %collective-permute-start.10 = (f32[64,256]{1,0:T(8,128)S(1)}, f32[64,256]{1,0:T(8,128)S(1)}, u32[]{:S(2)}, u32[]{:S(2)}) collective-permute-start(f32[64,256]{1,0:T(8,128)S(1)} %get-tuple-element.48), channel_id=1, source_target_pairs={{0,14},{2,0},{4,2},{6,4},{8,6},{10,8},{12,10},{14,12},{1,15},{3,1}... | collective-permute-start | bytes 196616 | tf_op jit(solution)/shard_map/reduce_a/ppermute | solution.py:23
  77.4 3.5 %collective-permute-done.6 = f32[64,256]{1,0:T(8,128)S(1)} collective-permute-done((f32[64,256]{1,0:T(8,128)S(1)}, f32[64,256]{1,0:T(8,128)S(1)}, u32[]{:S(2)}, u32[]{:S(2)}) %collective-permute-start.6) | collective-permute-done | bytes 65568 | tf_op jit(solution)/shard_map/reduce_a/ppermute | solution.py:23
  81.1 2.7 %collective-permute-start.11 = (f32[128,256]{1,0:T(8,128)S(1)}, f32[128,256]{1,0:T(8,128)S(1)}, u32[]{:S(2)}, u32[]{:S(2)}) collective-permute-start(f32[128,256]{1,0:T(8,128)S(1)} %pad_maximum_fusion.4), channel_id=1, source_target_pairs={{0,14},{2,0},{4,2},{6,4},{8,6},{10,8},{12,10},{14,12},{1,15},{3,1}... | collective-permute-start | bytes 393224 | tf_op jit(solution)/shard_map/reduce_a/ppermute | solution.py:23
  83.8 2.3 %collective-permute-done.7 = f32[128,256]{1,0:T(8,128)S(1)} collective-permute-done((f32[128,256]{1,0:T(8,128)S(1)}, f32[128,256]{1,0:T(8,128)S(1)}, u32[]{:S(2)}, u32[]{:S(2)}) %collective-permute-start.7) | collective-permute-done | bytes 131104 | tf_op jit(solution)/shard_map/reduce_a/ppermute | solution.py:23
  86.4 5.0 %collective-permute-done.8 = f32[128,256]{1,0:T(8,128)S(1)} collective-permute-done((f32[128,256]{1,0:T(8,128)S(1)}, f32[128,256]{1,0:T(8,128)S(1)}, u32[]{:S(2)}, u32[]{:S(2)}) %collective-permute-start.8) | collective-permute-done | bytes 131104 | tf_op jit(solution)/shard_map/reduce_a/ppermute | solution.py:23
  91.7 1.3 collective-permute-start.9
  93.0 1.0 dynamic-slice_bitcast_fusion.10
  94.0 2.7 %collective-permute-start.19 = (f32[64,256]{1,0:T(8,128)S(1)}, f32[64,256]{1,0:T(8,128)S(1)}, u32[]{:S(2)}, u32[]{:S(2)}) collective-permute-start(f32[64,256]{1,0:T(8,128)S(1)} %get-tuple-element.54), channel_id=1, source_target_pairs={{0,48},{16,0},{32,16},{48,32},{1,49},{17,1},{33,17},{49,33},{2,50}... | collective-permute-start | bytes 196616 | tf_op jit(solution)/shard_map/reduce_b2/ppermute | solution.py:23
  96.7 1.4 collective-permute-start.13
  98.3 0.9 fusion.10
  99.2 3.1 %collective-permute-start.20 = (f32[128,256]{1,0:T(8,128)S(1)}, f32[128,256]{1,0:T(8,128)S(1)}, u32[]{:S(2)}, u32[]{:S(2)}) collective-permute-start(f32[128,256]{1,0:T(8,128)S(1)} %pad_maximum_fusion.6), channel_id=1, source_target_pairs={{0,48},{16,0},{32,16},{48,32},{1,49},{17,1},{33,17},{49,33},{2,50}... | collective-permute-start | bytes 393224 | tf_op jit(solution)/shard_map/reduce_b2/ppermute | solution.py:23
  102.5 1.3 collective-permute-start.16
  103.8 2.6 %collective-permute-start.15 = (f32[128,256]{1,0:T(8,128)S(1)}, f32[128,256]{1,0:T(8,128)S(1)}, u32[]{:S(2)}, u32[]{:S(2)}) collective-permute-start(f32[128,256]{1,0:T(8,128)S(1)} %fusion.8.a0), channel_id=1, source_target_pairs={{0,128},{64,192},{128,0},{192,64},{1,129},{65,193},{129,1},{193,65... | collective-permute-start | bytes 393224 | tf_op jit(solution)/shard_map/members/ppermute | solution.py:23
  106.4 1.1 collective-permute-start.14
  107.5 0.9 fusion.7.b0
  108.4 1.3 collective-permute-start.23
  109.7 2.6 %collective-permute-start.22 = (f32[128,256]{1,0:T(8,128)S(1)}, f32[128,256]{1,0:T(8,128)S(1)}, u32[]{:S(2)}, u32[]{:S(2)}) collective-permute-start(f32[128,256]{1,0:T(8,128)S(1)} %fusion.7.b0), channel_id=1, source_target_pairs={{0,128},{64,192},{128,0},{192,64},{1,129},{65,193},{129,1},{193,65... | collective-permute-start | bytes 393224 | tf_op jit(solution)/shard_map/members/ppermute | solution.py:23
  112.3 1.1 collective-permute-start.21
  113.5 3.1 %collective-permute-done.22.b2 = f32[128,256]{1,0:T(8,128)S(1)} collective-permute-done((f32[128,256]{1,0:T(8,128)S(1)}, f32[128,256]{1,0:T(8,128)S(1)}, u32[]{:S(2)}, u32[]{:S(2)}) %collective-permute-start.22) | collective-permute-done | bytes 131104 | tf_op jit(solution)/shard_map/members/ppermute | solution.py:23
  116.7 0.6 collective-permute-done.21.b1
  117.3 0.6 copy-done.11
  118.0 2.3 %gram_rows.1 = (f32[4,128,512]{2,1,0:T(8,128)}, f32[64,1,128]{2,1,0:T(1,128)}) custom-call(f32[128,256]{1,0:T(8,128)} %copy-done.3, f32[128,256]{1,0:T(8,128)} %copy-done.8, f32[128,256]{1,0:T(8,128)} %copy-done.7, f32[128,256]{1,0:T(8,128)} %copy-done.6, f32[128,256]{1,0:T(8,128)} %copy-done.4, f32[128,256]{1,0:T(8,128)} %copy-done.11, ...), custom_call_target="tpu_custom_call" | custom-call | tf_op jit(solution)/shard_map/members/gram_rows/pallas_call | solution.py:116
  120.3 26.1 %all_to_all.10.everyone_ref = f32[64,1,128]{2,1,0:T(1,128)} all-to-all(f32[64,1,128]{2,1,0:T(1,128)} %get-tuple-element.22), channel_id=1, replica_groups=mesh['rep'=4,'x'=4,'z'=8,'core'=2] {'x','z','core'}, dimensions={0} | all-to-all | bytes 65536 | tf_op jit(solution)/shard_map/gram/all_to_all | solution.py:277
  146.4 2.9 %updated.1 = (f32[128,512]{1,0:T(8,128)}, f32[128,512]{1,0:T(8,128)}, f32[128,512]{1,0:T(8,128)}, bf16[80,512]{1,0:T(8,128)(2,1)}, bf16[48,512]{1,0:T(8,128)(2,1)}) custom-call(f32[64,1,128]{2,1,0:T(1,128)} %all_to_all.10.everyone_ref, f32[4,128,512]{2,1,0:T(8,128)} %get-tuple-element.23.members_ref, f32[128,512]{1,0:T(8,128)} %master_ref.1, ...), custom_call_target="tpu_custom_call" | custom-call | tf_op jit(solution)/shard_map/adamw/updated/pallas_call | solution.py:173
  149.3 0.8 collective-permute-start.26
  150.1 1.3 collective-permute-start.25
  151.3 1.5 collective-permute-done.26
  152.8 2.3 %collective-permute-done.25 = bf16[80,512]{1,0:T(8,128)(2,1)S(1)} collective-permute-done((bf16[80,512]{1,0:T(8,128)(2,1)}, bf16[80,512]{1,0:T(8,128)(2,1)S(1)}, u32[]{:S(2)}, u32[]{:S(2)}) %collective-permute-start.25) | collective-permute-done | bytes 81952 | tf_op jit(solution)/shard_map/params/ppermute | solution.py:23
  155.1 1.9 collective-permute-done.24
  157.0 0.9 select_select_fusion.3
  157.9 0.7 pad_maximum_fusion.2
  158.7 0.8 broadcast_in_dim.2
  159.5 16.5 %all_to_all.11.refs_0_ = bf16[8,48,512]{2,1,0:T(8,128)(2,1)S(1)} all-to-all(bf16[8,48,512]{2,1,0:T(8,128)(2,1)S(1)} %broadcast_in_dim.2), channel_id=1, replica_groups=mesh['rep'=4,'x'=4,'z'=8,'core'=2] {'z'}, dimensions={0} | all-to-all | bytes 786432 | tf_op jit(solution)/shard_map/params/all_to_all | solution.py:233
  176.1 1.7 collective-permute-start.28
  177.8 0.9 collective-permute-start.27
  178.7 6.9 %collective-permute-done.29.refs_3_ = bf16[8,48,512]{2,1,0:T(8,128)(2,1)S(1)} collective-permute-done((bf16[8,48,512]{2,1,0:T(8,128)(2,1)S(1)}, bf16[8,48,512]{2,1,0:T(8,128)(2,1)S(1)}, u32[]{:S(2)}, u32[]{:S(2)}) %collective-permute-start.29) | collective-permute-done | bytes 393248 | tf_op jit(solution)/shard_map/params/ppermute | solution.py:23
  185.7 5.3 %collective-permute-done.28.refs_2_ = bf16[8,48,512]{2,1,0:T(8,128)(2,1)S(1)} collective-permute-done((bf16[8,48,512]{2,1,0:T(8,128)(2,1)S(1)}, bf16[8,48,512]{2,1,0:T(8,128)(2,1)S(1)}, u32[]{:S(2)}, u32[]{:S(2)}) %collective-permute-start.28) | collective-permute-done | bytes 393248 | tf_op jit(solution)/shard_map/params/ppermute | solution.py:23
  191.0 3.3 %collective-permute-done.27.refs_1_ = bf16[8,48,512]{2,1,0:T(8,128)(2,1)S(1)} collective-permute-done((bf16[8,48,512]{2,1,0:T(8,128)(2,1)S(1)}, bf16[8,48,512]{2,1,0:T(8,128)(2,1)S(1)}, u32[]{:S(2)}, u32[]{:S(2)}) %collective-permute-start.27) | collective-permute-done | bytes 393248 | tf_op jit(solution)/shard_map/params/ppermute | solution.py:23
  194.3 4.8 %all-gather.2.cloned.1.call-done = bf16[2560,512]{1,0:T(8,128)(2,1)} async-done(((bf16[320,512]{1,0:T(8,128)(2,1)}), bf16[2560,512]{1,0:T(8,128)(2,1)}) %all-gather.2.cloned.1.call-update) | async-done | bytes 2621456 | tf_op jit(solution)/shard_map/params/all_gather | solution.py:232
  199.1 3.3 %collective-permute-start.30 = (bf16[8,4,80,512]{3,2,1,0:T(8,128)(2,1)}, bf16[8,4,80,512]{3,2,1,0:T(8,128)(2,1)S(1)}, u32[]{:S(2)}, u32[]{:S(2)}) collective-permute-start(bf16[8,4,80,512]{3,2,1,0:T(8,128)(2,1)} %bitcast.89), channel_id=1, source_target_pairs={{0,1},{1,0},{2,3},{3,2},{4,5},{5,4},{6,7},{7,6},{8,9},{9,8},{10,11... | collective-permute-start | bytes 7864328 | tf_op jit(solution)/shard_map/params/ppermute | solution.py:23
  202.4 0.5 collective-permute-start.32
  202.9 0.5 collective-permute-start.34
  203.4 3.9 %collective-permute-done.31.refs_4_ = bf16[8,48,512]{2,1,0:T(8,128)(2,1)S(1)} collective-permute-done((bf16[8,48,512]{2,1,0:T(8,128)(2,1)S(1)}, bf16[8,48,512]{2,1,0:T(8,128)(2,1)S(1)}, u32[]{:S(2)}, u32[]{:S(2)}) %collective-permute-start.31) | collective-permute-done | bytes 393248 | tf_op jit(solution)/shard_map/params/ppermute | solution.py:23
  207.4 0.6 collective-permute-done.32.refs_5_
  207.9 0.6 collective-permute-done.33.refs_6_
  208.5 0.6 collective-permute-done.34.refs_7_
  209.1 1.7 copy-done
  210.8 2.6 %placed.2.refs_1_ = bf16[4,8,2,128,512]{4,3,2,1,0:T(8,128)(2,1)} custom-call(bf16[8,48,512]{2,1,0:T(8,128)(2,1)S(1)} %all_to_all.11.refs_0_, bf16[8,48,512]{2,1,0:T(8,128)(2,1)S(1)} %collective-permute-done.27.refs_1_, bf16[8,48,512]{2,1,0:T(8,128)(2,1)S(1)} %collective-permute-done.28.refs_2_, bf16[8,48,512]{2,1,0:T(8,128)(2,1)S(1)} %collective-permute-done.29.refs_3_, ...), custom_call_target="tpu_custom_call" | custom-call | tf_op jit(solution)/shard_map/params/placed/pallas_call | solution.py:207
  213.4 1.5 placed.3
  (70 shorter events, 2.4 us)
Async XLA Ops:
  7.2 8.4 %copy-start.5 = (bf16[256,512]{1,0:T(8,128)(2,1)S(1)}, bf16[256,512]{1,0:T(8,128)(2,1)}, u32[]{:S(2)}) copy-start(bf16[256,512]{1,0:T(8,128)(2,1)} %param.5) | copy-start | bytes 786436
  7.2 85.8 %reduce-scatter.2.cloned.1.call-start = ((), (), s32[]{:S(2)}) async-start(), calls=%async_computation.3 | async-start | bytes 4718592 | tf_op jit(solution)/shard_map/reduce_b/reduce_scatter | solution.py:260
  12.4 7.6 %collective-permute-start = (bf16[256,4096]{1,0:T(8,128)(2,1)}, bf16[256,4096]{1,0:T(8,128)(2,1)S(1)}, u32[]{:S(2)}, u32[]{:S(2)}) collective-permute-start(bf16[256,4096]{1,0:T(8,128)(2,1)} %get-tuple-element.21), channel_id=1, source_target_pairs={{0,1},{1,0},{2,3},{3,2},{4,5},{5,4},{6,7},{7,6},{8,9},{9,8},{10,11... | collective-permute-start | bytes 6291464 | tf_op jit(solution)/shard_map/core_swap/ppermute | solution.py:23
  15.6 4.0 %collective-permute-start.1 = (bf16[256,512]{1,0:T(8,128)(2,1)S(1)}, bf16[256,512]{1,0:T(8,128)(2,1)S(1)}, u32[]{:S(2)}, u32[]{:S(2)}) collective-permute-start(bf16[256,512]{1,0:T(8,128)(2,1)S(1)} %copy-done.5), channel_id=1, source_target_pairs={{0,1},{1,0},{2,3},{3,2},{4,5},{5,4},{6,7},{7,6},{8,9},{9,8},{10,11... | collective-permute-start | bytes 786440 | tf_op jit(solution)/shard_map/core_swap/ppermute | solution.py:23
  20.2 2.0 copy-start.1
  25.5 173.6 %all-gather.2.cloned.1.call-start = ((), (), s32[]{:S(2)}) async-start(), calls=%async_computation.4 | async-start | bytes 2949120 | tf_op jit(solution)/shard_map/params/all_gather | solution.py:232
  29.1 15.0 %copy-start.2 = (f32[4096,256]{1,0:T(8,128)}, f32[4096,256]{1,0:T(8,128)S(1)}, u32[]{:S(2)}) copy-start(f32[4096,256]{1,0:T(8,128)S(1)} %fusion.5) | copy-start | bytes 12582916
  29.3 14.5 %collective-permute-start.2 = (f32[4,128,256]{2,1,0:T(8,128)S(1)}, f32[4,128,256]{2,1,0:T(8,128)S(1)}, u32[]{:S(2)}, u32[]{:S(2)}) collective-permute-start(f32[4,128,256]{2,1,0:T(8,128)S(1)} %get-tuple-element.38), channel_id=1, source_target_pairs={{0,16},{16,32},{32,48},{48,0},{1,17},{17,33},{33,49},{49,1},{2,18}... | collective-permute-start | bytes 1572872 | tf_op jit(solution)/shard_map/reduce_a/ppermute | solution.py:23
  29.4 14.4 %collective-permute-start.4 = (f32[4,128,256]{2,1,0:T(8,128)S(1)}, f32[4,128,256]{2,1,0:T(8,128)S(1)}, u32[]{:S(2)}, u32[]{:S(2)}) collective-permute-start(f32[4,128,256]{2,1,0:T(8,128)S(1)} %get-tuple-element.40), channel_id=1, source_target_pairs={{0,48},{16,0},{32,16},{48,32},{1,49},{17,1},{33,17},{49,33},{2,50}... | collective-permute-start | bytes 1572872 | tf_op jit(solution)/shard_map/reduce_a/ppermute | solution.py:23
  44.1 23.7 %collective-permute-start.5 = (f32[8,128,256]{2,1,0:T(8,128)S(1)}, f32[8,128,256]{2,1,0:T(8,128)S(1)}, u32[]{:S(2)}, u32[]{:S(2)}) collective-permute-start(f32[8,128,256]{2,1,0:T(8,128)S(1)} %pad_maximum_fusion.1), channel_id=1, source_target_pairs={{0,48},{16,0},{32,16},{48,32},{1,49},{17,1},{33,17},{49,33},{2,50}... | collective-permute-start | bytes 3145736 | tf_op jit(solution)/shard_map/reduce_a/ppermute | solution.py:23
  47.6 24.5 %collective-permute-start.3 = (f32[8,128,256]{2,1,0:T(8,128)}, f32[8,128,256]{2,1,0:T(8,128)S(1)}, u32[]{:S(2)}, u32[]{:S(2)}) collective-permute-start(f32[8,128,256]{2,1,0:T(8,128)} %pad_maximum_fusion), channel_id=1, source_target_pairs={{0,16},{16,32},{32,48},{48,0},{1,17},{17,33},{33,49},{49,1},{2,18}... | collective-permute-start | bytes 3145736 | tf_op jit(solution)/shard_map/reduce_a/ppermute | solution.py:23
  73.5 7.4 %collective-permute-start.6 = (f32[64,256]{1,0:T(8,128)S(1)}, f32[64,256]{1,0:T(8,128)S(1)}, u32[]{:S(2)}, u32[]{:S(2)}) collective-permute-start(f32[64,256]{1,0:T(8,128)S(1)} %get-tuple-element.46), channel_id=1, source_target_pairs={{0,2},{2,4},{4,6},{6,8},{8,10},{10,12},{12,14},{14,0},{1,3},{3,5},... | collective-permute-start | bytes 196616 | tf_op jit(solution)/shard_map/reduce_a/ppermute | solution.py:23
  73.6 7.3 %collective-permute-start.10 = (f32[64,256]{1,0:T(8,128)S(1)}, f32[64,256]{1,0:T(8,128)S(1)}, u32[]{:S(2)}, u32[]{:S(2)}) collective-permute-start(f32[64,256]{1,0:T(8,128)S(1)} %get-tuple-element.48), channel_id=1, source_target_pairs={{0,14},{2,0},{4,2},{6,4},{8,6},{10,8},{12,10},{14,12},{1,15},{3,1}... | collective-permute-start | bytes 196616 | tf_op jit(solution)/shard_map/reduce_a/ppermute | solution.py:23
  81.0 5.1 %collective-permute-start.7 = (f32[128,256]{1,0:T(8,128)S(1)}, f32[128,256]{1,0:T(8,128)S(1)}, u32[]{:S(2)}, u32[]{:S(2)}) collective-permute-start(f32[128,256]{1,0:T(8,128)S(1)} %pad_maximum_fusion.3), channel_id=1, source_target_pairs={{0,2},{2,4},{4,6},{6,8},{8,10},{10,12},{12,14},{14,0},{1,3},{3,5},... | collective-permute-start | bytes 393224 | tf_op jit(solution)/shard_map/reduce_a/ppermute | solution.py:23
  81.1 5.3 %collective-permute-start.11 = (f32[128,256]{1,0:T(8,128)S(1)}, f32[128,256]{1,0:T(8,128)S(1)}, u32[]{:S(2)}, u32[]{:S(2)}) collective-permute-start(f32[128,256]{1,0:T(8,128)S(1)} %pad_maximum_fusion.4), channel_id=1, source_target_pairs={{0,14},{2,0},{4,2},{6,4},{8,6},{10,8},{12,10},{14,12},{1,15},{3,1}... | collective-permute-start | bytes 393224 | tf_op jit(solution)/shard_map/reduce_a/ppermute | solution.py:23
  86.1 5.3 %collective-permute-start.8 = (f32[128,256]{1,0:T(8,128)S(1)}, f32[128,256]{1,0:T(8,128)S(1)}, u32[]{:S(2)}, u32[]{:S(2)}) collective-permute-start(f32[128,256]{1,0:T(8,128)S(1)} %bitcast_add_fusion.4), channel_id=1, source_target_pairs={{0,2},{2,4},{4,6},{6,8},{8,10},{10,12},{12,14},{14,0},{1,3},{3,5},... | collective-permute-start | bytes 393224 | tf_op jit(solution)/shard_map/reduce_a/ppermute | solution.py:23
  91.4 5.3 %collective-permute-start.12 = (f32[128,256]{1,0:T(8,128)S(1)}, f32[128,256]{1,0:T(8,128)S(1)}, u32[]{:S(2)}, u32[]{:S(2)}) collective-permute-start(f32[128,256]{1,0:T(8,128)S(1)} %get-tuple-element.43), channel_id=1, source_target_pairs={{0,14},{2,0},{4,2},{6,4},{8,6},{10,8},{12,10},{14,12},{1,15},{3,1}... | collective-permute-start | bytes 393224 | tf_op jit(solution)/shard_map/reduce_a/ppermute | solution.py:23
  91.7 10.8 %collective-permute-start.9 = (f32[128,256]{1,0:T(8,128)S(1)}, f32[128,256]{1,0:T(8,128)S(1)}, u32[]{:S(2)}, u32[]{:S(2)}) collective-permute-start(f32[128,256]{1,0:T(8,128)S(1)} %get-tuple-element.42), channel_id=1, source_target_pairs={{0,2},{2,4},{4,6},{6,8},{8,10},{10,12},{12,14},{14,0},{1,3},{3,5},... | collective-permute-start | bytes 393224 | tf_op jit(solution)/shard_map/reduce_a/ppermute | solution.py:23
  93.9 4.4 %collective-permute-start.17 = (f32[64,256]{1,0:T(8,128)S(1)}, f32[64,256]{1,0:T(8,128)S(1)}, u32[]{:S(2)}, u32[]{:S(2)}) collective-permute-start(f32[64,256]{1,0:T(8,128)S(1)} %get-tuple-element.52), channel_id=1, source_target_pairs={{0,16},{16,32},{32,48},{48,0},{1,17},{17,33},{33,49},{49,1},{2,18}... | collective-permute-start | bytes 196616 | tf_op jit(solution)/shard_map/reduce_b2/ppermute | solution.py:23
  94.0 4.3 %collective-permute-start.19 = (f32[64,256]{1,0:T(8,128)S(1)}, f32[64,256]{1,0:T(8,128)S(1)}, u32[]{:S(2)}, u32[]{:S(2)}) collective-permute-start(f32[64,256]{1,0:T(8,128)S(1)} %get-tuple-element.54), channel_id=1, source_target_pairs={{0,48},{16,0},{32,16},{48,32},{1,49},{17,1},{33,17},{49,33},{2,50}... | collective-permute-start | bytes 196616 | tf_op jit(solution)/shard_map/reduce_b2/ppermute | solution.py:23
  96.7 5.7 %collective-permute-start.13 = (f32[128,256]{1,0:T(8,128)S(1)}, f32[128,256]{1,0:T(8,128)S(1)}, u32[]{:S(2)}, u32[]{:S(2)}) collective-permute-start(f32[128,256]{1,0:T(8,128)S(1)} %bitcast_add_fusion.3), channel_id=1, source_target_pairs={{0,14},{2,0},{4,2},{6,4},{8,6},{10,8},{12,10},{14,12},{1,15},{3,1}... | collective-permute-start | bytes 393224 | tf_op jit(solution)/shard_map/reduce_a/ppermute | solution.py:23
  99.2 8.2 %collective-permute-start.20 = (f32[128,256]{1,0:T(8,128)S(1)}, f32[128,256]{1,0:T(8,128)S(1)}, u32[]{:S(2)}, u32[]{:S(2)}) collective-permute-start(f32[128,256]{1,0:T(8,128)S(1)} %pad_maximum_fusion.6), channel_id=1, source_target_pairs={{0,48},{16,0},{32,16},{48,32},{1,49},{17,1},{33,17},{49,33},{2,50}... | collective-permute-start | bytes 393224 | tf_op jit(solution)/shard_map/reduce_b2/ppermute | solution.py:23
  102.3 5.2 %collective-permute-start.18 = (f32[128,256]{1,0:T(8,128)S(1)}, f32[128,256]{1,0:T(8,128)S(1)}, u32[]{:S(2)}, u32[]{:S(2)}) collective-permute-start(f32[128,256]{1,0:T(8,128)S(1)} %pad_maximum_fusion.5), channel_id=1, source_target_pairs={{0,16},{16,32},{32,48},{48,0},{1,17},{17,33},{33,49},{49,1},{2,18}... | collective-permute-start | bytes 393224 | tf_op jit(solution)/shard_map/reduce_b2/ppermute | solution.py:23
  102.5 14.8 %copy-start.3 = (f32[128,256]{1,0:T(8,128)}, f32[128,256]{1,0:T(8,128)S(1)}, u32[]{:S(2)}) copy-start(f32[128,256]{1,0:T(8,128)S(1)} %fusion.8.a0) | copy-start | bytes 393220
  102.5 9.8 %collective-permute-start.16 = (f32[128,256]{1,0:T(8,128)S(1)}, f32[128,256]{1,0:T(8,128)S(1)}, u32[]{:S(2)}, u32[]{:S(2)}) collective-permute-start(f32[128,256]{1,0:T(8,128)S(1)} %fusion.8.a0), channel_id=1, source_target_pairs={{0,64},{64,128},{128,192},{192,0},{1,65},{65,129},{129,193},{193,1... | collective-permute-start | bytes 393224 | tf_op jit(solution)/shard_map/members/ppermute | solution.py:23
  103.8 9.6 %collective-permute-start.15 = (f32[128,256]{1,0:T(8,128)S(1)}, f32[128,256]{1,0:T(8,128)S(1)}, u32[]{:S(2)}, u32[]{:S(2)}) collective-permute-start(f32[128,256]{1,0:T(8,128)S(1)} %fusion.8.a0), channel_id=1, source_target_pairs={{0,128},{64,192},{128,0},{192,64},{1,129},{65,193},{129,1},{193,65... | collective-permute-start | bytes 393224 | tf_op jit(solution)/shard_map/members/ppermute | solution.py:23
  106.4 7.0 %collective-permute-start.14 = (f32[128,256]{1,0:T(8,128)S(1)}, f32[128,256]{1,0:T(8,128)S(1)}, u32[]{:S(2)}, u32[]{:S(2)}) collective-permute-start(f32[128,256]{1,0:T(8,128)S(1)} %fusion.8.a0), channel_id=1, source_target_pairs={{0,192},{64,0},{128,64},{192,128},{1,193},{65,1},{129,65},{193,129... | collective-permute-start | bytes 393224 | tf_op jit(solution)/shard_map/members/ppermute | solution.py:23
  108.4 8.9 %copy-start.4 = (f32[128,256]{1,0:T(8,128)}, f32[128,256]{1,0:T(8,128)S(1)}, u32[]{:S(2)}) copy-start(f32[128,256]{1,0:T(8,128)S(1)} %fusion.7.b0) | copy-start | bytes 393220
  108.4 5.1 %collective-permute-start.23 = (f32[128,256]{1,0:T(8,128)S(1)}, f32[128,256]{1,0:T(8,128)S(1)}, u32[]{:S(2)}, u32[]{:S(2)}) collective-permute-start(f32[128,256]{1,0:T(8,128)S(1)} %fusion.7.b0), channel_id=1, source_target_pairs={{0,64},{64,128},{128,192},{192,0},{1,65},{65,129},{129,193},{193,1... | collective-permute-start | bytes 393224 | tf_op jit(solution)/shard_map/members/ppermute | solution.py:23
  109.7 7.0 %collective-permute-start.22 = (f32[128,256]{1,0:T(8,128)S(1)}, f32[128,256]{1,0:T(8,128)S(1)}, u32[]{:S(2)}, u32[]{:S(2)}) collective-permute-start(f32[128,256]{1,0:T(8,128)S(1)} %fusion.7.b0), channel_id=1, source_target_pairs={{0,128},{64,192},{128,0},{192,64},{1,129},{65,193},{129,1},{193,65... | collective-permute-start | bytes 393224 | tf_op jit(solution)/shard_map/members/ppermute | solution.py:23
  112.3 5.0 %copy-start.6 = (f32[128,256]{1,0:T(8,128)}, f32[128,256]{1,0:T(8,128)S(1)}, u32[]{:S(2)}) copy-start(f32[128,256]{1,0:T(8,128)S(1)} %collective-permute-done.16.a3) | copy-start | bytes 393220
  112.3 5.0 %collective-permute-start.21 = (f32[128,256]{1,0:T(8,128)S(1)}, f32[128,256]{1,0:T(8,128)S(1)}, u32[]{:S(2)}, u32[]{:S(2)}) collective-permute-start(f32[128,256]{1,0:T(8,128)S(1)} %fusion.7.b0), channel_id=1, source_target_pairs={{0,192},{64,0},{128,64},{192,128},{1,193},{65,1},{129,65},{193,129... | collective-permute-start | bytes 393224 | tf_op jit(solution)/shard_map/members/ppermute | solution.py:23
  113.4 3.9 %copy-start.7 = (f32[128,256]{1,0:T(8,128)}, f32[128,256]{1,0:T(8,128)S(1)}, u32[]{:S(2)}) copy-start(f32[128,256]{1,0:T(8,128)S(1)} %collective-permute-done.15.a2) | copy-start | bytes 393220
  113.4 3.9 %copy-start.8 = (f32[128,256]{1,0:T(8,128)}, f32[128,256]{1,0:T(8,128)S(1)}, u32[]{:S(2)}) copy-start(f32[128,256]{1,0:T(8,128)S(1)} %collective-permute-done.14.a1) | copy-start | bytes 393220
  113.5 3.8 %copy-start.9 = (f32[128,256]{1,0:T(8,128)}, f32[128,256]{1,0:T(8,128)S(1)}, u32[]{:S(2)}) copy-start(f32[128,256]{1,0:T(8,128)S(1)} %collective-permute-done.23.b3) | copy-start | bytes 393220
  116.7 0.7 copy-start.10
  117.3 0.6 copy-start.11
  149.3 3.5 %collective-permute-start.26 = (bf16[80,512]{1,0:T(8,128)(2,1)}, bf16[80,512]{1,0:T(8,128)(2,1)S(1)}, u32[]{:S(2)}, u32[]{:S(2)}) collective-permute-start(bf16[80,512]{1,0:T(8,128)(2,1)} %get-tuple-element.27), channel_id=1, source_target_pairs={{0,48},{16,0},{32,16},{48,32},{1,49},{17,1},{33,17},{49,33},{2,50}... | collective-permute-start | bytes 245768 | tf_op jit(solution)/shard_map/params/ppermute | solution.py:23
  150.1 5.0 %collective-permute-start.25 = (bf16[80,512]{1,0:T(8,128)(2,1)}, bf16[80,512]{1,0:T(8,128)(2,1)S(1)}, u32[]{:S(2)}, u32[]{:S(2)}) collective-permute-start(bf16[80,512]{1,0:T(8,128)(2,1)} %get-tuple-element.27), channel_id=1, source_target_pairs={{0,32},{16,48},{32,0},{48,16},{1,33},{17,49},{33,1},{49,17},{2,34}... | collective-permute-start | bytes 245768 | tf_op jit(solution)/shard_map/params/ppermute | solution.py:23
  151.3 5.7 %collective-permute-start.24 = (bf16[80,512]{1,0:T(8,128)(2,1)}, bf16[80,512]{1,0:T(8,128)(2,1)S(1)}, u32[]{:S(2)}, u32[]{:S(2)}) collective-permute-start(bf16[80,512]{1,0:T(8,128)(2,1)} %get-tuple-element.27), channel_id=1, source_target_pairs={{0,16},{16,32},{32,48},{48,0},{1,17},{17,33},{33,49},{49,1},{2,18}... | collective-permute-start | bytes 245768 | tf_op jit(solution)/shard_map/params/ppermute | solution.py:23
  176.1 9.6 %collective-permute-start.29 = (bf16[8,48,512]{2,1,0:T(8,128)(2,1)S(1)}, bf16[8,48,512]{2,1,0:T(8,128)(2,1)S(1)}, u32[]{:S(2)}, u32[]{:S(2)}) collective-permute-start(bf16[8,48,512]{2,1,0:T(8,128)(2,1)S(1)} %all_to_all.11.refs_0_), channel_id=1, source_target_pairs={{0,16},{16,32},{32,48},{48,0},{1,17},{17,33},{33,49},{49,1},{2,18}... | collective-permute-start | bytes 1179656 | tf_op jit(solution)/shard_map/params/ppermute | solution.py:23
  176.1 14.9 %collective-permute-start.28 = (bf16[8,48,512]{2,1,0:T(8,128)(2,1)S(1)}, bf16[8,48,512]{2,1,0:T(8,128)(2,1)S(1)}, u32[]{:S(2)}, u32[]{:S(2)}) collective-permute-start(bf16[8,48,512]{2,1,0:T(8,128)(2,1)S(1)} %all_to_all.11.refs_0_), channel_id=1, source_target_pairs={{0,32},{16,48},{32,0},{48,16},{1,33},{17,49},{33,1},{49,17},{2,34}... | collective-permute-start | bytes 1179656 | tf_op jit(solution)/shard_map/params/ppermute | solution.py:23
  177.8 16.5 %collective-permute-start.27 = (bf16[8,48,512]{2,1,0:T(8,128)(2,1)S(1)}, bf16[8,48,512]{2,1,0:T(8,128)(2,1)S(1)}, u32[]{:S(2)}, u32[]{:S(2)}) collective-permute-start(bf16[8,48,512]{2,1,0:T(8,128)(2,1)S(1)} %all_to_all.11.refs_0_), channel_id=1, source_target_pairs={{0,48},{16,0},{32,16},{48,32},{1,49},{17,1},{33,17},{49,33},{2,50}... | collective-permute-start | bytes 1179656 | tf_op jit(solution)/shard_map/params/ppermute | solution.py:23
  199.1 14.3 %collective-permute-start.30 = (bf16[8,4,80,512]{3,2,1,0:T(8,128)(2,1)}, bf16[8,4,80,512]{3,2,1,0:T(8,128)(2,1)S(1)}, u32[]{:S(2)}, u32[]{:S(2)}) collective-permute-start(bf16[8,4,80,512]{3,2,1,0:T(8,128)(2,1)} %bitcast.89), channel_id=1, source_target_pairs={{0,1},{1,0},{2,3},{3,2},{4,5},{5,4},{6,7},{7,6},{8,9},{9,8},{10,11... | collective-permute-start | bytes 7864328 | tf_op jit(solution)/shard_map/params/ppermute | solution.py:23
  202.4 5.0 %collective-permute-start.31 = (bf16[8,48,512]{2,1,0:T(8,128)(2,1)S(1)}, bf16[8,48,512]{2,1,0:T(8,128)(2,1)S(1)}, u32[]{:S(2)}, u32[]{:S(2)}) collective-permute-start(bf16[8,48,512]{2,1,0:T(8,128)(2,1)S(1)} %all_to_all.11.refs_0_), channel_id=1, source_target_pairs={{0,1},{1,0},{2,3},{3,2},{4,5},{5,4},{6,7},{7,6},{8,9},{9,8},{10,11... | collective-permute-start | bytes 1179656 | tf_op jit(solution)/shard_map/params/ppermute | solution.py:23
  202.4 5.5 %collective-permute-start.32 = (bf16[8,48,512]{2,1,0:T(8,128)(2,1)S(1)}, bf16[8,48,512]{2,1,0:T(8,128)(2,1)S(1)}, u32[]{:S(2)}, u32[]{:S(2)}) collective-permute-start(bf16[8,48,512]{2,1,0:T(8,128)(2,1)S(1)} %collective-permute-done.27.refs_1_), channel_id=1, source_target_pairs={{0,1},{1,0},{2,3},{3,2},{4,5},{5,4},{6,7},{7,6},{8,9},{9,8},{10,11... | collective-permute-start | bytes 1179656 | tf_op jit(solution)/shard_map/params/ppermute | solution.py:23
  202.9 5.6 %collective-permute-start.33 = (bf16[8,48,512]{2,1,0:T(8,128)(2,1)S(1)}, bf16[8,48,512]{2,1,0:T(8,128)(2,1)S(1)}, u32[]{:S(2)}, u32[]{:S(2)}) collective-permute-start(bf16[8,48,512]{2,1,0:T(8,128)(2,1)S(1)} %collective-permute-done.28.refs_2_), channel_id=1, source_target_pairs={{0,1},{1,0},{2,3},{3,2},{4,5},{5,4},{6,7},{7,6},{8,9},{9,8},{10,11... | collective-permute-start | bytes 1179656 | tf_op jit(solution)/shard_map/params/ppermute | solution.py:23
  202.9 6.1 %collective-permute-start.34 = (bf16[8,48,512]{2,1,0:T(8,128)(2,1)S(1)}, bf16[8,48,512]{2,1,0:T(8,128)(2,1)S(1)}, u32[]{:S(2)}, u32[]{:S(2)}) collective-permute-start(bf16[8,48,512]{2,1,0:T(8,128)(2,1)S(1)} %collective-permute-done.29.refs_3_), channel_id=1, source_target_pairs={{0,1},{1,0},{2,3},{3,2},{4,5},{5,4},{6,7},{7,6},{8,9},{9,8},{10,11... | collective-permute-start | bytes 1179656 | tf_op jit(solution)/shard_map/params/ppermute | solution.py:23
  209.1 1.7 copy-start
Sparse Core Ops, SparseCore 0:
  25.7 57.0 reduce-scatter.1
  158.8 40.2 all-gather.1

commit v3 on v2

--- a/solution.py
+++ b/solution.py
@@ -33,7 +33,7 @@
     return jnp.concatenate([whole[:rows], whole[rows:] + part], axis=0)
 
 
-def ring_reduce(chunk, axis):
+def ring_reduce(chunk, axis, gates):
     size = lax.axis_size(axis)
     half = size // 2
     far = chunk(half)
@@ -45,6 +45,8 @@
             send_up, send_down = add_top(chunk(reach), up), add_bottom(chunk(-reach), down)
         else:
             send_up, send_down = chunk(reach) + up, chunk(-reach) + down
+        if reach in gates:
+            send_up, send_down = gates[reach](send_up, send_down)
         up = shifted(send_up, axis, 1)
         down = shifted(send_down, axis, -1)
     return chunk(0) + up + down
@@ -68,28 +70,44 @@
     return [pl.BlockSpec(memory_space=pltpu.VMEM)] * count
 
 
-def split_kernel(block, grads_ref, kept_ref, given_ref):
+def split_kernel(block, colour, grads_ref, kept_ref, given_ref):
     low = lax.axis_index("core") == 0
-    for z in range(8):
-        for x in range(4):
-            first = grads_ref[:, pl.ds((x * 16 + z * 2) * block, block)]
-            second = grads_ref[:, pl.ds((x * 16 + z * 2 + 1) * block, block)]
-            place = pl.ds((z * 4 + x) * block, block)
-            kept_ref[:, place] = jnp.where(low, first, second)
-            given_ref[:, place] = jnp.where(low, second, first)
-
-
-def split_columns(grads, block):
+    half = block // 2
+    lane = lax.broadcasted_iota(jnp.int32, (grads_ref.shape[0], block), 1)
+
+    def swapped_halves(value):
+        return pltpu.roll(value.astype(jnp.float32), half, 1).astype(value.dtype)
+
+    def pair(left, right):
+        if colour == "A":
+            return jnp.where(lane < half, left, swapped_halves(right))
+        return jnp.where(lane < half, swapped_halves(left), right)
+
+    def block_at(x, z, core):
+        return grads_ref[:, pl.ds((x * 16 + z * 2 + core) * block, block)]
+
+    if colour == "A":
+        order = [(x, z) for x in range(4) for z in range(8)]
+    else:
+        order = [(x, z) for z in range(8) for x in range(4)]
+    for index in range(0, len(order), 2):
+        sides = [pair(*(block_at(*place, core) for place in order[index : index + 2])) for core in range(2)]
+        where = pl.ds(index * half, block)
+        kept_ref[:, where] = jnp.where(low, sides[0], sides[1])
+        given_ref[:, where] = jnp.where(low, sides[1], sides[0])
+
+
+def split_columns(grads, block, colour):
     tokens, features = grads.shape
     step = tokens // 4
-    half = jax.ShapeDtypeStruct((tokens, features // 2), grads.dtype)
-    half_spec = pl.BlockSpec((step, features // 2), lambda i: (i, 0))
+    part = jax.ShapeDtypeStruct((tokens, features // 4), grads.dtype)
+    part_spec = pl.BlockSpec((step, features // 4), lambda i: (i, 0))
     return pl.pallas_call(
-        lambda *refs: split_kernel(block, *refs),
+        functools.partial(split_kernel, block, colour),
         grid=(4,),
         in_specs=[pl.BlockSpec((step, features), lambda i: (i, 0))],
-        out_specs=[half_spec, half_spec],
-        out_shape=[half, half],
+        out_specs=[part_spec, part_spec],
+        out_shape=[part, part],
         name="split_columns",
     )(grads)
 
@@ -99,11 +117,11 @@
 
 def gram_kernel(a0, a1, a2, a3, b0, b1, b2, b3, members_ref, rows_ref):
     place = lax.axis_index("rep")
-    half = a0.shape[1]
+    half = a0.shape[0]
     for step, (left, right) in enumerate(zip((a0, a1, a2, a3), (b0, b1, b2, b3))):
         member = lax.rem(place + step, 4)
-        members_ref[member, :, :half] = left[...]
-        members_ref[member, :, half:] = right[...]
+        members_ref[member, :half] = left[...]
+        members_ref[member, half:] = right[...]
     lane = lax.broadcasted_iota(jnp.int32, (1, 128), 1)
     row = jnp.zeros((1, 128), jnp.float32)
     for index, (i, j) in enumerate(PAIRS):
@@ -112,13 +130,13 @@
 
 
 def gram_rows(pieces_a, pieces_b):
-    rows, half = pieces_a[0].shape
+    half, width = pieces_a[0].shape
     return pl.pallas_call(
         gram_kernel,
         in_specs=in_vmem(8),
         out_specs=in_vmem(2),
         out_shape=[
-            jax.ShapeDtypeStruct((4, rows, 2 * half), jnp.float32),
+            jax.ShapeDtypeStruct((4, 2 * half, width), jnp.float32),
             jax.ShapeDtypeStruct((64, 1, 128), jnp.float32),
         ],
         name="gram_rows",
@@ -186,8 +204,9 @@
     for piece, (colour, side, step) in zip(pieces, order):
         owner = core if side == 0 else 1 - core
         if colour == 0:
-            for x in range(4):
-                copies.append((piece.at[:, x], out.at[x, :, owner, pl.ds(0, size_a)]))
+            for up in range(4):
+                x = lax.rem(x_place + up, 4)
+                copies.append((piece.at[:, up], out.at[x, :, owner, pl.ds(0, size_a)]))
         else:
             x = lax.rem(x_place + step, 4)
             rows = piece.shape[1]
@@ -219,25 +238,18 @@
 def gathered(params_a, params_b):
     rows_a, width = params_a.shape
     rows_b = params_b.shape[0]
-    x_place = lax.axis_index("x")
-    near = neighbours(params_a, "x")
-    ordered = []
-    for x in range(4):
-        value = near[0]
-        for step in range(1, 4):
-            value = jnp.where((x_place + step) % 4 == x, near[step], value)
-        ordered.append(value)
-    line = jnp.concatenate(ordered, axis=0)
+    line = jnp.concatenate(neighbours(params_a, "x"), axis=0)
     line, params_b = lax.optimization_barrier((line, params_b))
     own_a = lax.all_gather(line, "z", axis=0, tiled=True).reshape(8, 4, rows_a, width)
     column = lax.all_to_all(jnp.broadcast_to(params_b[None], (8, rows_b, width)), "z", 0, 0)
     own_b = neighbours(column, "x")
-    own_a, *own_b = lax.optimization_barrier((own_a, *own_b))
     other_b = [shifted(piece, "core", 1) for piece in own_b]
+    order = [(1, side, step) for side in range(2) for step in range(4)]
+    shape = (4, 8, 2, rows_a + rows_b, width)
+    out = placed(None, [*own_b, *other_b], order, shape, rows_a)
+    own_a, out = lax.optimization_barrier((own_a, out))
     other_a = shifted(own_a, "core", 1)
-    order = [(1, 0, step) for step in range(4)] + [(1, 1, step) for step in range(4)] + [(0, 0, 0)]
-    shape = (4, 8, 2, rows_a + rows_b, width)
-    out = placed(None, [*own_b, *other_b, own_a], order, shape, rows_a)
+    out = placed(out, [own_a], [(0, 0, 0)], shape, rows_a)
     out = placed(out, [other_a], [(0, 1, 0)], shape, rows_a)
     return out.reshape(-1, width)
 
@@ -245,34 +257,65 @@
 def local(activations, output_grads, master, first_moment, second_moment):
     width = activations.shape[1]
     rows = master.shape[0]
-    half = width // 2
+    half = rows // 2
+    x_place = lax.axis_index("x")
+
+    def product(grad_columns, act_rows):
+        return lax.dot_general(
+            grad_columns, act_rows, contract_first, preferred_element_type=jnp.float32
+        )
+
+    def pair_up_parts(own, given):
+        return jnp.concatenate([own, shifted(given, "core", 1)], axis=0)
+
+    def pair_up(own):
+        return pair_up_parts(own, own)
+
     with jax.named_scope("core_swap"):
-        kept, given = split_columns(output_grads, rows)
-        grads = jnp.concatenate([kept, shifted(given, "core", 1)], axis=0)
-        acts = jnp.concatenate([activations, shifted(activations, "core", 1)], axis=0)
-
-    def product(act_columns):
-        return lax.dot_general(
-            grads, act_columns, contract_first, preferred_element_type=jnp.float32
+        near_acts = neighbours(activations, "x")
+        kept_b, given_b = split_columns(output_grads, rows, "B")
+        own_acts = pair_up(activations)
+        grads_b = pair_up_parts(kept_b, given_b)
+        kept_a, given_a = split_columns(output_grads, rows, "A")
+        given_a, own_acts, near_acts[1], near_acts[3] = lax.optimization_barrier(
+            (given_a, own_acts, near_acts[1], near_acts[3])
         )
-
+        grads_a = pair_up_parts(kept_a, given_a)
+        line_acts = [own_acts] + [pair_up(part) for part in near_acts[1:]]
     with jax.named_scope("reduce_b"):
-        sums_b = lax.psum_scatter(
-            product(acts[:, half:]), "z", scatter_dimension=0, tiled=True
-        )
+        sums_b = product(grads_b, line_acts[0])
+        sums_b = lax.psum_scatter(sums_b, "z", scatter_dimension=0, tiled=True)
+        chunk_b = by_place(sums_b.reshape(4, half, width), "x")
+        chunks_b = [chunk_b(step) for step in range(4)]
     with jax.named_scope("reduce_a"):
-        sums_a = product(acts[:, :half]).reshape(8, 4, rows, half)
-        x_place = lax.axis_index("x")
-
-        def chunk_a(step):
-            return lax.dynamic_index_in_dim(sums_a, (x_place + step + 4) % 4, 1, keepdims=False)
-
-        sums_a = ring_reduce(chunk_a, "x")
-        grad_a = ring_reduce(by_place(sums_a, "z"), "z")
-    with jax.named_scope("reduce_b2"):
-        grad_b = ring_reduce(by_place(sums_b.reshape(4, rows, half), "x"), "x")
+        strip = 8 * half
+
+        def columns_of(step):
+            return lax.dynamic_slice_in_dim(grads_a, (x_place + step) % 4 * strip, strip, 1)
+
+        line_grads = [
+            columns_of(0),
+            shifted(columns_of(3), "x", -1),
+            shifted(columns_of(2), "x", 2),
+            shifted(columns_of(1), "x", 1),
+        ]
+        sums_a = sum(product(part, acts) for part, acts in zip(line_grads, line_acts))
+
+        exchanged_b = []
+
+        def start_b(send_up, send_down):
+            send_up, send_down, *chunks = lax.optimization_barrier(
+                (send_up, send_down, *chunks_b[1:])
+            )
+            with jax.named_scope("reduce_b2"):
+                near = shifted(chunks[2], "x", -1) + shifted(chunks[0], "x", 1)
+                exchanged_b.append(chunks_b[0] + (near + shifted(chunks[1], "x", 2)))
+            return send_up, send_down
+
+        gates = {2: start_b}
+        grad_a = ring_reduce(by_place(sums_a.reshape(8, half, width), "z"), "z", gates)
     with jax.named_scope("members"):
-        members, row = gram_rows(neighbours(grad_a, "rep"), neighbours(grad_b, "rep"))
+        members, row = gram_rows(neighbours(grad_a, "rep"), neighbours(exchanged_b.pop(), "rep"))
     with jax.named_scope("gram"):
         everyone = lax.all_to_all(row, GROUP, 0, 0)
     with jax.named_scope("adamw"):

time: 222 us -> 210 us (0.946)
  waiting for transfers between devices: 85.3 us -> 55.1 us
  starting transfers between devices: 43.3 us -> 66.1 us
  blocking collectives: 42.6 us -> 36.9 us
  Pallas kernels: 14.5 us -> 19.3 us
  other arithmetic: 6.42 us -> 2.75 us
    ppermute x35 -> x40, waiting for transfers between devices: 80.5 us -> 52.8 us  [shifted(): lax.ppermute(value, axis, [(i, (i + step) % size) for i in range(size)])]
    ppermute x35 -> x40, starting transfers between devices: 43.2 us -> 66 us  [shifted(): lax.ppermute(value, axis, [(i, (i + step) % size) for i in range(size)])]
    all_to_all x1, blocking collectives: 26.1 us -> 21.1 us  [local(): everyone = lax.all_to_all(row, GROUP, 0, 0)]
    all_gather x1, waiting for transfers between devices: 4.82 us -> 0.02 us  [gathered(): lax.all_gather(line, 'z', axis=0, tiled=True).reshape(8, 4, rows_a, width)]
    pallas_call x1 -> x2, Pallas kernels: 5.15 us -> 9.24 us  [split_columns(): pl.pallas_call(functools.partial(split_kernel, block, colour), grid=(4,),...]
    unnamed x26 -> x33, local copies, waits for them, and re-layouts: 6.2 us -> 2.54 us
    add x3 -> x1, other arithmetic: 2.41 us -> 0.03 us  [ring_reduce(): return chunk(0) + up + down]
    reduce_scatter x1, waiting for transfers between devices: 0.01 us -> 2.29 us  [local(): sums_b = lax.psum_scatter(sums_b, 'z', scatter_dimension=0, tiled=True)]
  transfers between devices with their start and end apart: 37 -> 42, of which waited for: 23 -> 21; matrix products, arithmetic and copies ran while one was open for 5% -> 4% of each run, Pallas kernels for 1% -> 4%
where the time goes in v3:
time: 210 us
  starting transfers between devices  66.1 us (31%)
  waiting for transfers between devices  55.1 us (26%)
  blocking collectives  36.9 us (18%)
  Pallas kernels  19.3 us (9%)
  between operations  14.4 us (7%)
  matrix products  8.4 us (4%)
  local copies, waits for them, and re-layouts  6.72 us (3%)
  other arithmetic  2.75 us (1%)
    ppermute x40, starting transfers between devices, shifted(): lax.ppermute(value, axis, [(i, (i + step) % size) for i in range(size)])  66 us
    ppermute x40, waiting for transfers between devices, shifted(): lax.ppermute(value, axis, [(i, (i + step) % size) for i in range(size)])  52.8 us
    all_to_all x1, blocking collectives, local(): everyone = lax.all_to_all(row, GROUP, 0, 0)  21.1 us
    all_to_all x1, blocking collectives, gathered(): lax.all_to_all(jnp.broadcast_to(params_b[None], (8, rows_b, width)), 'z',...  15.8 us
    pallas_call x2, Pallas kernels, split_columns(): pl.pallas_call(functools.partial(split_kernel, block, colour), grid=(4,),...  9.24 us
    dot_general x5, matrix products, product(): lax.dot_general(grad_columns, act_rows, contract_first, preferred_element...  8.4 us
    pallas_call x3, Pallas kernels, placed(): pl.pallas_call(functools.partial(place_kernel, size_a, order), in_specs=i...  4.78 us
  transfers between devices with their start and end apart: 42, of which 21 were waited for; matrix products, arithmetic and copies ran while one was open for 4% of the time, Pallas kernels for 4%

profile of v3, /device:TPU:1, one launch (start us, length us, event | category | flops | bytes accessed | tf_op | source)
XLA Modules:
  0.0 209.6 jit_solution(8056355430250009240)
XLA Ops:
  7.2 4.6 %split_columns.3 = (bf16[256,2048]{1,0:T(8,128)(2,1)}, bf16[256,2048]{1,0:T(8,128)(2,1)}) custom-call(bf16[256,8192]{1,0:T(8,128)(2,1)} %grads_ref.3), custom_call_target="tpu_custom_call" | custom-call | tf_op jit(solution)/shard_map/core_swap/split_columns/pallas_call | solution.py:105
  11.8 3.2 %collective-permute-start.15 = (bf16[256,2048]{1,0:T(8,128)(2,1)}, bf16[256,2048]{1,0:T(8,128)(2,1)S(1)}, u32[]{:S(2)}, u32[]{:S(2)}) collective-permute-start(bf16[256,2048]{1,0:T(8,128)(2,1)} %get-tuple-element.35), channel_id=1, source_target_pairs={{0,1},{1,0},{2,3},{3,2},{4,5},{5,4},{6,7},{7,6},{8,9},{9,8},{10,11... | collective-permute-start | bytes 3145736 | tf_op jit(solution)/shard_map/core_swap/ppermute | solution.py:23
  15.2 0.7 collective-permute-start.1
  16.6 4.6 %split_columns.2 = (bf16[256,2048]{1,0:T(8,128)(2,1)}, bf16[256,2048]{1,0:T(8,128)(2,1)}) custom-call(bf16[256,8192]{1,0:T(8,128)(2,1)} %grads_ref.3), custom_call_target="tpu_custom_call" | custom-call | tf_op jit(solution)/shard_map/core_swap/split_columns/pallas_call | solution.py:105
  21.3 1.4 collective-permute-done.1
  22.7 1.5 collective-permute-done.2
  24.3 3.3 %fusion = f32[2048,512]{1,0:T(8,128)} fusion(bf16[512,512]{1,0:T(8,128)(2,1)S(1)} %pad_maximum_fusion, bf16[256,2048]{1,0:T(8,128)(2,1)S(1)} %collective-permute-done.15, bf16[256,2048]{1,0:T(8,128)(2,1)S(1)} %copy-done.13), kind=kOutput, calls=%fused_computation | convolution fusion | flops 1077936128 | bytes 6815744 | tf_op jit(solution)/shard_map/reduce_b/dot_general | solution.py:264
  27.7 1.7 collective-permute-start.3
  29.5 2.5 %collective-permute-done.3 = bf16[256,2048]{1,0:T(8,128)(2,1)} collective-permute-done((bf16[256,2048]{1,0:T(8,128)(2,1)}, bf16[256,2048]{1,0:T(8,128)(2,1)}, u32[]{:S(2)}, u32[]{:S(2)}) %collective-permute-start.3) | collective-permute-done | bytes 1048608 | tf_op jit(solution)/shard_map/core_swap/ppermute | solution.py:23
  32.0 1.3 constant_dynamic-update-slice_fusion
  33.3 1.0 constant_dynamic-slice_fusion.2
  34.4 1.2 collective-permute-start.7
  35.5 0.9 collective-permute-start.5
  36.6 6.6 %collective-permute-done.7 = bf16[256,512]{1,0:T(8,128)(2,1)} collective-permute-done((bf16[256,512]{1,0:T(8,128)(2,1)S(1)}, bf16[256,512]{1,0:T(8,128)(2,1)}, u32[]{:S(2)}, u32[]{:S(2)}) %collective-permute-start.7) | collective-permute-done | bytes 262176 | tf_op jit(solution)/shard_map/core_swap/ppermute | solution.py:23
  43.2 2.6 %collective-permute-start.8 = (bf16[256,512]{1,0:T(8,128)(2,1)}, bf16[256,512]{1,0:T(8,128)(2,1)S(1)}, u32[]{:S(2)}, u32[]{:S(2)}) collective-permute-start(bf16[256,512]{1,0:T(8,128)(2,1)} %collective-permute-done.7), channel_id=1, source_target_pairs={{0,1},{1,0},{2,3},{3,2},{4,5},{5,4},{6,7},{7,6},{8,9},{9,8},{10,11... | collective-permute-start | bytes 786440 | tf_op jit(solution)/shard_map/core_swap/ppermute | solution.py:23
  45.9 1.2 collective-permute-start.6
  47.7 1.7 fusion.6
  49.4 7.1 %collective-permute-done.9 = bf16[512,512]{1,0:T(8,128)(2,1)} collective-permute-done((bf16[512,512]{1,0:T(8,128)(2,1)S(1)}, bf16[512,512]{1,0:T(8,128)(2,1)}, u32[]{:S(2)}, u32[]{:S(2)}) %collective-permute-start.9) | collective-permute-done | bytes 524320 | tf_op jit(solution)/shard_map/reduce_a/ppermute | solution.py:23
  56.5 1.5 fusion.14
  58.1 7.5 %collective-permute-done.6 = bf16[512,512]{1,0:T(8,128)(2,1)S(1)} collective-permute-done((bf16[512,512]{1,0:T(8,128)(2,1)S(1)}, bf16[512,512]{1,0:T(8,128)(2,1)S(1)}, u32[]{:S(2)}, u32[]{:S(2)}) %collective-permute-start.6) | collective-permute-done | bytes 524320 | tf_op jit(solution)/shard_map/reduce_a/ppermute | solution.py:23
  65.6 1.4 fusion.10
  67.5 1.7 collective-permute-start.11
  69.2 4.2 %collective-permute-start.13 = (f32[32,512]{1,0:T(8,128)S(1)}, f32[32,512]{1,0:T(8,128)S(1)}, u32[]{:S(2)}, u32[]{:S(2)}) collective-permute-start(f32[32,512]{1,0:T(8,128)S(1)} %get-tuple-element.61), channel_id=1, source_target_pairs={{0,14},{2,0},{4,2},{6,4},{8,6},{10,8},{12,10},{14,12},{1,15},{3,1}... | collective-permute-start | bytes 196616 | tf_op jit(solution)/shard_map/reduce_a/ppermute | solution.py:23
  73.5 3.5 %collective-permute-done.11 = f32[32,512]{1,0:T(8,128)S(1)} collective-permute-done((f32[32,512]{1,0:T(8,128)S(1)}, f32[32,512]{1,0:T(8,128)S(1)}, u32[]{:S(2)}, u32[]{:S(2)}) %collective-permute-start.11) | collective-permute-done | bytes 65568 | tf_op jit(solution)/shard_map/reduce_a/ppermute | solution.py:23
  77.1 2.8 %collective-permute-start.14 = (f32[64,512]{1,0:T(8,128)S(1)}, f32[64,512]{1,0:T(8,128)S(1)}, u32[]{:S(2)}, u32[]{:S(2)}) collective-permute-start(f32[64,512]{1,0:T(8,128)S(1)} %pad_maximum_fusion.3), channel_id=1, source_target_pairs={{0,14},{2,0},{4,2},{6,4},{8,6},{10,8},{12,10},{14,12},{1,15},{3,1}... | collective-permute-start | bytes 393224 | tf_op jit(solution)/shard_map/reduce_a/ppermute | solution.py:23
  79.9 6.2 %collective-permute-done.12 = f32[64,512]{1,0:T(8,128)S(1)} collective-permute-done((f32[64,512]{1,0:T(8,128)S(1)}, f32[64,512]{1,0:T(8,128)S(1)}, u32[]{:S(2)}, u32[]{:S(2)}) %collective-permute-start.12) | collective-permute-done | bytes 131104 | tf_op jit(solution)/shard_map/reduce_a/ppermute | solution.py:23
  86.1 2.3 %reduce-scatter.2.cloned.1.call-done = f32[256,512]{1,0:T(8,128)} async-done(((f32[2048,512]{1,0:T(8,128)}), f32[256,512]{1,0:T(8,128)}) %reduce-scatter.2.cloned.1.call-update) | async-done | bytes 524304 | tf_op jit(solution)/shard_map/reduce_b/reduce_scatter | solution.py:287
  88.4 1.1 dynamic-slice_bitcast_fusion
  89.5 2.7 %collective-permute-start.18 = (f32[64,512]{1,0:T(8,128)S(1)}, f32[64,512]{1,0:T(8,128)S(1)}, u32[]{:S(2)}, u32[]{:S(2)}) collective-permute-start(f32[64,512]{1,0:T(8,128)S(1)} %get-tuple-element.37), channel_id=1, source_target_pairs={{0,14},{2,0},{4,2},{6,4},{8,6},{10,8},{12,10},{14,12},{1,15},{3,1}... | collective-permute-start | bytes 393224 | tf_op jit(solution)/shard_map/reduce_a/ppermute | solution.py:23
  92.9 0.7 collective-permute-start.24
  93.6 3.1 %collective-permute-start.25 = (f32[64,512]{1,0:T(8,128)S(1)}, f32[64,512]{1,0:T(8,128)S(1)}, u32[]{:S(2)}, u32[]{:S(2)}) collective-permute-start(f32[64,512]{1,0:T(8,128)S(1)} %get-tuple-element.40), channel_id=1, source_target_pairs={{0,32},{16,48},{32,0},{48,16},{1,33},{17,49},{33,1},{49,17},{2,34}... | collective-permute-start | bytes 393224 | tf_op jit(solution)/shard_map/reduce_a/reduce_b2/ppermute | solution.py:23
  96.9 2.7 %collective-permute-start.19 = (f32[64,512]{1,0:T(8,128)S(1)}, f32[64,512]{1,0:T(8,128)S(1)}, u32[]{:S(2)}, u32[]{:S(2)}) collective-permute-start(f32[64,512]{1,0:T(8,128)S(1)} %get-tuple-element.56), channel_id=1, source_target_pairs={{0,14},{2,0},{4,2},{6,4},{8,6},{10,8},{12,10},{14,12},{1,15},{3,1}... | collective-permute-start | bytes 393224 | tf_op jit(solution)/shard_map/reduce_a/ppermute | solution.py:23
  99.6 1.8 collective-permute-done.25
  101.3 0.9 bitcast_add_fusion.b0
  102.3 1.3 collective-permute-start.28
  103.6 2.4 %collective-permute-start.27 = (f32[64,512]{1,0:T(8,128)S(1)}, f32[64,512]{1,0:T(8,128)S(1)}, u32[]{:S(2)}, u32[]{:S(2)}) collective-permute-start(f32[64,512]{1,0:T(8,128)S(1)} %bitcast_add_fusion.b0), channel_id=1, source_target_pairs={{0,128},{64,192},{128,0},{192,64},{1,129},{65,193},{129,1},{193,65... | collective-permute-start | bytes 393224 | tf_op jit(solution)/shard_map/members/ppermute | solution.py:23
  106.0 1.2 collective-permute-start.26
  107.6 0.9 collective-permute-start.21
  108.5 1.6 collective-permute-start.20
  110.1 3.2 %collective-permute-done.22.a3 = f32[64,512]{1,0:T(8,128)S(1)} collective-permute-done((f32[64,512]{1,0:T(8,128)S(1)}, f32[64,512]{1,0:T(8,128)S(1)}, u32[]{:S(2)}, u32[]{:S(2)}) %collective-permute-start.22) | collective-permute-done | bytes 131104 | tf_op jit(solution)/shard_map/members/ppermute | solution.py:23
  113.3 1.7 collective-permute-done.21.a2
  115.0 1.1 collective-permute-done.20.a1
  116.8 2.3 %gram_rows.1 = (f32[4,128,512]{2,1,0:T(8,128)}, f32[64,1,128]{2,1,0:T(1,128)}) custom-call(f32[64,512]{1,0:T(8,128)} %copy-done.4, f32[64,512]{1,0:T(8,128)} %copy-done.12, f32[64,512]{1,0:T(8,128)} %copy-done.11, f32[64,512]{1,0:T(8,128)} %copy-done.10, f32[64,512]{1,0:T(8,128)} %copy-done.5, f32[64,512]{1,0:T(8,128)} %copy-done.9, f32[64,512]{1,0:T(8,128)} %copy-done.8, ...), custom_call_target="tpu_custom_call" | custom-call | tf_op jit(solution)/shard_map/members/gram_rows/pallas_call | solution.py:134
  119.1 21.1 %all_to_all.10.everyone_ref = f32[64,1,128]{2,1,0:T(1,128)} all-to-all(f32[64,1,128]{2,1,0:T(1,128)} %get-tuple-element.41), channel_id=1, replica_groups=mesh['rep'=4,'x'=4,'z'=8,'core'=2] {'x','z','core'}, dimensions={0} | all-to-all | bytes 65536 | tf_op jit(solution)/shard_map/gram/all_to_all | solution.py:320
  140.2 2.9 %updated.1 = (f32[128,512]{1,0:T(8,128)}, f32[128,512]{1,0:T(8,128)}, f32[128,512]{1,0:T(8,128)}, bf16[80,512]{1,0:T(8,128)(2,1)}, bf16[48,512]{1,0:T(8,128)(2,1)}) custom-call(f32[64,1,128]{2,1,0:T(1,128)} %all_to_all.10.everyone_ref, f32[4,128,512]{2,1,0:T(8,128)} %get-tuple-element.42.members_ref, f32[128,512]{1,0:T(8,128)} %master_ref.1, ...), custom_call_target="tpu_custom_call" | custom-call | tf_op jit(solution)/shard_map/adamw/updated/pallas_call | solution.py:191
  143.4 1.6 collective-permute-start.30
  145.0 1.2 collective-permute-start.29
  146.2 2.5 %collective-permute-done.31 = bf16[80,512]{1,0:T(8,128)(2,1)S(1)} collective-permute-done((bf16[80,512]{1,0:T(8,128)(2,1)}, bf16[80,512]{1,0:T(8,128)(2,1)S(1)}, u32[]{:S(2)}, u32[]{:S(2)}) %collective-permute-start.31) | collective-permute-done | bytes 81952 | tf_op jit(solution)/shard_map/params/ppermute | solution.py:23
  148.8 0.8 collective-permute-done.30
  150.1 1.6 pad_maximum_fusion.1
  151.7 0.8 broadcast_in_dim.2
  152.6 15.8 %all_to_all.11.refs_0_ = bf16[8,48,512]{2,1,0:T(8,128)(2,1)S(1)} all-to-all(bf16[8,48,512]{2,1,0:T(8,128)(2,1)S(1)} %broadcast_in_dim.2), channel_id=1, replica_groups=mesh['rep'=4,'x'=4,'z'=8,'core'=2] {'z'}, dimensions={0} | all-to-all | bytes 786432 | tf_op jit(solution)/shard_map/params/all_to_all | solution.py:244
  168.4 1.9 collective-permute-start.34
  170.3 3.5 %collective-permute-start.33 = (bf16[8,48,512]{2,1,0:T(8,128)(2,1)S(1)}, bf16[8,48,512]{2,1,0:T(8,128)(2,1)S(1)}, u32[]{:S(2)}, u32[]{:S(2)}) collective-permute-start(bf16[8,48,512]{2,1,0:T(8,128)(2,1)S(1)} %all_to_all.11.refs_0_), channel_id=1, source_target_pairs={{0,32},{16,48},{32,0},{48,16},{1,33},{17,49},{33,1},{49,17},{2,34}... | collective-permute-start | bytes 1179656 | tf_op jit(solution)/shard_map/params/ppermute | solution.py:23
  173.9 4.6 %collective-permute-start.35 = (bf16[8,48,512]{2,1,0:T(8,128)(2,1)S(1)}, bf16[8,48,512]{2,1,0:T(8,128)(2,1)S(1)}, u32[]{:S(2)}, u32[]{:S(2)}) collective-permute-start(bf16[8,48,512]{2,1,0:T(8,128)(2,1)S(1)} %all_to_all.11.refs_0_), channel_id=1, source_target_pairs={{0,1},{1,0},{2,3},{3,2},{4,5},{5,4},{6,7},{7,6},{8,9},{9,8},{10,11... | collective-permute-start | bytes 1179656 | tf_op jit(solution)/shard_map/params/ppermute | solution.py:23
  178.5 7.8 %collective-permute-start.38 = (bf16[8,48,512]{2,1,0:T(8,128)(2,1)S(1)}, bf16[8,48,512]{2,1,0:T(8,128)(2,1)S(1)}, u32[]{:S(2)}, u32[]{:S(2)}) collective-permute-start(bf16[8,48,512]{2,1,0:T(8,128)(2,1)S(1)} %collective-permute-done.34.refs_3_), channel_id=1, source_target_pairs={{0,1},{1,0},{2,3},{3,2},{4,5},{5,4},{6,7},{7,6},{8,9},{9,8},{10,11... | collective-permute-start | bytes 1179656 | tf_op jit(solution)/shard_map/params/ppermute | solution.py:23
  186.2 0.8 collective-permute-done.33.refs_2_
  187.1 5.3 %collective-permute-start.37 = (bf16[8,48,512]{2,1,0:T(8,128)(2,1)S(1)}, bf16[8,48,512]{2,1,0:T(8,128)(2,1)S(1)}, u32[]{:S(2)}, u32[]{:S(2)}) collective-permute-start(bf16[8,48,512]{2,1,0:T(8,128)(2,1)S(1)} %collective-permute-done.33.refs_2_), channel_id=1, source_target_pairs={{0,1},{1,0},{2,3},{3,2},{4,5},{5,4},{6,7},{7,6},{8,9},{9,8},{10,11... | collective-permute-start | bytes 1179656 | tf_op jit(solution)/shard_map/params/ppermute | solution.py:23
  192.4 1.3 collective-permute-done.37.refs_6_
  194.3 1.7 placed.3.refs_1_
  196.5 1.7 copy-done
  198.2 1.5 placed.4.refs_1_
  199.8 1.5 collective-permute-done.39.refs_0_
  201.2 1.5 placed.5
  (83 shorter events, 6.6 us)
Async XLA Ops:
  7.2 7.9 %copy-start.6 = (bf16[256,512]{1,0:T(8,128)(2,1)S(1)}, bf16[256,512]{1,0:T(8,128)(2,1)}, u32[]{:S(2)}) copy-start(bf16[256,512]{1,0:T(8,128)(2,1)} %param.5) | copy-start | bytes 786436
  7.2 81.2 %reduce-scatter.2.cloned.1.call-start = ((), (), s32[]{:S(2)}) async-start(), calls=%async_computation.3 | async-start | bytes 4718592 | tf_op jit(solution)/shard_map/reduce_b/reduce_scatter | solution.py:287
  11.8 12.4 %copy-start.13 = (bf16[256,2048]{1,0:T(8,128)(2,1)S(1)}, bf16[256,2048]{1,0:T(8,128)(2,1)}, u32[]{:S(2)}) copy-start(bf16[256,2048]{1,0:T(8,128)(2,1)} %get-tuple-element.34) | copy-start | bytes 3145732
  11.8 12.4 %collective-permute-start.15 = (bf16[256,2048]{1,0:T(8,128)(2,1)}, bf16[256,2048]{1,0:T(8,128)(2,1)S(1)}, u32[]{:S(2)}, u32[]{:S(2)}) collective-permute-start(bf16[256,2048]{1,0:T(8,128)(2,1)} %get-tuple-element.35), channel_id=1, source_target_pairs={{0,1},{1,0},{2,3},{3,2},{4,5},{5,4},{6,7},{7,6},{8,9},{9,8},{10,11... | collective-permute-start | bytes 3145736 | tf_op jit(solution)/shard_map/core_swap/ppermute | solution.py:23
  15.1 6.2 %collective-permute-start = (bf16[256,512]{1,0:T(8,128)(2,1)S(1)}, bf16[256,512]{1,0:T(8,128)(2,1)S(1)}, u32[]{:S(2)}, u32[]{:S(2)}) collective-permute-start(bf16[256,512]{1,0:T(8,128)(2,1)S(1)} %copy-done.6), channel_id=1, source_target_pairs={{0,1},{1,0},{2,3},{3,2},{4,5},{5,4},{6,7},{7,6},{8,9},{9,8},{10,11... | collective-permute-start | bytes 786440 | tf_op jit(solution)/shard_map/core_swap/ppermute | solution.py:23
  15.2 7.6 %collective-permute-start.1 = (bf16[256,512]{1,0:T(8,128)(2,1)S(1)}, bf16[256,512]{1,0:T(8,128)(2,1)}, u32[]{:S(2)}, u32[]{:S(2)}) collective-permute-start(bf16[256,512]{1,0:T(8,128)(2,1)S(1)} %copy-done.6), channel_id=1, source_target_pairs={{0,48},{16,0},{32,16},{48,32},{1,49},{17,1},{33,17},{49,33},{2,50}... | collective-permute-start | bytes 786440 | tf_op jit(solution)/shard_map/core_swap/ppermute | solution.py:23
  15.9 8.4 %collective-permute-start.2 = (bf16[256,512]{1,0:T(8,128)(2,1)S(1)}, bf16[256,512]{1,0:T(8,128)(2,1)S(1)}, u32[]{:S(2)}, u32[]{:S(2)}) collective-permute-start(bf16[256,512]{1,0:T(8,128)(2,1)S(1)} %copy-done.6), channel_id=1, source_target_pairs={{0,16},{16,32},{32,48},{48,0},{1,17},{17,33},{33,49},{49,1},{2,18}... | collective-permute-start | bytes 786440 | tf_op jit(solution)/shard_map/core_swap/ppermute | solution.py:23
  21.3 3.0 %copy-start.1 = (bf16[512,512]{1,0:T(8,128)(2,1)}, bf16[512,512]{1,0:T(8,128)(2,1)S(1)}, u32[]{:S(2)}) copy-start(bf16[512,512]{1,0:T(8,128)(2,1)S(1)} %pad_maximum_fusion) | copy-start | bytes 1572868
  24.3 3.3 %copy-start.14 = (bf16[256,512]{1,0:T(8,128)(2,1)}, bf16[256,512]{1,0:T(8,128)(2,1)S(1)}, u32[]{:S(2)}) copy-start(bf16[256,512]{1,0:T(8,128)(2,1)S(1)} %collective-permute-done.2) | copy-start | bytes 786436
  27.6 1.7 copy-start.3
  27.6 168.4 %all-gather.2.cloned.1.call-start = ((), (), s32[]{:S(2)}) async-start(), calls=%async_computation.4 | async-start | bytes 2949120 | tf_op jit(solution)/shard_map/params/all_gather | solution.py:243
  27.7 4.3 %collective-permute-start.3 = (bf16[256,2048]{1,0:T(8,128)(2,1)}, bf16[256,2048]{1,0:T(8,128)(2,1)}, u32[]{:S(2)}, u32[]{:S(2)}) collective-permute-start(bf16[256,2048]{1,0:T(8,128)(2,1)} %get-tuple-element.30), channel_id=1, source_target_pairs={{0,1},{1,0},{2,3},{3,2},{4,5},{5,4},{6,7},{7,6},{8,9},{9,8},{10,11... | collective-permute-start | bytes 3145736 | tf_op jit(solution)/shard_map/core_swap/ppermute | solution.py:23
  34.2 13.5 %collective-permute-start.4 = (bf16[512,512]{1,0:T(8,128)(2,1)}, bf16[512,512]{1,0:T(8,128)(2,1)}, u32[]{:S(2)}, u32[]{:S(2)}) collective-permute-start(bf16[512,512]{1,0:T(8,128)(2,1)} %get-tuple-element.52), channel_id=1, source_target_pairs={{0,48},{16,0},{32,16},{48,32},{1,49},{17,1},{33,17},{49,33},{2,50}... | collective-permute-start | bytes 1572872 | tf_op jit(solution)/shard_map/reduce_a/ppermute | solution.py:23
  34.4 8.8 %collective-permute-start.7 = (bf16[256,512]{1,0:T(8,128)(2,1)S(1)}, bf16[256,512]{1,0:T(8,128)(2,1)}, u32[]{:S(2)}, u32[]{:S(2)}) collective-permute-start(bf16[256,512]{1,0:T(8,128)(2,1)S(1)} %copy-done.6), channel_id=1, source_target_pairs={{0,32},{16,48},{32,0},{48,16},{1,33},{17,49},{33,1},{49,17},{2,34}... | collective-permute-start | bytes 786440 | tf_op jit(solution)/shard_map/core_swap/ppermute | solution.py:23
  35.5 10.3 %collective-permute-start.5 = (bf16[256,512]{1,0:T(8,128)(2,1)}, bf16[256,512]{1,0:T(8,128)(2,1)}, u32[]{:S(2)}, u32[]{:S(2)}) collective-permute-start(bf16[256,512]{1,0:T(8,128)(2,1)} %collective-permute-done.1), channel_id=1, source_target_pairs={{0,1},{1,0},{2,3},{3,2},{4,5},{5,4},{6,7},{7,6},{8,9},{9,8},{10,11... | collective-permute-start | bytes 786440 | tf_op jit(solution)/shard_map/core_swap/ppermute | solution.py:23
  36.5 20.1 %collective-permute-start.9 = (bf16[512,512]{1,0:T(8,128)(2,1)S(1)}, bf16[512,512]{1,0:T(8,128)(2,1)}, u32[]{:S(2)}, u32[]{:S(2)}) collective-permute-start(bf16[512,512]{1,0:T(8,128)(2,1)S(1)} %get-tuple-element.53), channel_id=1, source_target_pairs={{0,16},{16,32},{32,48},{48,0},{1,17},{17,33},{33,49},{49,1},{2,18}... | collective-permute-start | bytes 1572872 | tf_op jit(solution)/shard_map/reduce_a/ppermute | solution.py:23
  36.5 20.1 %copy-start.15 = (bf16[256,512]{1,0:T(8,128)(2,1)S(1)}, bf16[256,512]{1,0:T(8,128)(2,1)}, u32[]{:S(2)}) copy-start(bf16[256,512]{1,0:T(8,128)(2,1)} %copy-done.14) | copy-start | bytes 786436
  36.5 12.9 %collective-permute-start.10 = (bf16[256,512]{1,0:T(8,128)(2,1)}, bf16[256,512]{1,0:T(8,128)(2,1)S(1)}, u32[]{:S(2)}, u32[]{:S(2)}) collective-permute-start(bf16[256,512]{1,0:T(8,128)(2,1)} %copy-done.14), channel_id=1, source_target_pairs={{0,1},{1,0},{2,3},{3,2},{4,5},{5,4},{6,7},{7,6},{8,9},{9,8},{10,11... | collective-permute-start | bytes 786440 | tf_op jit(solution)/shard_map/core_swap/ppermute | solution.py:23
  43.2 14.8 %collective-permute-start.8 = (bf16[256,512]{1,0:T(8,128)(2,1)}, bf16[256,512]{1,0:T(8,128)(2,1)S(1)}, u32[]{:S(2)}, u32[]{:S(2)}) collective-permute-start(bf16[256,512]{1,0:T(8,128)(2,1)} %collective-permute-done.7), channel_id=1, source_target_pairs={{0,1},{1,0},{2,3},{3,2},{4,5},{5,4},{6,7},{7,6},{8,9},{9,8},{10,11... | collective-permute-start | bytes 786440 | tf_op jit(solution)/shard_map/core_swap/ppermute | solution.py:23
  45.9 19.7 %collective-permute-start.6 = (bf16[512,512]{1,0:T(8,128)(2,1)S(1)}, bf16[512,512]{1,0:T(8,128)(2,1)S(1)}, u32[]{:S(2)}, u32[]{:S(2)}) collective-permute-start(bf16[512,512]{1,0:T(8,128)(2,1)S(1)} %get-tuple-element.54), channel_id=1, source_target_pairs={{0,32},{16,48},{32,0},{48,16},{1,33},{17,49},{33,1},{49,17},{2,34}... | collective-permute-start | bytes 1572872 | tf_op jit(solution)/shard_map/reduce_a/ppermute | solution.py:23
  49.4 17.6 %copy-start.2 = (bf16[512,512]{1,0:T(8,128)(2,1)S(1)}, bf16[512,512]{1,0:T(8,128)(2,1)}, u32[]{:S(2)}) copy-start(bf16[512,512]{1,0:T(8,128)(2,1)} %copy-done.1) | copy-start | bytes 1572868
  67.5 9.4 %collective-permute-start.11 = (f32[32,512]{1,0:T(8,128)S(1)}, f32[32,512]{1,0:T(8,128)S(1)}, u32[]{:S(2)}, u32[]{:S(2)}) collective-permute-start(f32[32,512]{1,0:T(8,128)S(1)} %get-tuple-element.60), channel_id=1, source_target_pairs={{0,2},{2,4},{4,6},{6,8},{8,10},{10,12},{12,14},{14,0},{1,3},{3,5},... | collective-permute-start | bytes 196616 | tf_op jit(solution)/shard_map/reduce_a/ppermute | solution.py:23
  69.2 7.7 %collective-permute-start.13 = (f32[32,512]{1,0:T(8,128)S(1)}, f32[32,512]{1,0:T(8,128)S(1)}, u32[]{:S(2)}, u32[]{:S(2)}) collective-permute-start(f32[32,512]{1,0:T(8,128)S(1)} %get-tuple-element.61), channel_id=1, source_target_pairs={{0,14},{2,0},{4,2},{6,4},{8,6},{10,8},{12,10},{14,12},{1,15},{3,1}... | collective-permute-start | bytes 196616 | tf_op jit(solution)/shard_map/reduce_a/ppermute | solution.py:23
  77.0 9.0 %collective-permute-start.12 = (f32[64,512]{1,0:T(8,128)S(1)}, f32[64,512]{1,0:T(8,128)S(1)}, u32[]{:S(2)}, u32[]{:S(2)}) collective-permute-start(f32[64,512]{1,0:T(8,128)S(1)} %pad_maximum_fusion.2), channel_id=1, source_target_pairs={{0,2},{2,4},{4,6},{6,8},{8,10},{10,12},{12,14},{14,0},{1,3},{3,5},... | collective-permute-start | bytes 393224 | tf_op jit(solution)/shard_map/reduce_a/ppermute | solution.py:23
  77.1 8.9 %collective-permute-start.14 = (f32[64,512]{1,0:T(8,128)S(1)}, f32[64,512]{1,0:T(8,128)S(1)}, u32[]{:S(2)}, u32[]{:S(2)}) collective-permute-start(f32[64,512]{1,0:T(8,128)S(1)} %pad_maximum_fusion.3), channel_id=1, source_target_pairs={{0,14},{2,0},{4,2},{6,4},{8,6},{10,8},{12,10},{14,12},{1,15},{3,1}... | collective-permute-start | bytes 393224 | tf_op jit(solution)/shard_map/reduce_a/ppermute | solution.py:23
  89.4 7.3 %collective-permute-start.16 = (f32[64,512]{1,0:T(8,128)S(1)}, f32[64,512]{1,0:T(8,128)S(1)}, u32[]{:S(2)}, u32[]{:S(2)}) collective-permute-start(f32[64,512]{1,0:T(8,128)S(1)} %get-tuple-element.36), channel_id=1, source_target_pairs={{0,2},{2,4},{4,6},{6,8},{8,10},{10,12},{12,14},{14,0},{1,3},{3,5},... | collective-permute-start | bytes 393224 | tf_op jit(solution)/shard_map/reduce_a/ppermute | solution.py:23
  89.5 7.3 %collective-permute-start.18 = (f32[64,512]{1,0:T(8,128)S(1)}, f32[64,512]{1,0:T(8,128)S(1)}, u32[]{:S(2)}, u32[]{:S(2)}) collective-permute-start(f32[64,512]{1,0:T(8,128)S(1)} %get-tuple-element.37), channel_id=1, source_target_pairs={{0,14},{2,0},{4,2},{6,4},{8,6},{10,8},{12,10},{14,12},{1,15},{3,1}... | collective-permute-start | bytes 393224 | tf_op jit(solution)/shard_map/reduce_a/ppermute | solution.py:23
  92.2 7.4 %collective-permute-start.23 = (f32[64,512]{1,0:T(8,128)S(1)}, f32[64,512]{1,0:T(8,128)S(1)}, u32[]{:S(2)}, u32[]{:S(2)}) collective-permute-start(f32[64,512]{1,0:T(8,128)S(1)} %get-tuple-element.38), channel_id=1, source_target_pairs={{0,48},{16,0},{32,16},{48,32},{1,49},{17,1},{33,17},{49,33},{2,50}... | collective-permute-start | bytes 393224 | tf_op jit(solution)/shard_map/reduce_a/reduce_b2/ppermute | solution.py:23
  92.9 6.7 %collective-permute-start.24 = (f32[64,512]{1,0:T(8,128)S(1)}, f32[64,512]{1,0:T(8,128)S(1)}, u32[]{:S(2)}, u32[]{:S(2)}) collective-permute-start(f32[64,512]{1,0:T(8,128)S(1)} %get-tuple-element.39), channel_id=1, source_target_pairs={{0,16},{16,32},{32,48},{48,0},{1,17},{17,33},{33,49},{49,1},{2,18}... | collective-permute-start | bytes 393224 | tf_op jit(solution)/shard_map/reduce_a/reduce_b2/ppermute | solution.py:23
  93.6 7.7 %collective-permute-start.25 = (f32[64,512]{1,0:T(8,128)S(1)}, f32[64,512]{1,0:T(8,128)S(1)}, u32[]{:S(2)}, u32[]{:S(2)}) collective-permute-start(f32[64,512]{1,0:T(8,128)S(1)} %get-tuple-element.40), channel_id=1, source_target_pairs={{0,32},{16,48},{32,0},{48,16},{1,33},{17,49},{33,1},{49,17},{2,34}... | collective-permute-start | bytes 393224 | tf_op jit(solution)/shard_map/reduce_a/reduce_b2/ppermute | solution.py:23
  96.8 10.4 %collective-permute-start.17 = (f32[64,512]{1,0:T(8,128)S(1)}, f32[64,512]{1,0:T(8,128)S(1)}, u32[]{:S(2)}, u32[]{:S(2)}) collective-permute-start(f32[64,512]{1,0:T(8,128)S(1)} %get-tuple-element.55), channel_id=1, source_target_pairs={{0,2},{2,4},{4,6},{6,8},{8,10},{10,12},{12,14},{14,0},{1,3},{3,5},... | collective-permute-start | bytes 393224 | tf_op jit(solution)/shard_map/reduce_a/ppermute | solution.py:23
  96.9 10.3 %collective-permute-start.19 = (f32[64,512]{1,0:T(8,128)S(1)}, f32[64,512]{1,0:T(8,128)S(1)}, u32[]{:S(2)}, u32[]{:S(2)}) collective-permute-start(f32[64,512]{1,0:T(8,128)S(1)} %get-tuple-element.56), channel_id=1, source_target_pairs={{0,14},{2,0},{4,2},{6,4},{8,6},{10,8},{12,10},{14,12},{1,15},{3,1}... | collective-permute-start | bytes 393224 | tf_op jit(solution)/shard_map/reduce_a/ppermute | solution.py:23
  102.3 13.8 %copy-start.5 = (f32[64,512]{1,0:T(8,128)}, f32[64,512]{1,0:T(8,128)S(1)}, u32[]{:S(2)}) copy-start(f32[64,512]{1,0:T(8,128)S(1)} %bitcast_add_fusion.b0) | copy-start | bytes 393220
  102.3 6.2 %collective-permute-start.28 = (f32[64,512]{1,0:T(8,128)S(1)}, f32[64,512]{1,0:T(8,128)S(1)}, u32[]{:S(2)}, u32[]{:S(2)}) collective-permute-start(f32[64,512]{1,0:T(8,128)S(1)} %bitcast_add_fusion.b0), channel_id=1, source_target_pairs={{0,64},{64,128},{128,192},{192,0},{1,65},{65,129},{129,193},{193,1... | collective-permute-start | bytes 393224 | tf_op jit(solution)/shard_map/members/ppermute | solution.py:23
  103.6 6.5 %collective-permute-start.27 = (f32[64,512]{1,0:T(8,128)S(1)}, f32[64,512]{1,0:T(8,128)S(1)}, u32[]{:S(2)}, u32[]{:S(2)}) collective-permute-start(f32[64,512]{1,0:T(8,128)S(1)} %bitcast_add_fusion.b0), channel_id=1, source_target_pairs={{0,128},{64,192},{128,0},{192,64},{1,129},{65,193},{129,1},{193,65... | collective-permute-start | bytes 393224 | tf_op jit(solution)/shard_map/members/ppermute | solution.py:23
  106.0 4.1 %collective-permute-start.26 = (f32[64,512]{1,0:T(8,128)S(1)}, f32[64,512]{1,0:T(8,128)S(1)}, u32[]{:S(2)}, u32[]{:S(2)}) collective-permute-start(f32[64,512]{1,0:T(8,128)S(1)} %bitcast_add_fusion.b0), channel_id=1, source_target_pairs={{0,192},{64,0},{128,64},{192,128},{1,193},{65,1},{129,65},{193,129... | collective-permute-start | bytes 393224 | tf_op jit(solution)/shard_map/members/ppermute | solution.py:23
  107.2 8.9 %copy-start.4 = (f32[64,512]{1,0:T(8,128)}, f32[64,512]{1,0:T(8,128)S(1)}, u32[]{:S(2)}) copy-start(f32[64,512]{1,0:T(8,128)S(1)} %fusion.19.a0) | copy-start | bytes 393220
  107.2 6.1 %collective-permute-start.22 = (f32[64,512]{1,0:T(8,128)S(1)}, f32[64,512]{1,0:T(8,128)S(1)}, u32[]{:S(2)}, u32[]{:S(2)}) collective-permute-start(f32[64,512]{1,0:T(8,128)S(1)} %fusion.19.a0), channel_id=1, source_target_pairs={{0,64},{64,128},{128,192},{192,0},{1,65},{65,129},{129,193},{193,1... | collective-permute-start | bytes 393224 | tf_op jit(solution)/shard_map/members/ppermute | solution.py:23
  107.6 7.4 %collective-permute-start.21 = (f32[64,512]{1,0:T(8,128)S(1)}, f32[64,512]{1,0:T(8,128)S(1)}, u32[]{:S(2)}, u32[]{:S(2)}) collective-permute-start(f32[64,512]{1,0:T(8,128)S(1)} %fusion.19.a0), channel_id=1, source_target_pairs={{0,128},{64,192},{128,0},{192,64},{1,129},{65,193},{129,1},{193,65... | collective-permute-start | bytes 393224 | tf_op jit(solution)/shard_map/members/ppermute | solution.py:23
  108.5 7.6 %copy-start.7 = (f32[64,512]{1,0:T(8,128)}, f32[64,512]{1,0:T(8,128)S(1)}, u32[]{:S(2)}) copy-start(f32[64,512]{1,0:T(8,128)S(1)} %collective-permute-done.28.b3) | copy-start | bytes 393220
  108.5 7.6 %collective-permute-start.20 = (f32[64,512]{1,0:T(8,128)S(1)}, f32[64,512]{1,0:T(8,128)S(1)}, u32[]{:S(2)}, u32[]{:S(2)}) collective-permute-start(f32[64,512]{1,0:T(8,128)S(1)} %fusion.19.a0), channel_id=1, source_target_pairs={{0,192},{64,0},{128,64},{192,128},{1,193},{65,1},{129,65},{193,129... | collective-permute-start | bytes 393224 | tf_op jit(solution)/shard_map/members/ppermute | solution.py:23
  110.1 6.0 %copy-start.8 = (f32[64,512]{1,0:T(8,128)}, f32[64,512]{1,0:T(8,128)S(1)}, u32[]{:S(2)}) copy-start(f32[64,512]{1,0:T(8,128)S(1)} %collective-permute-done.27.b2) | copy-start | bytes 393220
  110.1 6.0 %copy-start.9 = (f32[64,512]{1,0:T(8,128)}, f32[64,512]{1,0:T(8,128)S(1)}, u32[]{:S(2)}) copy-start(f32[64,512]{1,0:T(8,128)S(1)} %collective-permute-done.26.b1) | copy-start | bytes 393220
  113.3 2.8 %copy-start.10 = (f32[64,512]{1,0:T(8,128)}, f32[64,512]{1,0:T(8,128)S(1)}, u32[]{:S(2)}) copy-start(f32[64,512]{1,0:T(8,128)S(1)} %collective-permute-done.22.a3) | copy-start | bytes 393220
  115.0 1.1 copy-start.11
  116.1 0.7 copy-start.12
  143.1 5.6 %collective-permute-start.31 = (bf16[80,512]{1,0:T(8,128)(2,1)}, bf16[80,512]{1,0:T(8,128)(2,1)S(1)}, u32[]{:S(2)}, u32[]{:S(2)}) collective-permute-start(bf16[80,512]{1,0:T(8,128)(2,1)} %get-tuple-element.46), channel_id=1, source_target_pairs={{0,16},{16,32},{32,48},{48,0},{1,17},{17,33},{33,49},{49,1},{2,18}... | collective-permute-start | bytes 245768 | tf_op jit(solution)/shard_map/params/ppermute | solution.py:23
  143.4 6.2 %collective-permute-start.30 = (bf16[80,512]{1,0:T(8,128)(2,1)}, bf16[80,512]{1,0:T(8,128)(2,1)S(1)}, u32[]{:S(2)}, u32[]{:S(2)}) collective-permute-start(bf16[80,512]{1,0:T(8,128)(2,1)} %get-tuple-element.46), channel_id=1, source_target_pairs={{0,32},{16,48},{32,0},{48,16},{1,33},{17,49},{33,1},{49,17},{2,34}... | collective-permute-start | bytes 245768 | tf_op jit(solution)/shard_map/params/ppermute | solution.py:23
  145.0 5.1 %collective-permute-start.29 = (bf16[80,512]{1,0:T(8,128)(2,1)}, bf16[80,512]{1,0:T(8,128)(2,1)S(1)}, u32[]{:S(2)}, u32[]{:S(2)}) collective-permute-start(bf16[80,512]{1,0:T(8,128)(2,1)} %get-tuple-element.46), channel_id=1, source_target_pairs={{0,48},{16,0},{32,16},{48,32},{1,49},{17,1},{33,17},{49,33},{2,50}... | collective-permute-start | bytes 245768 | tf_op jit(solution)/shard_map/params/ppermute | solution.py:23
  168.4 10.1 %collective-permute-start.34 = (bf16[8,48,512]{2,1,0:T(8,128)(2,1)S(1)}, bf16[8,48,512]{2,1,0:T(8,128)(2,1)S(1)}, u32[]{:S(2)}, u32[]{:S(2)}) collective-permute-start(bf16[8,48,512]{2,1,0:T(8,128)(2,1)S(1)} %all_to_all.11.refs_0_), channel_id=1, source_target_pairs={{0,16},{16,32},{32,48},{48,0},{1,17},{17,33},{33,49},{49,1},{2,18}... | collective-permute-start | bytes 1179656 | tf_op jit(solution)/shard_map/params/ppermute | solution.py:23
  170.3 16.8 %collective-permute-start.33 = (bf16[8,48,512]{2,1,0:T(8,128)(2,1)S(1)}, bf16[8,48,512]{2,1,0:T(8,128)(2,1)S(1)}, u32[]{:S(2)}, u32[]{:S(2)}) collective-permute-start(bf16[8,48,512]{2,1,0:T(8,128)(2,1)S(1)} %all_to_all.11.refs_0_), channel_id=1, source_target_pairs={{0,32},{16,48},{32,0},{48,16},{1,33},{17,49},{33,1},{49,17},{2,34}... | collective-permute-start | bytes 1179656 | tf_op jit(solution)/shard_map/params/ppermute | solution.py:23
  173.8 18.5 %collective-permute-start.32 = (bf16[8,48,512]{2,1,0:T(8,128)(2,1)S(1)}, bf16[8,48,512]{2,1,0:T(8,128)(2,1)S(1)}, u32[]{:S(2)}, u32[]{:S(2)}) collective-permute-start(bf16[8,48,512]{2,1,0:T(8,128)(2,1)S(1)} %all_to_all.11.refs_0_), channel_id=1, source_target_pairs={{0,48},{16,0},{32,16},{48,32},{1,49},{17,1},{33,17},{49,33},{2,50}... | collective-permute-start | bytes 1179656 | tf_op jit(solution)/shard_map/params/ppermute | solution.py:23
  173.9 18.5 %collective-permute-start.35 = (bf16[8,48,512]{2,1,0:T(8,128)(2,1)S(1)}, bf16[8,48,512]{2,1,0:T(8,128)(2,1)S(1)}, u32[]{:S(2)}, u32[]{:S(2)}) collective-permute-start(bf16[8,48,512]{2,1,0:T(8,128)(2,1)S(1)} %all_to_all.11.refs_0_), channel_id=1, source_target_pairs={{0,1},{1,0},{2,3},{3,2},{4,5},{5,4},{6,7},{7,6},{8,9},{9,8},{10,11... | collective-permute-start | bytes 1179656 | tf_op jit(solution)/shard_map/params/ppermute | solution.py:23
  178.5 13.9 %collective-permute-start.38 = (bf16[8,48,512]{2,1,0:T(8,128)(2,1)S(1)}, bf16[8,48,512]{2,1,0:T(8,128)(2,1)S(1)}, u32[]{:S(2)}, u32[]{:S(2)}) collective-permute-start(bf16[8,48,512]{2,1,0:T(8,128)(2,1)S(1)} %collective-permute-done.34.refs_3_), channel_id=1, source_target_pairs={{0,1},{1,0},{2,3},{3,2},{4,5},{5,4},{6,7},{7,6},{8,9},{9,8},{10,11... | collective-permute-start | bytes 1179656 | tf_op jit(solution)/shard_map/params/ppermute | solution.py:23
  187.1 6.6 %collective-permute-start.37 = (bf16[8,48,512]{2,1,0:T(8,128)(2,1)S(1)}, bf16[8,48,512]{2,1,0:T(8,128)(2,1)S(1)}, u32[]{:S(2)}, u32[]{:S(2)}) collective-permute-start(bf16[8,48,512]{2,1,0:T(8,128)(2,1)S(1)} %collective-permute-done.33.refs_2_), channel_id=1, source_target_pairs={{0,1},{1,0},{2,3},{3,2},{4,5},{5,4},{6,7},{7,6},{8,9},{9,8},{10,11... | collective-permute-start | bytes 1179656 | tf_op jit(solution)/shard_map/params/ppermute | solution.py:23
  192.3 1.9 collective-permute-start.36
  196.0 5.2 %collective-permute-start.39 = (bf16[8,4,80,512]{3,2,1,0:T(8,128)(2,1)}, bf16[8,4,80,512]{3,2,1,0:T(8,128)(2,1)S(1)}, u32[]{:S(2)}, u32[]{:S(2)}) collective-permute-start(bf16[8,4,80,512]{3,2,1,0:T(8,128)(2,1)} %bitcast.45), channel_id=1, source_target_pairs={{0,1},{1,0},{2,3},{3,2},{4,5},{5,4},{6,7},{7,6},{8,9},{9,8},{10,11... | collective-permute-start | bytes 7864328 | tf_op jit(solution)/shard_map/params/ppermute | solution.py:23
  196.5 1.7 copy-start
Sparse Core Ops, SparseCore 0:
  27.7 60.5 reduce-scatter.1
  151.9 40.4 all-gather.1

commit v4 on v3

--- a/solution.py
+++ b/solution.py
@@ -52,12 +52,12 @@
     return chunk(0) + up + down
 
 
-def by_place(whole, axis):
+def by_place(whole, axis, flip):
     size = lax.axis_size(axis)
     place = lax.axis_index(axis)
 
     def chunk(step):
-        return lax.dynamic_index_in_dim(whole, (place + step + size) % size, 0, keepdims=False)
+        return lax.dynamic_index_in_dim(whole, ((place + step + size) % size) ^ flip, 0, keepdims=False)
 
     return chunk
 
@@ -70,46 +70,42 @@
     return [pl.BlockSpec(memory_space=pltpu.VMEM)] * count
 
 
-def split_kernel(block, colour, grads_ref, kept_ref, given_ref):
-    low = lax.axis_index("core") == 0
+def split_kernel(block, colour, *refs):
+    *strips, kept_ref, given_ref = refs
+    core = lax.axis_index("core")
     half = block // 2
-    lane = lax.broadcasted_iota(jnp.int32, (grads_ref.shape[0], block), 1)
-
-    def swapped_halves(value):
-        return pltpu.roll(value.astype(jnp.float32), half, 1).astype(value.dtype)
-
-    def pair(left, right):
-        if colour == "A":
-            return jnp.where(lane < half, left, swapped_halves(right))
-        return jnp.where(lane < half, swapped_halves(left), right)
-
-    def block_at(x, z, core):
-        return grads_ref[:, pl.ds((x * 16 + z * 2 + core) * block, block)]
-
+    first_lanes = lax.broadcasted_iota(jnp.int32, (kept_ref.shape[0], block), 1) < half
     if colour == "A":
-        order = [(x, z) for x in range(4) for z in range(8)]
+        order = [(x, slot ^ (x & 1)) for x in range(4) for slot in range(8)]
     else:
-        order = [(x, z) for z in range(8) for x in range(4)]
-    for index in range(0, len(order), 2):
-        sides = [pair(*(block_at(*place, core) for place in order[index : index + 2])) for core in range(2)]
-        where = pl.ds(index * half, block)
-        kept_ref[:, where] = jnp.where(low, sides[0], sides[1])
-        given_ref[:, where] = jnp.where(low, sides[1], sides[0])
+        order = [(slot ^ (z & 1) ^ 1, z) for z in range(8) for slot in range(4)]
+    for out_ref, side in ((given_ref, 1 - core), (kept_ref, core)):
+        for index in range(0, len(order), 2):
+            left, right = (
+                strips[x * 2 + z // 4][
+                    :, pl.ds(pl.multiple_of((z % 4 * 2 + side) * block, block), block)
+                ]
+                for x, z in order[index : index + 2]
+            )
+            out_ref[:, pl.ds(index * half, block)] = jnp.where(first_lanes, left, right)
 
 
 def split_columns(grads, block, colour):
     tokens, features = grads.shape
-    step = tokens // 4
+    step = tokens // 2
     part = jax.ShapeDtypeStruct((tokens, features // 4), grads.dtype)
     part_spec = pl.BlockSpec((step, features // 4), lambda i: (i, 0))
     return pl.pallas_call(
         functools.partial(split_kernel, block, colour),
-        grid=(4,),
-        in_specs=[pl.BlockSpec((step, features), lambda i: (i, 0))],
+        grid=(2,),
+        in_specs=[
+            pl.BlockSpec((step, features // 8), functools.partial(lambda strip, i: (i, strip), strip))
+            for strip in range(8)
+        ],
         out_specs=[part_spec, part_spec],
         out_shape=[part, part],
         name="split_columns",
-    )(grads)
+    )(*[grads] * 8)
 
 
 PAIRS = [(i, j) for i in range(4) for j in range(i, 4)]
@@ -118,10 +114,11 @@
 def gram_kernel(a0, a1, a2, a3, b0, b1, b2, b3, members_ref, rows_ref):
     place = lax.axis_index("rep")
     half = a0.shape[0]
+    odd = lax.rem(lax.axis_index("x") + lax.axis_index("z"), 2)
     for step, (left, right) in enumerate(zip((a0, a1, a2, a3), (b0, b1, b2, b3))):
         member = lax.rem(place + step, 4)
-        members_ref[member, :half] = left[...]
-        members_ref[member, half:] = right[...]
+        members_ref[member, pl.ds(pl.multiple_of(odd * half, half), half)] = left[...]
+        members_ref[member, pl.ds(pl.multiple_of((1 - odd) * half, half), half)] = right[...]
     lane = lax.broadcasted_iota(jnp.int32, (1, 128), 1)
     row = jnp.zeros((1, 128), jnp.float32)
     for index, (i, j) in enumerate(PAIRS):
@@ -180,14 +177,16 @@
     new_master_ref[...] = new_master
     half = params_a_ref.shape[0]
     params_a_ref[...] = new_master[:half].astype(jnp.bfloat16)
-    params_b_ref[...] = new_master[half:].astype(jnp.bfloat16)
+    params_b_ref[...] = jnp.broadcast_to(
+        new_master[half:].astype(jnp.bfloat16)[None], params_b_ref.shape
+    )
 
 
 def updated(everyone, members, master, first, second):
     rows, width = master.shape
     whole = jax.ShapeDtypeStruct((rows, width), jnp.float32)
     part_a = jax.ShapeDtypeStruct((ROWS_A, width), jnp.bfloat16)
-    part_b = jax.ShapeDtypeStruct((rows - ROWS_A, width), jnp.bfloat16)
+    part_b = jax.ShapeDtypeStruct((8, rows - ROWS_A, width), jnp.bfloat16)
     return pl.pallas_call(
         update_kernel,
         in_specs=in_vmem(5),
@@ -206,7 +205,9 @@
         if colour == 0:
             for up in range(4):
                 x = lax.rem(x_place + up, 4)
-                copies.append((piece.at[:, up], out.at[x, :, owner, pl.ds(0, size_a)]))
+                for owner in range(2):
+                    source = piece.at[:, owner, up]
+                    copies.append((source, out.at[x, :, owner, pl.ds(0, size_a)]))
         else:
             x = lax.rem(x_place + step, 4)
             rows = piece.shape[1]
@@ -228,29 +229,28 @@
         in_specs=in_vmem(len(pieces)) + ([] if first else [pl.BlockSpec(memory_space=pl.ANY)]),
         out_specs=pl.BlockSpec(memory_space=pl.ANY),
         out_shape=jax.ShapeDtypeStruct(shape, jnp.bfloat16),
-        scratch_shapes=[pltpu.SemaphoreType.DMA((len(pieces) + 3,))],
+        scratch_shapes=[pltpu.SemaphoreType.DMA((8,))],
         input_output_aliases={} if first else {len(pieces): 0},
         compiler_params=pltpu.CompilerParams(vmem_limit_bytes=32 * 1024 * 1024),
         name="placed",
     )(*pieces, *([] if first else [out]))
 
 
-def gathered(params_a, params_b):
+def gathered(params_a, column_rows):
     rows_a, width = params_a.shape
-    rows_b = params_b.shape[0]
+    rows_b = column_rows.shape[1]
     line = jnp.concatenate(neighbours(params_a, "x"), axis=0)
-    line, params_b = lax.optimization_barrier((line, params_b))
-    own_a = lax.all_gather(line, "z", axis=0, tiled=True).reshape(8, 4, rows_a, width)
-    column = lax.all_to_all(jnp.broadcast_to(params_b[None], (8, rows_b, width)), "z", 0, 0)
+    line, column_rows = lax.optimization_barrier((line, column_rows))
+    own_a = lax.all_gather(line, ("z", "core"), axis=0, tiled=True)
+    own_a = own_a.reshape(8, 2, 4, rows_a, width)
+    column = lax.all_to_all(column_rows, "z", 0, 0)
     own_b = neighbours(column, "x")
     other_b = [shifted(piece, "core", 1) for piece in own_b]
     order = [(1, side, step) for side in range(2) for step in range(4)]
     shape = (4, 8, 2, rows_a + rows_b, width)
     out = placed(None, [*own_b, *other_b], order, shape, rows_a)
     own_a, out = lax.optimization_barrier((own_a, out))
-    other_a = shifted(own_a, "core", 1)
     out = placed(out, [own_a], [(0, 0, 0)], shape, rows_a)
-    out = placed(out, [other_a], [(0, 1, 0)], shape, rows_a)
     return out.reshape(-1, width)
 
 
@@ -283,9 +283,10 @@
         grads_a = pair_up_parts(kept_a, given_a)
         line_acts = [own_acts] + [pair_up(part) for part in near_acts[1:]]
     with jax.named_scope("reduce_b"):
-        sums_b = product(grads_b, line_acts[0])
-        sums_b = lax.psum_scatter(sums_b, "z", scatter_dimension=0, tiled=True)
-        chunk_b = by_place(sums_b.reshape(4, half, width), "x")
+        sums_b = lax.psum_scatter(
+            product(grads_b, own_acts), "z", scatter_dimension=0, tiled=True
+        )
+        chunk_b = by_place(sums_b.reshape(4, half, width), "x", (lax.axis_index("z") & 1) ^ 1)
         chunks_b = [chunk_b(step) for step in range(4)]
     with jax.named_scope("reduce_a"):
         strip = 8 * half
@@ -313,7 +314,7 @@
             return send_up, send_down
 
         gates = {2: start_b}
-        grad_a = ring_reduce(by_place(sums_a.reshape(8, half, width), "z"), "z", gates)
+        grad_a = ring_reduce(by_place(sums_a.reshape(8, half, width), "z", x_place & 1), "z", gates)
     with jax.named_scope("members"):
         members, row = gram_rows(neighbours(grad_a, "rep"), neighbours(exchanged_b.pop(), "rep"))
     with jax.named_scope("gram"):

time: 210 us -> 208 us (level)
  Pallas kernels: 19.3 us -> 16.9 us
    pallas_call x3 -> x2, Pallas kernels: 4.78 us -> 4.13 us  [placed(): pl.pallas_call(functools.partial(place_kernel, size_a, order), in_specs=i...]
    ppermute x40 -> x39, waiting for transfers between devices: 52.8 us -> 52.5 us  [shifted(): lax.ppermute(value, axis, [(i, (i + step) % size) for i in range(size)])]
    ppermute x40 -> x39, starting transfers between devices: 66 us -> 65.9 us  [shifted(): lax.ppermute(value, axis, [(i, (i + step) % size) for i in range(size)])]
  transfers between devices with their start and end apart: 42 -> 41, of which waited for: 21 -> 20; matrix products, arithmetic and copies ran while one was open for 4% -> 4% of each run, Pallas kernels for 4% -> 3%
where the time goes in v4:
time: 208 us
  starting transfers between devices  65.9 us (32%)
  waiting for transfers between devices  54.6 us (26%)
  blocking collectives  37.9 us (18%)
  Pallas kernels  16.9 us (8%)
  between operations  14.4 us (7%)
  matrix products  8.4 us (4%)
  local copies, waits for them, and re-layouts  6.63 us (3%)
  other arithmetic  2.77 us (1%)
    ppermute x39, starting transfers between devices, shifted(): lax.ppermute(value, axis, [(i, (i + step) % size) for i in range(size)])  65.9 us
    ppermute x39, waiting for transfers between devices, shifted(): lax.ppermute(value, axis, [(i, (i + step) % size) for i in range(size)])  52.5 us
    all_to_all x1, blocking collectives, local(): everyone = lax.all_to_all(row, GROUP, 0, 0)  21 us
    all_to_all x1, blocking collectives, gathered(): column = lax.all_to_all(column_rows, 'z', 0, 0)  16.9 us
    dot_general x5, matrix products, product(): lax.dot_general(grad_columns, act_rows, contract_first, preferred_element...  8.4 us
    pallas_call x2, Pallas kernels, split_columns(): pl.pallas_call(functools.partial(split_kernel, block, colour), grid=(2,),...  7.4 us
  transfers between devices with their start and end apart: 41, of which 20 were waited for; matrix products, arithmetic and copies ran while one was open for 4% of the time, Pallas kernels for 3%

profile of v4, /device:TPU:1, one launch (start us, length us, event | category | flops | bytes accessed | tf_op | source)
XLA Modules:
  0.0 207.5 jit_solution(6095273287465013504)
XLA Ops:
  7.2 3.7 %split_columns.3 = (bf16[256,2048]{1,0:T(8,128)(2,1)}, bf16[256,2048]{1,0:T(8,128)(2,1)}) custom-call(bf16[256,8192]{1,0:T(8,128)(2,1)} %refs_7_.3, bf16[256,8192]{1,0:T(8,128)(2,1)} %refs_7_.3, bf16[256,8192]{1,0:T(8,128)(2,1)} %refs_7_.3, bf16[256,8192]{1,0:T(8,128)(2,1)} %refs_7_.3, bf16[256,8192]{1,0:T(8,128)(2,1)} %refs_7_.3, ...), custom_call_target="tpu_custom_call" | custom-call | tf_op jit(solution)/shard_map/core_swap/split_columns/pallas_call | solution.py:98
  10.9 3.3 %collective-permute-start.15 = (bf16[256,2048]{1,0:T(8,128)(2,1)}, bf16[256,2048]{1,0:T(8,128)(2,1)S(1)}, u32[]{:S(2)}, u32[]{:S(2)}) collective-permute-start(bf16[256,2048]{1,0:T(8,128)(2,1)} %get-tuple-element.35), channel_id=1, source_target_pairs={{0,1},{1,0},{2,3},{3,2},{4,5},{5,4},{6,7},{7,6},{8,9},{9,8},{10,11... | collective-permute-start | bytes 3145736 | tf_op jit(solution)/shard_map/core_swap/ppermute | solution.py:23
  14.4 0.7 collective-permute-start.1
  15.1 0.7 collective-permute-start.2
  15.8 3.7 %split_columns.2 = (bf16[256,2048]{1,0:T(8,128)(2,1)}, bf16[256,2048]{1,0:T(8,128)(2,1)}) custom-call(bf16[256,8192]{1,0:T(8,128)(2,1)} %refs_7_.3, bf16[256,8192]{1,0:T(8,128)(2,1)} %refs_7_.3, bf16[256,8192]{1,0:T(8,128)(2,1)} %refs_7_.3, bf16[256,8192]{1,0:T(8,128)(2,1)} %refs_7_.3, bf16[256,8192]{1,0:T(8,128)(2,1)} %refs_7_.3, ...), custom_call_target="tpu_custom_call" | custom-call | tf_op jit(solution)/shard_map/core_swap/split_columns/pallas_call | solution.py:98
  19.6 2.4 %collective-permute-done.1 = bf16[256,512]{1,0:T(8,128)(2,1)} collective-permute-done((bf16[256,512]{1,0:T(8,128)(2,1)S(1)}, bf16[256,512]{1,0:T(8,128)(2,1)}, u32[]{:S(2)}, u32[]{:S(2)}) %collective-permute-start.1) | collective-permute-done | bytes 262176 | tf_op jit(solution)/shard_map/core_swap/ppermute | solution.py:23
  22.0 1.5 collective-permute-done.2
  23.5 3.3 %fusion = f32[2048,512]{1,0:T(8,128)} fusion(bf16[512,512]{1,0:T(8,128)(2,1)S(1)} %pad_maximum_fusion, bf16[256,2048]{1,0:T(8,128)(2,1)S(1)} %collective-permute-done.15, bf16[256,2048]{1,0:T(8,128)(2,1)S(1)} %copy-done.13), kind=kOutput, calls=%fused_computation | convolution fusion | flops 1077936128 | bytes 6815744 | tf_op jit(solution)/shard_map/reduce_b/dot_general | solution.py:264
  26.9 1.6 collective-permute-start.3
  28.6 2.5 %collective-permute-done.3 = bf16[256,2048]{1,0:T(8,128)(2,1)} collective-permute-done((bf16[256,2048]{1,0:T(8,128)(2,1)}, bf16[256,2048]{1,0:T(8,128)(2,1)}, u32[]{:S(2)}, u32[]{:S(2)}) %collective-permute-start.3) | collective-permute-done | bytes 1048608 | tf_op jit(solution)/shard_map/core_swap/ppermute | solution.py:23
  31.2 1.3 constant_dynamic-update-slice_fusion
  32.5 1.0 constant_dynamic-slice_fusion.2
  33.5 1.2 collective-permute-start.7
  34.7 0.9 collective-permute-start.5
  35.8 6.6 %collective-permute-done.7 = bf16[256,512]{1,0:T(8,128)(2,1)} collective-permute-done((bf16[256,512]{1,0:T(8,128)(2,1)S(1)}, bf16[256,512]{1,0:T(8,128)(2,1)}, u32[]{:S(2)}, u32[]{:S(2)}) %collective-permute-start.7) | collective-permute-done | bytes 262176 | tf_op jit(solution)/shard_map/core_swap/ppermute | solution.py:23
  42.4 2.6 %collective-permute-start.8 = (bf16[256,512]{1,0:T(8,128)(2,1)}, bf16[256,512]{1,0:T(8,128)(2,1)S(1)}, u32[]{:S(2)}, u32[]{:S(2)}) collective-permute-start(bf16[256,512]{1,0:T(8,128)(2,1)} %collective-permute-done.7), channel_id=1, source_target_pairs={{0,1},{1,0},{2,3},{3,2},{4,5},{5,4},{6,7},{7,6},{8,9},{9,8},{10,11... | collective-permute-start | bytes 786440 | tf_op jit(solution)/shard_map/core_swap/ppermute | solution.py:23
  45.0 1.2 collective-permute-start.6
  46.2 0.6 collective-permute-done.4
  46.9 1.7 fusion.6
  48.6 7.1 %collective-permute-done.9 = bf16[512,512]{1,0:T(8,128)(2,1)} collective-permute-done((bf16[512,512]{1,0:T(8,128)(2,1)S(1)}, bf16[512,512]{1,0:T(8,128)(2,1)}, u32[]{:S(2)}, u32[]{:S(2)}) %collective-permute-start.9) | collective-permute-done | bytes 524320 | tf_op jit(solution)/shard_map/reduce_a/ppermute | solution.py:23
  55.7 1.5 fusion.14
  57.2 7.5 %collective-permute-done.6 = bf16[512,512]{1,0:T(8,128)(2,1)S(1)} collective-permute-done((bf16[512,512]{1,0:T(8,128)(2,1)S(1)}, bf16[512,512]{1,0:T(8,128)(2,1)S(1)}, u32[]{:S(2)}, u32[]{:S(2)}) %collective-permute-start.6) | collective-permute-done | bytes 524320 | tf_op jit(solution)/shard_map/reduce_a/ppermute | solution.py:23
  64.7 1.4 fusion.10
  66.7 1.9 collective-permute-start.11
  68.6 4.0 %collective-permute-start.13 = (f32[32,512]{1,0:T(8,128)S(1)}, f32[32,512]{1,0:T(8,128)S(1)}, u32[]{:S(2)}, u32[]{:S(2)}) collective-permute-start(f32[32,512]{1,0:T(8,128)S(1)} %get-tuple-element.61), channel_id=1, source_target_pairs={{0,14},{2,0},{4,2},{6,4},{8,6},{10,8},{12,10},{14,12},{1,15},{3,1}... | collective-permute-start | bytes 196616 | tf_op jit(solution)/shard_map/reduce_a/ppermute | solution.py:23
  72.6 3.7 %collective-permute-done.11 = f32[32,512]{1,0:T(8,128)S(1)} collective-permute-done((f32[32,512]{1,0:T(8,128)S(1)}, f32[32,512]{1,0:T(8,128)S(1)}, u32[]{:S(2)}, u32[]{:S(2)}) %collective-permute-start.11) | collective-permute-done | bytes 65568 | tf_op jit(solution)/shard_map/reduce_a/ppermute | solution.py:23
  76.5 2.7 %collective-permute-start.14 = (f32[64,512]{1,0:T(8,128)S(1)}, f32[64,512]{1,0:T(8,128)S(1)}, u32[]{:S(2)}, u32[]{:S(2)}) collective-permute-start(f32[64,512]{1,0:T(8,128)S(1)} %pad_maximum_fusion.3), channel_id=1, source_target_pairs={{0,14},{2,0},{4,2},{6,4},{8,6},{10,8},{12,10},{14,12},{1,15},{3,1}... | collective-permute-start | bytes 393224 | tf_op jit(solution)/shard_map/reduce_a/ppermute | solution.py:23
  79.2 6.2 %collective-permute-done.12 = f32[64,512]{1,0:T(8,128)S(1)} collective-permute-done((f32[64,512]{1,0:T(8,128)S(1)}, f32[64,512]{1,0:T(8,128)S(1)}, u32[]{:S(2)}, u32[]{:S(2)}) %collective-permute-start.12) | collective-permute-done | bytes 131104 | tf_op jit(solution)/shard_map/reduce_a/ppermute | solution.py:23
  85.4 2.0 reduce-scatter.2.cloned.1.call-done
  87.5 1.1 dynamic-slice_bitcast_fusion
  88.6 2.7 %collective-permute-start.18 = (f32[64,512]{1,0:T(8,128)S(1)}, f32[64,512]{1,0:T(8,128)S(1)}, u32[]{:S(2)}, u32[]{:S(2)}) collective-permute-start(f32[64,512]{1,0:T(8,128)S(1)} %get-tuple-element.37), channel_id=1, source_target_pairs={{0,14},{2,0},{4,2},{6,4},{8,6},{10,8},{12,10},{14,12},{1,15},{3,1}... | collective-permute-start | bytes 393224 | tf_op jit(solution)/shard_map/reduce_a/ppermute | solution.py:23
  91.3 0.9 collective-permute-start.23
  92.8 3.2 %collective-permute-start.25 = (f32[64,512]{1,0:T(8,128)S(1)}, f32[64,512]{1,0:T(8,128)S(1)}, u32[]{:S(2)}, u32[]{:S(2)}) collective-permute-start(f32[64,512]{1,0:T(8,128)S(1)} %get-tuple-element.40), channel_id=1, source_target_pairs={{0,32},{16,48},{32,0},{48,16},{1,33},{17,49},{33,1},{49,17},{2,34}... | collective-permute-start | bytes 393224 | tf_op jit(solution)/shard_map/reduce_a/reduce_b2/ppermute | solution.py:23
  96.1 2.7 %collective-permute-start.19 = (f32[64,512]{1,0:T(8,128)S(1)}, f32[64,512]{1,0:T(8,128)S(1)}, u32[]{:S(2)}, u32[]{:S(2)}) collective-permute-start(f32[64,512]{1,0:T(8,128)S(1)} %get-tuple-element.56), channel_id=1, source_target_pairs={{0,14},{2,0},{4,2},{6,4},{8,6},{10,8},{12,10},{14,12},{1,15},{3,1}... | collective-permute-start | bytes 393224 | tf_op jit(solution)/shard_map/reduce_a/ppermute | solution.py:23
  98.7 1.8 collective-permute-done.25
  100.5 0.9 bitcast_add_fusion.b0
  101.5 1.3 collective-permute-start.28
  102.7 2.4 %collective-permute-start.27 = (f32[64,512]{1,0:T(8,128)S(1)}, f32[64,512]{1,0:T(8,128)S(1)}, u32[]{:S(2)}, u32[]{:S(2)}) collective-permute-start(f32[64,512]{1,0:T(8,128)S(1)} %bitcast_add_fusion.b0), channel_id=1, source_target_pairs={{0,128},{64,192},{128,0},{192,64},{1,129},{65,193},{129,1},{193,65... | collective-permute-start | bytes 393224 | tf_op jit(solution)/shard_map/members/ppermute | solution.py:23
  105.2 1.2 collective-permute-start.26
  106.8 0.9 collective-permute-start.21
  107.7 1.8 collective-permute-start.20
  109.5 3.1 %collective-permute-done.22.a3 = f32[64,512]{1,0:T(8,128)S(1)} collective-permute-done((f32[64,512]{1,0:T(8,128)S(1)}, f32[64,512]{1,0:T(8,128)S(1)}, u32[]{:S(2)}, u32[]{:S(2)}) %collective-permute-start.22) | collective-permute-done | bytes 131104 | tf_op jit(solution)/shard_map/members/ppermute | solution.py:23
  112.5 1.5 collective-permute-done.21.a2
  114.0 1.3 collective-permute-done.20.a1
  115.4 0.6 copy-done.12
  116.1 2.4 %gram_rows.1 = (f32[4,128,512]{2,1,0:T(8,128)}, f32[64,1,128]{2,1,0:T(1,128)}) custom-call(f32[64,512]{1,0:T(8,128)} %copy-done.4, f32[64,512]{1,0:T(8,128)} %copy-done.12, f32[64,512]{1,0:T(8,128)} %copy-done.11, f32[64,512]{1,0:T(8,128)} %copy-done.10, f32[64,512]{1,0:T(8,128)} %copy-done.5, f32[64,512]{1,0:T(8,128)} %copy-done.9, f32[64,512]{1,0:T(8,128)} %copy-done.8, ...), custom_call_target="tpu_custom_call" | custom-call | tf_op jit(solution)/shard_map/members/gram_rows/pallas_call | solution.py:131
  118.4 21.0 %all_to_all.10.everyone_ref = f32[64,1,128]{2,1,0:T(1,128)} all-to-all(f32[64,1,128]{2,1,0:T(1,128)} %get-tuple-element.41), channel_id=1, replica_groups=mesh['rep'=4,'x'=4,'z'=8,'core'=2] {'x','z','core'}, dimensions={0} | all-to-all | bytes 65536 | tf_op jit(solution)/shard_map/gram/all_to_all | solution.py:321
  139.4 3.0 %updated.1 = (f32[128,512]{1,0:T(8,128)}, f32[128,512]{1,0:T(8,128)}, f32[128,512]{1,0:T(8,128)}, bf16[80,512]{1,0:T(8,128)(2,1)}, bf16[8,48,512]{2,1,0:T(8,128)(2,1)}) custom-call(f32[64,1,128]{2,1,0:T(1,128)} %all_to_all.10.everyone_ref, f32[4,128,512]{2,1,0:T(8,128)} %get-tuple-element.42.members_ref, f32[128,512]{1,0:T(8,128)} %master_ref.1, ...), custom_call_target="tpu_custom_call" | custom-call | tf_op jit(solution)/shard_map/adamw/updated/pallas_call | solution.py:190
  142.7 1.7 collective-permute-start.30
  144.4 1.2 collective-permute-start.29
  145.6 2.5 %collective-permute-done.31 = bf16[80,512]{1,0:T(8,128)(2,1)S(1)} collective-permute-done((bf16[80,512]{1,0:T(8,128)(2,1)}, bf16[80,512]{1,0:T(8,128)(2,1)S(1)}, u32[]{:S(2)}, u32[]{:S(2)}) %collective-permute-start.31) | collective-permute-done | bytes 81952 | tf_op jit(solution)/shard_map/params/ppermute | solution.py:23
  148.4 1.0 collective-permute-done.29
  149.4 1.7 pad_maximum_fusion.1
  151.1 16.9 %all_to_all.11.refs_0_ = bf16[8,48,512]{2,1,0:T(8,128)(2,1)S(1)} all-to-all(bf16[8,48,512]{2,1,0:T(8,128)(2,1)} %get-tuple-element.49), channel_id=1, replica_groups=mesh['rep'=4,'x'=4,'z'=8,'core'=2] {'z'}, dimensions={0} | all-to-all | bytes 786432 | tf_op jit(solution)/shard_map/params/all_to_all | solution.py:246
  168.0 1.4 collective-permute-start.34
  169.4 4.2 %collective-permute-start.33 = (bf16[8,48,512]{2,1,0:T(8,128)(2,1)S(1)}, bf16[8,48,512]{2,1,0:T(8,128)(2,1)S(1)}, u32[]{:S(2)}, u32[]{:S(2)}) collective-permute-start(bf16[8,48,512]{2,1,0:T(8,128)(2,1)S(1)} %all_to_all.11.refs_0_), channel_id=1, source_target_pairs={{0,32},{16,48},{32,0},{48,16},{1,33},{17,49},{33,1},{49,17},{2,34}... | collective-permute-start | bytes 1179656 | tf_op jit(solution)/shard_map/params/ppermute | solution.py:23
  173.6 4.6 %collective-permute-start.35 = (bf16[8,48,512]{2,1,0:T(8,128)(2,1)S(1)}, bf16[8,48,512]{2,1,0:T(8,128)(2,1)S(1)}, u32[]{:S(2)}, u32[]{:S(2)}) collective-permute-start(bf16[8,48,512]{2,1,0:T(8,128)(2,1)S(1)} %all_to_all.11.refs_0_), channel_id=1, source_target_pairs={{0,1},{1,0},{2,3},{3,2},{4,5},{5,4},{6,7},{7,6},{8,9},{9,8},{10,11... | collective-permute-start | bytes 1179656 | tf_op jit(solution)/shard_map/params/ppermute | solution.py:23
  178.2 7.7 %collective-permute-start.38 = (bf16[8,48,512]{2,1,0:T(8,128)(2,1)S(1)}, bf16[8,48,512]{2,1,0:T(8,128)(2,1)S(1)}, u32[]{:S(2)}, u32[]{:S(2)}) collective-permute-start(bf16[8,48,512]{2,1,0:T(8,128)(2,1)S(1)} %collective-permute-done.34.refs_3_), channel_id=1, source_target_pairs={{0,1},{1,0},{2,3},{3,2},{4,5},{5,4},{6,7},{7,6},{8,9},{9,8},{10,11... | collective-permute-start | bytes 1179656 | tf_op jit(solution)/shard_map/params/ppermute | solution.py:23
  185.9 0.9 collective-permute-done.33.refs_2_
  186.9 5.2 %collective-permute-start.37 = (bf16[8,48,512]{2,1,0:T(8,128)(2,1)S(1)}, bf16[8,48,512]{2,1,0:T(8,128)(2,1)S(1)}, u32[]{:S(2)}, u32[]{:S(2)}) collective-permute-start(bf16[8,48,512]{2,1,0:T(8,128)(2,1)S(1)} %collective-permute-done.33.refs_2_), channel_id=1, source_target_pairs={{0,1},{1,0},{2,3},{3,2},{4,5},{5,4},{6,7},{7,6},{8,9},{9,8},{10,11... | collective-permute-start | bytes 1179656 | tf_op jit(solution)/shard_map/params/ppermute | solution.py:23
  192.1 1.3 collective-permute-done.37.refs_6_
  194.0 1.7 placed.2.refs_1_
  195.8 2.5 %copy-done = bf16[5120,512]{1,0:T(8,128)(2,1)S(1)} copy-done((bf16[5120,512]{1,0:T(8,128)(2,1)S(1)}, bf16[5120,512]{1,0:T(8,128)(2,1)}, u32[]{:S(2)}) %copy-start) | copy-done | bytes 5242904
  198.3 2.4 %placed.3 = bf16[4,8,2,128,512]{4,3,2,1,0:T(8,128)(2,1)} custom-call(bf16[8,2,4,80,512]{4,3,2,1,0:T(8,128)(2,1)S(1)} %bitcast.45, bf16[4,8,2,128,512]{4,3,2,1,0:T(8,128)(2,1)} %placed.2.refs_1_), custom_call_target="tpu_custom_call", output_to_operand_aliasing={{}: (1, {})} | custom-call | tf_op jit(solution)/shard_map/params/placed/pallas_call | solution.py:227
  (79 shorter events, 3.7 us)
Async XLA Ops:
  7.2 7.1 %copy-start.6 = (bf16[256,512]{1,0:T(8,128)(2,1)S(1)}, bf16[256,512]{1,0:T(8,128)(2,1)}, u32[]{:S(2)}) copy-start(bf16[256,512]{1,0:T(8,128)(2,1)} %param.5) | copy-start | bytes 786436
  7.2 80.3 %reduce-scatter.2.cloned.1.call-start = ((), (), s32[]{:S(2)}) async-start(), calls=%async_computation.3 | async-start | bytes 4718592 | tf_op jit(solution)/shard_map/reduce_b/reduce_scatter | solution.py:286
  10.9 12.6 %copy-start.13 = (bf16[256,2048]{1,0:T(8,128)(2,1)S(1)}, bf16[256,2048]{1,0:T(8,128)(2,1)}, u32[]{:S(2)}) copy-start(bf16[256,2048]{1,0:T(8,128)(2,1)} %get-tuple-element.34) | copy-start | bytes 3145732
  10.9 12.6 %collective-permute-start.15 = (bf16[256,2048]{1,0:T(8,128)(2,1)}, bf16[256,2048]{1,0:T(8,128)(2,1)S(1)}, u32[]{:S(2)}, u32[]{:S(2)}) collective-permute-start(bf16[256,2048]{1,0:T(8,128)(2,1)} %get-tuple-element.35), channel_id=1, source_target_pairs={{0,1},{1,0},{2,3},{3,2},{4,5},{5,4},{6,7},{7,6},{8,9},{9,8},{10,11... | collective-permute-start | bytes 3145736 | tf_op jit(solution)/shard_map/core_swap/ppermute | solution.py:23
  14.3 5.3 %collective-permute-start = (bf16[256,512]{1,0:T(8,128)(2,1)S(1)}, bf16[256,512]{1,0:T(8,128)(2,1)S(1)}, u32[]{:S(2)}, u32[]{:S(2)}) collective-permute-start(bf16[256,512]{1,0:T(8,128)(2,1)S(1)} %copy-done.6), channel_id=1, source_target_pairs={{0,1},{1,0},{2,3},{3,2},{4,5},{5,4},{6,7},{7,6},{8,9},{9,8},{10,11... | collective-permute-start | bytes 786440 | tf_op jit(solution)/shard_map/core_swap/ppermute | solution.py:23
  14.4 7.6 %collective-permute-start.1 = (bf16[256,512]{1,0:T(8,128)(2,1)S(1)}, bf16[256,512]{1,0:T(8,128)(2,1)}, u32[]{:S(2)}, u32[]{:S(2)}) collective-permute-start(bf16[256,512]{1,0:T(8,128)(2,1)S(1)} %copy-done.6), channel_id=1, source_target_pairs={{0,48},{16,0},{32,16},{48,32},{1,49},{17,1},{33,17},{49,33},{2,50}... | collective-permute-start | bytes 786440 | tf_op jit(solution)/shard_map/core_swap/ppermute | solution.py:23
  15.1 8.4 %collective-permute-start.2 = (bf16[256,512]{1,0:T(8,128)(2,1)S(1)}, bf16[256,512]{1,0:T(8,128)(2,1)S(1)}, u32[]{:S(2)}, u32[]{:S(2)}) collective-permute-start(bf16[256,512]{1,0:T(8,128)(2,1)S(1)} %copy-done.6), channel_id=1, source_target_pairs={{0,16},{16,32},{32,48},{48,0},{1,17},{17,33},{33,49},{49,1},{2,18}... | collective-permute-start | bytes 786440 | tf_op jit(solution)/shard_map/core_swap/ppermute | solution.py:23
  19.6 3.9 %copy-start.1 = (bf16[512,512]{1,0:T(8,128)(2,1)}, bf16[512,512]{1,0:T(8,128)(2,1)S(1)}, u32[]{:S(2)}) copy-start(bf16[512,512]{1,0:T(8,128)(2,1)S(1)} %pad_maximum_fusion) | copy-start | bytes 1572868
  23.5 3.3 %copy-start.14 = (bf16[256,512]{1,0:T(8,128)(2,1)}, bf16[256,512]{1,0:T(8,128)(2,1)S(1)}, u32[]{:S(2)}) copy-start(bf16[256,512]{1,0:T(8,128)(2,1)S(1)} %collective-permute-done.2) | copy-start | bytes 786436
  26.8 1.7 copy-start.3
  26.8 168.9 %all-gather.2.cloned.1.call-start = ((), (), s32[]{:S(2)}) async-start(), calls=%async_computation.4 | async-start | bytes 5570560 | tf_op jit(solution)/shard_map/params/all_gather | solution.py:244
  26.9 4.3 %collective-permute-start.3 = (bf16[256,2048]{1,0:T(8,128)(2,1)}, bf16[256,2048]{1,0:T(8,128)(2,1)}, u32[]{:S(2)}, u32[]{:S(2)}) collective-permute-start(bf16[256,2048]{1,0:T(8,128)(2,1)} %get-tuple-element.30), channel_id=1, source_target_pairs={{0,1},{1,0},{2,3},{3,2},{4,5},{5,4},{6,7},{7,6},{8,9},{9,8},{10,11... | collective-permute-start | bytes 3145736 | tf_op jit(solution)/shard_map/core_swap/ppermute | solution.py:23
  33.4 13.5 %collective-permute-start.4 = (bf16[512,512]{1,0:T(8,128)(2,1)}, bf16[512,512]{1,0:T(8,128)(2,1)}, u32[]{:S(2)}, u32[]{:S(2)}) collective-permute-start(bf16[512,512]{1,0:T(8,128)(2,1)} %get-tuple-element.52), channel_id=1, source_target_pairs={{0,48},{16,0},{32,16},{48,32},{1,49},{17,1},{33,17},{49,33},{2,50}... | collective-permute-start | bytes 1572872 | tf_op jit(solution)/shard_map/reduce_a/ppermute | solution.py:23
  33.5 8.8 %collective-permute-start.7 = (bf16[256,512]{1,0:T(8,128)(2,1)S(1)}, bf16[256,512]{1,0:T(8,128)(2,1)}, u32[]{:S(2)}, u32[]{:S(2)}) collective-permute-start(bf16[256,512]{1,0:T(8,128)(2,1)S(1)} %copy-done.6), channel_id=1, source_target_pairs={{0,32},{16,48},{32,0},{48,16},{1,33},{17,49},{33,1},{49,17},{2,34}... | collective-permute-start | bytes 786440 | tf_op jit(solution)/shard_map/core_swap/ppermute | solution.py:23
  34.7 10.3 %collective-permute-start.5 = (bf16[256,512]{1,0:T(8,128)(2,1)}, bf16[256,512]{1,0:T(8,128)(2,1)}, u32[]{:S(2)}, u32[]{:S(2)}) collective-permute-start(bf16[256,512]{1,0:T(8,128)(2,1)} %collective-permute-done.1), channel_id=1, source_target_pairs={{0,1},{1,0},{2,3},{3,2},{4,5},{5,4},{6,7},{7,6},{8,9},{9,8},{10,11... | collective-permute-start | bytes 786440 | tf_op jit(solution)/shard_map/core_swap/ppermute | solution.py:23
  35.7 20.0 %collective-permute-start.9 = (bf16[512,512]{1,0:T(8,128)(2,1)S(1)}, bf16[512,512]{1,0:T(8,128)(2,1)}, u32[]{:S(2)}, u32[]{:S(2)}) collective-permute-start(bf16[512,512]{1,0:T(8,128)(2,1)S(1)} %get-tuple-element.53), channel_id=1, source_target_pairs={{0,16},{16,32},{32,48},{48,0},{1,17},{17,33},{33,49},{49,1},{2,18}... | collective-permute-start | bytes 1572872 | tf_op jit(solution)/shard_map/reduce_a/ppermute | solution.py:23
  35.7 20.0 %copy-start.15 = (bf16[256,512]{1,0:T(8,128)(2,1)S(1)}, bf16[256,512]{1,0:T(8,128)(2,1)}, u32[]{:S(2)}) copy-start(bf16[256,512]{1,0:T(8,128)(2,1)} %copy-done.14) | copy-start | bytes 786436
  35.7 12.9 %collective-permute-start.10 = (bf16[256,512]{1,0:T(8,128)(2,1)}, bf16[256,512]{1,0:T(8,128)(2,1)S(1)}, u32[]{:S(2)}, u32[]{:S(2)}) collective-permute-start(bf16[256,512]{1,0:T(8,128)(2,1)} %copy-done.14), channel_id=1, source_target_pairs={{0,1},{1,0},{2,3},{3,2},{4,5},{5,4},{6,7},{7,6},{8,9},{9,8},{10,11... | collective-permute-start | bytes 786440 | tf_op jit(solution)/shard_map/core_swap/ppermute | solution.py:23
  42.4 14.8 %collective-permute-start.8 = (bf16[256,512]{1,0:T(8,128)(2,1)}, bf16[256,512]{1,0:T(8,128)(2,1)S(1)}, u32[]{:S(2)}, u32[]{:S(2)}) collective-permute-start(bf16[256,512]{1,0:T(8,128)(2,1)} %collective-permute-done.7), channel_id=1, source_target_pairs={{0,1},{1,0},{2,3},{3,2},{4,5},{5,4},{6,7},{7,6},{8,9},{9,8},{10,11... | collective-permute-start | bytes 786440 | tf_op jit(solution)/shard_map/core_swap/ppermute | solution.py:23
  45.0 19.7 %collective-permute-start.6 = (bf16[512,512]{1,0:T(8,128)(2,1)S(1)}, bf16[512,512]{1,0:T(8,128)(2,1)S(1)}, u32[]{:S(2)}, u32[]{:S(2)}) collective-permute-start(bf16[512,512]{1,0:T(8,128)(2,1)S(1)} %get-tuple-element.54), channel_id=1, source_target_pairs={{0,32},{16,48},{32,0},{48,16},{1,33},{17,49},{33,1},{49,17},{2,34}... | collective-permute-start | bytes 1572872 | tf_op jit(solution)/shard_map/reduce_a/ppermute | solution.py:23
  48.6 17.6 %copy-start.2 = (bf16[512,512]{1,0:T(8,128)(2,1)S(1)}, bf16[512,512]{1,0:T(8,128)(2,1)}, u32[]{:S(2)}) copy-start(bf16[512,512]{1,0:T(8,128)(2,1)} %copy-done.1) | copy-start | bytes 1572868
  66.7 9.6 %collective-permute-start.11 = (f32[32,512]{1,0:T(8,128)S(1)}, f32[32,512]{1,0:T(8,128)S(1)}, u32[]{:S(2)}, u32[]{:S(2)}) collective-permute-start(f32[32,512]{1,0:T(8,128)S(1)} %get-tuple-element.60), channel_id=1, source_target_pairs={{0,2},{2,4},{4,6},{6,8},{8,10},{10,12},{12,14},{14,0},{1,3},{3,5},... | collective-permute-start | bytes 196616 | tf_op jit(solution)/shard_map/reduce_a/ppermute | solution.py:23
  68.6 7.7 %collective-permute-start.13 = (f32[32,512]{1,0:T(8,128)S(1)}, f32[32,512]{1,0:T(8,128)S(1)}, u32[]{:S(2)}, u32[]{:S(2)}) collective-permute-start(f32[32,512]{1,0:T(8,128)S(1)} %get-tuple-element.61), channel_id=1, source_target_pairs={{0,14},{2,0},{4,2},{6,4},{8,6},{10,8},{12,10},{14,12},{1,15},{3,1}... | collective-permute-start | bytes 196616 | tf_op jit(solution)/shard_map/reduce_a/ppermute | solution.py:23
  76.3 9.1 %collective-permute-start.12 = (f32[64,512]{1,0:T(8,128)S(1)}, f32[64,512]{1,0:T(8,128)S(1)}, u32[]{:S(2)}, u32[]{:S(2)}) collective-permute-start(f32[64,512]{1,0:T(8,128)S(1)} %pad_maximum_fusion.2), channel_id=1, source_target_pairs={{0,2},{2,4},{4,6},{6,8},{8,10},{10,12},{12,14},{14,0},{1,3},{3,5},... | collective-permute-start | bytes 393224 | tf_op jit(solution)/shard_map/reduce_a/ppermute | solution.py:23
  76.5 8.9 %collective-permute-start.14 = (f32[64,512]{1,0:T(8,128)S(1)}, f32[64,512]{1,0:T(8,128)S(1)}, u32[]{:S(2)}, u32[]{:S(2)}) collective-permute-start(f32[64,512]{1,0:T(8,128)S(1)} %pad_maximum_fusion.3), channel_id=1, source_target_pairs={{0,14},{2,0},{4,2},{6,4},{8,6},{10,8},{12,10},{14,12},{1,15},{3,1}... | collective-permute-start | bytes 393224 | tf_op jit(solution)/shard_map/reduce_a/ppermute | solution.py:23
  88.5 7.4 %collective-permute-start.16 = (f32[64,512]{1,0:T(8,128)S(1)}, f32[64,512]{1,0:T(8,128)S(1)}, u32[]{:S(2)}, u32[]{:S(2)}) collective-permute-start(f32[64,512]{1,0:T(8,128)S(1)} %get-tuple-element.36), channel_id=1, source_target_pairs={{0,2},{2,4},{4,6},{6,8},{8,10},{10,12},{12,14},{14,0},{1,3},{3,5},... | collective-permute-start | bytes 393224 | tf_op jit(solution)/shard_map/reduce_a/ppermute | solution.py:23
  88.6 7.3 %collective-permute-start.18 = (f32[64,512]{1,0:T(8,128)S(1)}, f32[64,512]{1,0:T(8,128)S(1)}, u32[]{:S(2)}, u32[]{:S(2)}) collective-permute-start(f32[64,512]{1,0:T(8,128)S(1)} %get-tuple-element.37), channel_id=1, source_target_pairs={{0,14},{2,0},{4,2},{6,4},{8,6},{10,8},{12,10},{14,12},{1,15},{3,1}... | collective-permute-start | bytes 393224 | tf_op jit(solution)/shard_map/reduce_a/ppermute | solution.py:23
  91.3 7.4 %collective-permute-start.23 = (f32[64,512]{1,0:T(8,128)S(1)}, f32[64,512]{1,0:T(8,128)S(1)}, u32[]{:S(2)}, u32[]{:S(2)}) collective-permute-start(f32[64,512]{1,0:T(8,128)S(1)} %get-tuple-element.38), channel_id=1, source_target_pairs={{0,48},{16,0},{32,16},{48,32},{1,49},{17,1},{33,17},{49,33},{2,50}... | collective-permute-start | bytes 393224 | tf_op jit(solution)/shard_map/reduce_a/reduce_b2/ppermute | solution.py:23
  92.2 6.5 %collective-permute-start.24 = (f32[64,512]{1,0:T(8,128)S(1)}, f32[64,512]{1,0:T(8,128)S(1)}, u32[]{:S(2)}, u32[]{:S(2)}) collective-permute-start(f32[64,512]{1,0:T(8,128)S(1)} %get-tuple-element.39), channel_id=1, source_target_pairs={{0,16},{16,32},{32,48},{48,0},{1,17},{17,33},{33,49},{49,1},{2,18}... | collective-permute-start | bytes 393224 | tf_op jit(solution)/shard_map/reduce_a/reduce_b2/ppermute | solution.py:23
  92.8 7.7 %collective-permute-start.25 = (f32[64,512]{1,0:T(8,128)S(1)}, f32[64,512]{1,0:T(8,128)S(1)}, u32[]{:S(2)}, u32[]{:S(2)}) collective-permute-start(f32[64,512]{1,0:T(8,128)S(1)} %get-tuple-element.40), channel_id=1, source_target_pairs={{0,32},{16,48},{32,0},{48,16},{1,33},{17,49},{33,1},{49,17},{2,34}... | collective-permute-start | bytes 393224 | tf_op jit(solution)/shard_map/reduce_a/reduce_b2/ppermute | solution.py:23
  96.0 10.4 %collective-permute-start.17 = (f32[64,512]{1,0:T(8,128)S(1)}, f32[64,512]{1,0:T(8,128)S(1)}, u32[]{:S(2)}, u32[]{:S(2)}) collective-permute-start(f32[64,512]{1,0:T(8,128)S(1)} %get-tuple-element.55), channel_id=1, source_target_pairs={{0,2},{2,4},{4,6},{6,8},{8,10},{10,12},{12,14},{14,0},{1,3},{3,5},... | collective-permute-start | bytes 393224 | tf_op jit(solution)/shard_map/reduce_a/ppermute | solution.py:23
  96.1 10.3 %collective-permute-start.19 = (f32[64,512]{1,0:T(8,128)S(1)}, f32[64,512]{1,0:T(8,128)S(1)}, u32[]{:S(2)}, u32[]{:S(2)}) collective-permute-start(f32[64,512]{1,0:T(8,128)S(1)} %get-tuple-element.56), channel_id=1, source_target_pairs={{0,14},{2,0},{4,2},{6,4},{8,6},{10,8},{12,10},{14,12},{1,15},{3,1}... | collective-permute-start | bytes 393224 | tf_op jit(solution)/shard_map/reduce_a/ppermute | solution.py:23
  101.4 13.9 %copy-start.5 = (f32[64,512]{1,0:T(8,128)}, f32[64,512]{1,0:T(8,128)S(1)}, u32[]{:S(2)}) copy-start(f32[64,512]{1,0:T(8,128)S(1)} %bitcast_add_fusion.b0) | copy-start | bytes 393220
  101.5 6.2 %collective-permute-start.28 = (f32[64,512]{1,0:T(8,128)S(1)}, f32[64,512]{1,0:T(8,128)S(1)}, u32[]{:S(2)}, u32[]{:S(2)}) collective-permute-start(f32[64,512]{1,0:T(8,128)S(1)} %bitcast_add_fusion.b0), channel_id=1, source_target_pairs={{0,64},{64,128},{128,192},{192,0},{1,65},{65,129},{129,193},{193,1... | collective-permute-start | bytes 393224 | tf_op jit(solution)/shard_map/members/ppermute | solution.py:23
  102.7 6.7 %collective-permute-start.27 = (f32[64,512]{1,0:T(8,128)S(1)}, f32[64,512]{1,0:T(8,128)S(1)}, u32[]{:S(2)}, u32[]{:S(2)}) collective-permute-start(f32[64,512]{1,0:T(8,128)S(1)} %bitcast_add_fusion.b0), channel_id=1, source_target_pairs={{0,128},{64,192},{128,0},{192,64},{1,129},{65,193},{129,1},{193,65... | collective-permute-start | bytes 393224 | tf_op jit(solution)/shard_map/members/ppermute | solution.py:23
  105.2 4.3 %collective-permute-start.26 = (f32[64,512]{1,0:T(8,128)S(1)}, f32[64,512]{1,0:T(8,128)S(1)}, u32[]{:S(2)}, u32[]{:S(2)}) collective-permute-start(f32[64,512]{1,0:T(8,128)S(1)} %bitcast_add_fusion.b0), channel_id=1, source_target_pairs={{0,192},{64,0},{128,64},{192,128},{1,193},{65,1},{129,65},{193,129... | collective-permute-start | bytes 393224 | tf_op jit(solution)/shard_map/members/ppermute | solution.py:23
  106.4 9.0 %copy-start.4 = (f32[64,512]{1,0:T(8,128)}, f32[64,512]{1,0:T(8,128)S(1)}, u32[]{:S(2)}) copy-start(f32[64,512]{1,0:T(8,128)S(1)} %fusion.19.a0) | copy-start | bytes 393220
  106.4 6.1 %collective-permute-start.22 = (f32[64,512]{1,0:T(8,128)S(1)}, f32[64,512]{1,0:T(8,128)S(1)}, u32[]{:S(2)}, u32[]{:S(2)}) collective-permute-start(f32[64,512]{1,0:T(8,128)S(1)} %fusion.19.a0), channel_id=1, source_target_pairs={{0,64},{64,128},{128,192},{192,0},{1,65},{65,129},{129,193},{193,1... | collective-permute-start | bytes 393224 | tf_op jit(solution)/shard_map/members/ppermute | solution.py:23
  106.8 7.3 %collective-permute-start.21 = (f32[64,512]{1,0:T(8,128)S(1)}, f32[64,512]{1,0:T(8,128)S(1)}, u32[]{:S(2)}, u32[]{:S(2)}) collective-permute-start(f32[64,512]{1,0:T(8,128)S(1)} %fusion.19.a0), channel_id=1, source_target_pairs={{0,128},{64,192},{128,0},{192,64},{1,129},{65,193},{129,1},{193,65... | collective-permute-start | bytes 393224 | tf_op jit(solution)/shard_map/members/ppermute | solution.py:23
  107.7 7.7 %copy-start.7 = (f32[64,512]{1,0:T(8,128)}, f32[64,512]{1,0:T(8,128)S(1)}, u32[]{:S(2)}) copy-start(f32[64,512]{1,0:T(8,128)S(1)} %collective-permute-done.28.b3) | copy-start | bytes 393220
  107.7 7.7 %collective-permute-start.20 = (f32[64,512]{1,0:T(8,128)S(1)}, f32[64,512]{1,0:T(8,128)S(1)}, u32[]{:S(2)}, u32[]{:S(2)}) collective-permute-start(f32[64,512]{1,0:T(8,128)S(1)} %fusion.19.a0), channel_id=1, source_target_pairs={{0,192},{64,0},{128,64},{192,128},{1,193},{65,1},{129,65},{193,129... | collective-permute-start | bytes 393224 | tf_op jit(solution)/shard_map/members/ppermute | solution.py:23
  109.5 5.9 %copy-start.8 = (f32[64,512]{1,0:T(8,128)}, f32[64,512]{1,0:T(8,128)S(1)}, u32[]{:S(2)}) copy-start(f32[64,512]{1,0:T(8,128)S(1)} %collective-permute-done.27.b2) | copy-start | bytes 393220
  109.5 5.9 %copy-start.9 = (f32[64,512]{1,0:T(8,128)}, f32[64,512]{1,0:T(8,128)S(1)}, u32[]{:S(2)}) copy-start(f32[64,512]{1,0:T(8,128)S(1)} %collective-permute-done.26.b1) | copy-start | bytes 393220
  112.5 2.8 %copy-start.10 = (f32[64,512]{1,0:T(8,128)}, f32[64,512]{1,0:T(8,128)S(1)}, u32[]{:S(2)}) copy-start(f32[64,512]{1,0:T(8,128)S(1)} %collective-permute-done.22.a3) | copy-start | bytes 393220
  114.0 1.4 copy-start.11
  115.4 0.7 copy-start.12
  142.5 5.6 %collective-permute-start.31 = (bf16[80,512]{1,0:T(8,128)(2,1)}, bf16[80,512]{1,0:T(8,128)(2,1)S(1)}, u32[]{:S(2)}, u32[]{:S(2)}) collective-permute-start(bf16[80,512]{1,0:T(8,128)(2,1)} %get-tuple-element.46), channel_id=1, source_target_pairs={{0,16},{16,32},{32,48},{48,0},{1,17},{17,33},{33,49},{49,1},{2,18}... | collective-permute-start | bytes 245768 | tf_op jit(solution)/shard_map/params/ppermute | solution.py:23
  142.7 5.7 %collective-permute-start.30 = (bf16[80,512]{1,0:T(8,128)(2,1)}, bf16[80,512]{1,0:T(8,128)(2,1)S(1)}, u32[]{:S(2)}, u32[]{:S(2)}) collective-permute-start(bf16[80,512]{1,0:T(8,128)(2,1)} %get-tuple-element.46), channel_id=1, source_target_pairs={{0,32},{16,48},{32,0},{48,16},{1,33},{17,49},{33,1},{49,17},{2,34}... | collective-permute-start | bytes 245768 | tf_op jit(solution)/shard_map/params/ppermute | solution.py:23
  144.4 5.0 %collective-permute-start.29 = (bf16[80,512]{1,0:T(8,128)(2,1)}, bf16[80,512]{1,0:T(8,128)(2,1)S(1)}, u32[]{:S(2)}, u32[]{:S(2)}) collective-permute-start(bf16[80,512]{1,0:T(8,128)(2,1)} %get-tuple-element.46), channel_id=1, source_target_pairs={{0,48},{16,0},{32,16},{48,32},{1,49},{17,1},{33,17},{49,33},{2,50}... | collective-permute-start | bytes 245768 | tf_op jit(solution)/shard_map/params/ppermute | solution.py:23
  168.0 10.2 %collective-permute-start.34 = (bf16[8,48,512]{2,1,0:T(8,128)(2,1)S(1)}, bf16[8,48,512]{2,1,0:T(8,128)(2,1)S(1)}, u32[]{:S(2)}, u32[]{:S(2)}) collective-permute-start(bf16[8,48,512]{2,1,0:T(8,128)(2,1)S(1)} %all_to_all.11.refs_0_), channel_id=1, source_target_pairs={{0,16},{16,32},{32,48},{48,0},{1,17},{17,33},{33,49},{49,1},{2,18}... | collective-permute-start | bytes 1179656 | tf_op jit(solution)/shard_map/params/ppermute | solution.py:23
  169.4 17.5 %collective-permute-start.33 = (bf16[8,48,512]{2,1,0:T(8,128)(2,1)S(1)}, bf16[8,48,512]{2,1,0:T(8,128)(2,1)S(1)}, u32[]{:S(2)}, u32[]{:S(2)}) collective-permute-start(bf16[8,48,512]{2,1,0:T(8,128)(2,1)S(1)} %all_to_all.11.refs_0_), channel_id=1, source_target_pairs={{0,32},{16,48},{32,0},{48,16},{1,33},{17,49},{33,1},{49,17},{2,34}... | collective-permute-start | bytes 1179656 | tf_op jit(solution)/shard_map/params/ppermute | solution.py:23
  173.6 18.5 %collective-permute-start.32 = (bf16[8,48,512]{2,1,0:T(8,128)(2,1)S(1)}, bf16[8,48,512]{2,1,0:T(8,128)(2,1)S(1)}, u32[]{:S(2)}, u32[]{:S(2)}) collective-permute-start(bf16[8,48,512]{2,1,0:T(8,128)(2,1)S(1)} %all_to_all.11.refs_0_), channel_id=1, source_target_pairs={{0,48},{16,0},{32,16},{48,32},{1,49},{17,1},{33,17},{49,33},{2,50}... | collective-permute-start | bytes 1179656 | tf_op jit(solution)/shard_map/params/ppermute | solution.py:23
  173.6 18.5 %collective-permute-start.35 = (bf16[8,48,512]{2,1,0:T(8,128)(2,1)S(1)}, bf16[8,48,512]{2,1,0:T(8,128)(2,1)S(1)}, u32[]{:S(2)}, u32[]{:S(2)}) collective-permute-start(bf16[8,48,512]{2,1,0:T(8,128)(2,1)S(1)} %all_to_all.11.refs_0_), channel_id=1, source_target_pairs={{0,1},{1,0},{2,3},{3,2},{4,5},{5,4},{6,7},{7,6},{8,9},{9,8},{10,11... | collective-permute-start | bytes 1179656 | tf_op jit(solution)/shard_map/params/ppermute | solution.py:23
  178.2 13.9 %collective-permute-start.38 = (bf16[8,48,512]{2,1,0:T(8,128)(2,1)S(1)}, bf16[8,48,512]{2,1,0:T(8,128)(2,1)S(1)}, u32[]{:S(2)}, u32[]{:S(2)}) collective-permute-start(bf16[8,48,512]{2,1,0:T(8,128)(2,1)S(1)} %collective-permute-done.34.refs_3_), channel_id=1, source_target_pairs={{0,1},{1,0},{2,3},{3,2},{4,5},{5,4},{6,7},{7,6},{8,9},{9,8},{10,11... | collective-permute-start | bytes 1179656 | tf_op jit(solution)/shard_map/params/ppermute | solution.py:23
  186.9 6.6 %collective-permute-start.37 = (bf16[8,48,512]{2,1,0:T(8,128)(2,1)S(1)}, bf16[8,48,512]{2,1,0:T(8,128)(2,1)S(1)}, u32[]{:S(2)}, u32[]{:S(2)}) collective-permute-start(bf16[8,48,512]{2,1,0:T(8,128)(2,1)S(1)} %collective-permute-done.33.refs_2_), channel_id=1, source_target_pairs={{0,1},{1,0},{2,3},{3,2},{4,5},{5,4},{6,7},{7,6},{8,9},{9,8},{10,11... | collective-permute-start | bytes 1179656 | tf_op jit(solution)/shard_map/params/ppermute | solution.py:23
  192.1 1.9 collective-permute-start.36
  195.8 2.5 %copy-start = (bf16[5120,512]{1,0:T(8,128)(2,1)S(1)}, bf16[5120,512]{1,0:T(8,128)(2,1)}, u32[]{:S(2)}) copy-start(bf16[5120,512]{1,0:T(8,128)(2,1)} %all-gather.2.cloned.1.call-done) | copy-start | bytes 15728644
Sparse Core Ops, SparseCore 0:
  27.0 60.4 reduce-scatter.1
  151.2 44.4 all-gather.1
